TPU v7x, 256 devices: a whole 4x4x8 slice. The times are simulated.
256 devices in a mesh: seq: 16 (over z, core), head: 16 (over x, y).
Axes of the slice: x: 4, y: 4, z: 8, core: 2. Of those that a mesh axis runs over, the one named last changes fastest.
Arguments:
- x_in: bfloat16 [16384, 8192], P('seq', 'head'), may hold values from -6 to 6
- z_gate: bfloat16 [16384, 8192], P('seq', 'head'), may hold values from -6 to 6
- b_in: bfloat16 [16384, 128], P('seq'), may hold values from -6.5 to 6.5
- c_in: bfloat16 [16384, 128], P('seq'), may hold values from -6 to 6
- dt_raw: float32 [16384, 128], P('seq', 'head'), may hold values from -7.5 to 263.144
- a_log: float32 [128], P('head'), may hold values from -12 to 3.5, as said below
- d_skip: float32 [128], P('head'), may hold values from 0.5 to 1.5
- conv_x: float32 [4, 8192], P(None, 'head'), may hold values from -3 to 3
- conv_bc: float32 [4, 256], replicated, may hold values from -0.8 to 0.8
- norm_gain: float32 [8192], P('head'), may hold values from 0.1 to 1.9
- w_out: bfloat16 [8192, 4096], P('head'), may hold values from -0.0625 to 0.0625
Outputs:
- mixed: bfloat16 [16384, 4096], P(('seq', 'head'))
Inputs may be any that keep to these rules, and one draw needn't show every extreme that they name: `a_log`: logarithm of each head's decay rate.
All inputs are finite; a program needn't handle non-finite values.
Results may differ from a plain program's by a relative error of at most 0.018.
Values may be sent and summed in bfloat16 or wider, within the bound.
No kernel may reach another device: no remote copies, remote signals or barrier semaphores. Data moves between devices by JAX's collectives and lax.ppermute only.
A program may use at most 64 MiB of HBM per device.

v0:
```python
import jax
import jax.numpy as jnp
from jax import lax
from jax.experimental import pallas as pl
from jax.experimental.pallas import tpu as pltpu
from jax.sharding import PartitionSpec as P


INNER = 8192
norm_eps = 1e-05
Q = 128
bf16 = jnp.bfloat16
f32 = jnp.float32


def silu(v):
    half = 0.5 * v
    return half + half * jnp.tanh(half)


def dot(a, b):
    return jnp.dot(a, b, preferred_element_type=f32)


def dot_t(a, b):
    return lax.dot_general(a, b, (((1,), (1,)), ((), ())), preferred_element_type=f32)


def head_column(ref, shape):
    rows = lax.broadcasted_iota(jnp.int32, shape, 0)
    out = jnp.full(shape, ref[0], f32)
    for h in range(1, 8):
        out = jnp.where(rows == h, ref[h], out)
    return out


def edge_kernel(x_ref, b_ref, c_ref, o_ref):
    o_ref[:, :512] = x_ref[...]
    o_ref[:, 512:640] = b_ref[...]
    o_ref[:, 640:] = c_ref[...]


def edge_rows(x_in, b_in, c_in):
    last = lambda n: pl.BlockSpec((16, n), lambda i: (63, 0))
    return pl.pallas_call(
        edge_kernel,
        grid=(1,),
        in_specs=[last(512), last(128), last(128)],
        out_specs=pl.BlockSpec((16, 768), lambda i: (0, 0)),
        out_shape=jax.ShapeDtypeStruct((16, 768), bf16),
        name="edge",
    )(x_in, b_in, c_in)


def pair_row(low, values, h):
    return jnp.where(low, values[h : h + 1, :], values[h + 1 : h + 2, :])


def decay_kernel(a_ref, dt_ref, run_ref, step_ref, late_ref, grow_ref):
    rate = -jnp.exp(head_column(a_ref, (8, Q)))
    lane8 = lax.broadcasted_iota(jnp.int32, (8, Q), 1)

    def halves(v):
        high = v.astype(bf16).astype(f32)
        return jnp.transpose(jnp.concatenate([high, v - high], axis=0)).astype(bf16)

    for i in range(1024 // Q):
        lanes = slice(i * Q, i * Q + Q)
        raw = dt_ref[:, lanes]
        dt = jnp.maximum(raw, 0.0) + jnp.log1p(jnp.exp(-jnp.abs(raw)))
        run = rate * dt
        shift = 1
        while shift < Q:
            run = run + jnp.where(lane8 >= shift, pltpu.roll(run, shift, 1), 0.0)
            shift *= 2
        fin = jnp.broadcast_to(run[:, Q - 1 : Q], (8, Q))
        run_ref[:, lanes] = run
        step_ref[:, lanes] = dt
        late_ref[lanes, :] = halves(jnp.exp(jnp.minimum(fin - run, 0.0)) * dt)
        grow_ref[lanes, :] = halves(jnp.exp(run))


def decays(dt_raw, a_log):
    full = lambda *s: pl.BlockSpec(s, lambda i: (0,) * len(s))
    return pl.pallas_call(
        decay_kernel,
        grid=(1,),
        in_specs=[pl.BlockSpec(memory_space=pltpu.SMEM), full(8, 1024)],
        out_specs=[full(8, 1024)] * 2 + [full(1024, 16)] * 2,
        out_shape=[jax.ShapeDtypeStruct((8, 1024), f32)] * 2
        + [jax.ShapeDtypeStruct((1024, 16), bf16)] * 2,
        name="decays",
    )(a_log, dt_raw.T)


def spread():
    lane = lax.broadcasted_iota(jnp.int32, (16, 512), 1)
    row = lax.broadcasted_iota(jnp.int32, (16, 512), 0)
    first = jnp.where(row >= 8, row - 8, row) * 64
    return jnp.where((lane >= first) & (lane < first + 64), 1.0, 0.0).astype(bf16)


def state_kernel(
    x_ref, b_ref, c_ref, rim_ref, run_ref, late_ref, wx_ref, wbc_ref,
    xc_ref, bc_ref, before_ref, states_ref, msg_ref,
    xs, bs, st, tot,
):
    i = pl.program_id(0)

    @pl.when(i == 0)
    def _():
        xs[0:8, :] = rim_ref[8:16, :512].astype(f32)
        bs[0:8, :] = rim_ref[8:16, 512:].astype(f32)
        st[...] = jnp.zeros_like(st)
        tot[...] = jnp.zeros_like(tot)

    @pl.when(i > 0)
    def _():
        xs[0:8, :] = xs[Q : Q + 8, :]
        bs[0:8, :] = bs[Q : Q + 8, :]

    xs[8 : Q + 8, :] = x_ref[...].astype(f32)
    bs[8 : Q + 8, :128] = b_ref[...].astype(f32)
    bs[8 : Q + 8, 128:] = c_ref[...].astype(f32)

    def conv(buf, w_ref, cols):
        whole = buf[:, cols]
        half = 0.5 * w_ref[:, cols]
        total = half[3:4] * whole[8:]
        for k in range(3):
            total = total + half[k : k + 1] * pltpu.roll(whole, 3 - k, 0)[8:]
        return total + total * jnp.tanh(total)

    fin = jnp.broadcast_to(run_ref[:, Q - 1 : Q], (8, 128))
    b = conv(bs, wbc_ref, slice(0, 128))
    bc_ref[:, :128] = b.astype(bf16)
    bc_ref[:, 128:] = conv(bs, wbc_ref, slice(128, 256)).astype(bf16)
    b_t = jnp.transpose(b).astype(bf16)
    low1 = lax.broadcasted_iota(jnp.int32, (1, 128), 1) < 64
    late = dot(late_ref[...], spread())
    states_ref[...] = st[...].astype(bf16)
    before_ref[...] = tot[...]
    for p in range(4):
        cols = slice(128 * p, 128 * p + 128)
        xp = conv(xs, wx_ref, cols)
        xc_ref[:, cols] = xp.astype(bf16)
        end = jnp.exp(pair_row(low1, fin, 2 * p))
        st[:, cols] = st[:, cols] * end + dot(b_t, (xp * late[:, cols]).astype(bf16))
    tot[...] = tot[...] + fin

    @pl.when(i == pl.num_programs(0) - 1)
    def _():
        total = tot[...]
        row8 = lax.broadcasted_iota(jnp.int32, (8, 128), 0)
        for p in range(4):
            decay = jnp.broadcast_to(pair_row(low1, total, 2 * p), (8, 128))
            high = decay.astype(bf16).astype(f32)
            tile = jnp.where(row8 == 0, high, decay - high).astype(bf16)
            for group in range(4):
                j = 4 * group + p
                msg_ref[j, 0:32, :] = st[
                    32 * group : 32 * group + 32, 128 * p : 128 * p + 128
                ].astype(bf16)
                msg_ref[j, 32:40, :] = tile


def block_states(x_in, b_in, c_in, rim, run, late, conv_x, conv_bc):
    rows = lambda n: pl.BlockSpec((Q, n), lambda i: (i, 0))
    full = lambda *s: pl.BlockSpec(s, lambda i: (0,) * len(s))
    lanes = pl.BlockSpec((8, Q), lambda i: (0, i))
    return pl.pallas_call(
        state_kernel,
        grid=(1024 // Q,),
        in_specs=[
            rows(512), rows(128), rows(128), full(16, 768), lanes, rows(16),
            full(4, 512), full(4, 256),
        ],
        out_specs=[rows(512), rows(256), lanes, rows(512), full(16, 40, 128)],
        out_shape=[
            jax.ShapeDtypeStruct((1024, 512), bf16),
            jax.ShapeDtypeStruct((1024, 256), bf16),
            jax.ShapeDtypeStruct((8, 1024), f32),
            jax.ShapeDtypeStruct((1024, 512), bf16),
            jax.ShapeDtypeStruct((16, 40, 128), bf16),
        ],
        scratch_shapes=[
            pltpu.VMEM((Q + 8, 512), f32),
            pltpu.VMEM((Q + 8, 256), f32),
            pltpu.VMEM((128, 512), f32),
            pltpu.VMEM((8, Q), f32),
        ],
        name="states",
    )(x_in, b_in, c_in, rim, run, late, conv_x, conv_bc)


def inside_kernel(skip_ref, xc_ref, bc_ref, run_ref, step_ref, y_ref):
    b = bc_ref[:, :128]
    c = bc_ref[:, 128:]
    run = run_ref[...]
    dt = step_ref[...]
    run_t = jnp.transpose(run)
    row = lax.broadcasted_iota(jnp.int32, (Q, Q), 0)
    col = lax.broadcasted_iota(jnp.int32, (Q, Q), 1)
    scores = jnp.where(row >= col, dot_t(c, b), 0.0)
    low = col < 64
    for p in range(4):
        h = 2 * p
        cols = slice(128 * p, 128 * p + 128)
        xf = xc_ref[:, cols].astype(f32)
        xb = jnp.concatenate(
            [jnp.where(low, xf, 0.0).astype(bf16), jnp.where(low, 0.0, xf).astype(bf16)], axis=0
        )
        mix = []
        for k in (h, h + 1):
            fade = jnp.exp(jnp.minimum(run_t[:, k : k + 1] - run[k : k + 1, :], 0.0))
            mix.append((fade * scores * dt[k : k + 1, :]).astype(bf16))
        skip = jnp.where(low[:1], skip_ref[h], skip_ref[h + 1])
        y_ref[:, cols] = dot(jnp.concatenate(mix, axis=1), xb) + skip * xf


def inside(xc, bc, run, step, d_skip):
    rows = lambda n: pl.BlockSpec((Q, n), lambda i: (i, 0))
    lanes = pl.BlockSpec((8, Q), lambda i: (0, i))
    return pl.pallas_call(
        inside_kernel,
        grid=(1024 // Q,),
        in_specs=[
            pl.BlockSpec(memory_space=pltpu.SMEM), rows(512), rows(256), lanes, lanes,
        ],
        out_specs=rows(512),
        out_shape=jax.ShapeDtypeStruct((1024, 512), f32),
        name="inside",
    )(d_skip, xc, bc, run, step)


def prefix_kernel(in_ref, out_ref):
    acc = jnp.zeros((32, 128), f32)
    for j in range(16):
        out_ref[j] = acc.astype(bf16)
        if j < 15:
            t = in_ref[j, 32:40, :].astype(f32)
            decay = jnp.exp(t[0:1] + t[1:2])
            acc = acc * decay + in_ref[j, 0:32, :].astype(f32)


def prefix(msg):
    return pl.pallas_call(
        prefix_kernel, out_shape=jax.ShapeDtypeStruct((16, 32, 128), bf16), name="prefix"
    )(msg)


SETS = ((0, 1, 0), (0, 3, 1), (1, 1, 2), (1, 3, 3))
WIDTHS = (1152, 1024, 1024, 1024)


def projected(g_ref, w_ref, out, here, axis, picks):
    parts = []
    for pick in picks:
        for k in range(4):
            mask = pick * 4 + k if axis == 0 else k * 4 + pick
            owner = jnp.bitwise_xor(here, mask)
            parts.append(g_ref[pl.ds(pl.multiple_of(owner * 64, 64), 64), :])
    rows = jnp.concatenate(parts, axis=0)
    out[:, :1024] = dot(rows[:, :512], w_ref[...]).astype(bf16)
    if out.shape[1] > 1024:
        out[:, 1024:] = rows[:, 512:]


def gate_kernel(
    y_ref, bc_ref, grow_ref, before_ref, states_ref, z_ref, sin_ref, gain_ref, w_ref,
    *rest,
):
    outs, (st, g, b0, b1, b2, b3, sems) = rest[:9], rest[9:]
    i = pl.program_id(0)
    here = lax.axis_index("head")
    bufs = (b0, b1, b2, b3)

    def out_copy(n):
        if n == 8:
            return pltpu.make_async_copy(g, outs[8], sems.at[8])
        q, part = n % 4, n // 4
        return pltpu.make_async_copy(
            bufs[q].at[part * 256 : part * 256 + 256], outs[n], sems.at[n]
        )

    @pl.when(i == 0)
    def _():
        for j in range(16):
            group, p = j // 4, j % 4
            st[32 * group : 32 * group + 32, 128 * p : 128 * p + 128] = sin_ref[j].astype(f32)

    @pl.when(i < 8)
    def _():
        before = jnp.exp(before_ref[...])
        low1 = lax.broadcasted_iota(jnp.int32, (1, 128), 1) < 64
        grow = dot(grow_ref[...], spread())
        c = bc_ref[:, 128:]
        squares = jnp.zeros((Q, 128), f32)
        rows = pl.ds(pl.multiple_of(i * Q, Q), Q)
        for p in range(4):
            cols = slice(128 * p, 128 * p + 128)
            entering = states_ref[:, cols].astype(f32) + st[:, cols] * pair_row(
                low1, before, 2 * p
            )
            ssd = y_ref[:, cols] + grow[:, cols] * dot(c, entering.astype(bf16))
            v = ssd * silu(z_ref[:, cols].astype(f32))
            squares = squares + v * v
            g[rows, cols] = (v * gain_ref[:, cols]).astype(bf16)
        g[rows, 512:] = dot(squares.astype(bf16), jnp.ones((128, 128), bf16)).astype(bf16)

    for q, (ax, m, _) in enumerate(SETS):

        @pl.when(i == 8 + q)
        def _(q=q, ax=ax, m=m):
            projected(g, w_ref, bufs[q], here, ax, (2, m))
            out_copy(q).start()
            out_copy(4 + q).start()

    @pl.when(i == 8)
    def _():
        out_copy(8).start()

    @pl.when(i == 11)
    def _():
        for n in range(9):
            out_copy(n).wait()


def gate(y, bc, grow, before, states, z_gate, incoming, gain, w_out):
    row = lambda i: jnp.minimum(i, 7)
    rows = lambda n: pl.BlockSpec((Q, n), lambda i: (row(i), 0))
    full = lambda *s: pl.BlockSpec(s, lambda i: (0,) * len(s))
    lanes = pl.BlockSpec((8, Q), lambda i: (0, row(i)))
    return pl.pallas_call(
        gate_kernel,
        grid=(12,),
        in_specs=[
            rows(512), rows(256), rows(16), lanes, rows(512), rows(512), full(16, 32, 128),
            full(1, 512), pl.BlockSpec((512, 1024), lambda i: (0, jnp.maximum(i - 8, 0))),
        ],
        out_specs=[pl.BlockSpec(memory_space=pl.ANY)] * 9,
        out_shape=[jax.ShapeDtypeStruct((256, n), bf16) for n in WIDTHS * 2]
        + [jax.ShapeDtypeStruct((1024, 640), bf16)],
        scratch_shapes=[pltpu.VMEM((128, 512), f32), pltpu.VMEM((1024, 640), bf16)]
        + [pltpu.VMEM((512, n), bf16) for n in WIDTHS]
        + [pltpu.SemaphoreType.DMA((9,))],
        name="gate",
    )(y, bc, grow, before, states, z_gate, incoming, gain, w_out)


def keep_kernel(g_ref, w_ref, *rest):
    outs, (b0, b1, b2, b3, sems) = rest[:8], rest[8:]
    bufs = (b0, b1, b2, b3)
    i = pl.program_id(0)
    here = lax.axis_index("head")

    def out_copy(n):
        q, part = n % 4, n // 4
        return pltpu.make_async_copy(
            bufs[q].at[part * 256 : part * 256 + 256], outs[n], sems.at[n]
        )

    for q, (ax, m, _) in enumerate(SETS):

        @pl.when(i == q)
        def _(q=q, ax=ax, m=m):
            projected(g_ref, w_ref, bufs[q], here, ax, (m ^ 2, 0))
            out_copy(q).start()
            out_copy(4 + q).start()

    @pl.when(i == 3)
    def _():
        for n in range(8):
            out_copy(n).wait()


def keep(g, w_out):
    return pl.pallas_call(
        keep_kernel,
        grid=(4,),
        in_specs=[
            pl.BlockSpec((1024, 640), lambda i: (0, 0)),
            pl.BlockSpec((512, 1024), lambda i: (0, i)),
        ],
        out_specs=[pl.BlockSpec(memory_space=pl.ANY)] * 8,
        out_shape=[jax.ShapeDtypeStruct((256, n), bf16) for n in WIDTHS * 2],
        scratch_shapes=[pltpu.VMEM((512, n), bf16) for n in WIDTHS]
        + [pltpu.SemaphoreType.DMA((8,))],
        name="keep",
    )(g, w_out)


def swap(values, axis, mask):
    mask = mask * 4 if axis == 0 else mask
    return lax.ppermute(values, "head", [(h, h ^ mask) for h in range(16)])


def added(*values):
    total = values[0].astype(f32)
    for v in values[1:]:
        total = total + v.astype(f32)
    return total


def summed_to_owners(g, sends, w_out):
    far = []
    for q, (ax, m, _) in enumerate(SETS):
        far.append(swap(sends[q], ax, m))
    near = []
    for q, (ax, m, _) in enumerate(SETS):
        near.append(swap(sends[4 + q], ax, m))
    kept = keep(g, w_out)
    passed, own = kept[:4], kept[4:]
    second = [
        swap(added(a, b).astype(bf16), ax, m ^ 2) for a, b, (ax, m, q) in zip(passed, far, SETS)
    ]
    later = []
    for (ax, m, q), a, b, c in zip(SETS, own, near, second):
        total = added(a, b, c).reshape(4, 64, -1)
        away = jnp.stack([total[m], total[2]]).astype(bf16)
        later.append((total[0], total[m ^ 2], swap(away, 1 - ax, m)))
    last = []
    for (ax, m, q), (first, second, got) in zip(SETS, later):
        last.append(
            (
                added(first, got[0]),
                swap(added(second, got[1]).astype(bf16), 1 - ax, m ^ 2),
            )
        )
    parts = [added(a, b) for a, b in last]
    scale = lax.rsqrt(parts[0][:, 1024:1025] / INNER + norm_eps)
    return jnp.concatenate([v[:, :1024] * scale for v in parts], axis=1).astype(bf16)


def layer(x_in, z_gate, b_in, c_in, dt_raw, a_log, d_skip, conv_x, conv_bc, norm_gain, w_out):
    rim = lax.ppermute(
        edge_rows(x_in, b_in, c_in), "seq", [(i, i + 1) for i in range(15)]
    )
    run, step, late, grow = decays(dt_raw, a_log)
    xc, bc, before, states, msg = block_states(
        x_in, b_in, c_in, rim, run, late, conv_x, conv_bc
    )
    pieces = prefix(lax.all_to_all(msg, "seq", 0, 0))
    incoming = lax.all_to_all(pieces, "seq", 0, 0)
    y = inside(xc, bc, run, step, d_skip)
    *sends, g = gate(
        y, bc, grow, before, states, z_gate, incoming, norm_gain[None, :], w_out
    )
    return summed_to_owners(g, sends, w_out)


def solution(mesh):
    in_specs = (
        P("seq", "head"),
        P("seq", "head"),
        P("seq", None),
        P("seq", None),
        P("seq", "head"),
        P("head"),
        P("head"),
        P(None, "head"),
        P(),
        P("head"),
        P("head", None),
    )
    out_specs = P(("seq", "head"), None)
    return jax.shard_map(
        layer, mesh=mesh, in_specs=in_specs, out_specs=out_specs, check_vma=False
    )
```

profile of v0, /device:TPU:6, one launch (start us, length us, event | category | flops | bytes accessed | tf_op | source)
XLA Modules:
  0.0 150.1 jit_solution(13106383929612924519)
XLA Ops:
  0.0 1.3 edge.1
  1.3 1.7 %collective-permute-start = (bf16[16,768]{1,0:T(8,128)(2,1)}, bf16[16,768]{1,0:T(8,128)(2,1)S(1)}, u32[]{:S(2)}, u32[]{:S(2)}) collective-permute-start(bf16[16,768]{1,0:T(8,128)(2,1)} %edge.1), channel_id=1, source_target_pairs={{0,16},{16,32},{32,48},{48,64},{64,80},{80,96},{96,112},{112,128},... | collective-permute-start | bytes 73736 | tf_op jit(solution)/shard_map/ppermute | solution.py:436
  3.1 2.6 %decays.1 = (f32[8,1024]{1,0:T(8,128)}, f32[8,1024]{1,0:T(8,128)}, bf16[1024,16]{1,0:T(8,128)(2,1)}, bf16[1024,16]{1,0:T(8,128)(2,1)}) custom-call(f32[8]{0:T(128)} %a_ref.1, f32[8,1024]{1,0:T(8,128)} %bitcast.58), custom_call_target="tpu_custom_call" | custom-call | tf_op jit(solution)/shard_map/decays/pallas_call | solution.py:85
  6.3 7.4 %states.1 = (bf16[1024,512]{1,0:T(8,128)(2,1)}, bf16[1024,256]{1,0:T(8,128)(2,1)}, f32[8,1024]{1,0:T(8,128)}, bf16[1024,512]{1,0:T(8,128)(2,1)}, bf16[16,40,128]{2,1,0:T(8,128)(2,1)}) custom-call(bf16[1024,512]{1,0:T(8,128)(2,1)} %x_ref.3, bf16[1024,128]{1,0:T(8,128)(2,1)} %b_ref.3, bf16[1024,128]{1,0:T(8,128)(2,1)} %c_ref.3, bf16[16,768]{1,0:T(8,128)(2,1)} %copy-done.8, ...), custom_call_target="tpu_custom_call" | custom-call | tf_op jit(solution)/shard_map/states/pallas_call | solution.py:171
  13.7 20.1 %all_to_all.10.in_ref = bf16[16,40,128]{2,1,0:T(8,128)(2,1)} all-to-all(bf16[16,40,128]{2,1,0:T(8,128)(2,1)} %get-tuple-element.39), channel_id=1, replica_groups=mesh['seq'=16,'head'=16] {'seq'}, dimensions={0} | all-to-all | bytes 327680 | tf_op jit(solution)/shard_map/all_to_all | solution.py:443
  33.8 1.6 %prefix.1 = bf16[16,32,128]{2,1,0:T(8,128)(2,1)} custom-call(bf16[16,40,128]{2,1,0:T(8,128)(2,1)} %all_to_all.10.in_ref), custom_call_target="tpu_custom_call" | custom-call | tf_op jit(solution)/shard_map/prefix/pallas_call | solution.py:247
  35.4 3.5 %all-to-all-start.1 = ((bf16[16,32,128]{2,1,0:T(8,128)(2,1)}), bf16[16,32,128]{2,1,0:T(8,128)(2,1)S(1)}, u32[]{:S(2)}, u32[]{:S(2)}) async-start(bf16[16,32,128]{2,1,0:T(8,128)(2,1)} %prefix.1), calls=%async_computation.1 | async-start | bytes 262144 | tf_op jit(solution)/shard_map/all_to_all | solution.py:444
  38.9 7.6 %inside.1.y_ref = f32[1024,512]{1,0:T(8,128)} custom-call(f32[8]{0:T(128)} %skip_ref.1, bf16[1024,512]{1,0:T(8,128)(2,1)} %get-tuple-element.33.xc_ref, bf16[1024,256]{1,0:T(8,128)(2,1)} %get-tuple-element.34.bc_ref, f32[8,1024]{1,0:T(8,128)} %get-tuple-element.31.run_ref, f32[8,1024]{1,0:T(8,128)} %get-tuple-element.35.step_ref), custom_call_target="tpu_custom_call" | custom-call | tf_op jit(solution)/shard_map/inside/pallas_call | solution.py:224
  46.5 1.0 all-to-all-done.1.sin_ref
  48.2 12.5 %gate.1 = (bf16[256,1152]{1,0:T(8,128)(2,1)}, bf16[256,1024]{1,0:T(8,128)(2,1)}, bf16[256,1024]{1,0:T(8,128)(2,1)}, bf16[256,1024]{1,0:T(8,128)(2,1)}, bf16[256,...) custom-call(f32[1024,512]{1,0:T(8,128)} %inside.1.y_ref, ...), custom_call_target="tpu_custom_call" | custom-call | tf_op jit(solution)/shard_map/gate/pallas_call | solution.py:334
  60.7 3.1 %collective-permute-start.17 = (bf16[256,1024]{1,0:T(8,128)(2,1)}, bf16[256,1024]{1,0:T(8,128)(2,1)S(1)}, u32[]{:S(2)}, u32[]{:S(2)}) collective-permute-start(bf16[256,1024]{1,0:T(8,128)(2,1)} %get-tuple-element.56), channel_id=1, source_target_pairs={{0,3},{1,2},{2,1},{3,0},{4,7},{5,6},{6,5},{7,4},{8,11},{9,10},{10,... | collective-permute-start | bytes 1572872 | tf_op jit(solution)/shard_map/ppermute | solution.py:395
  64.4 2.8 %collective-permute-start.7 = (bf16[256,1024]{1,0:T(8,128)(2,1)}, bf16[256,1024]{1,0:T(8,128)(2,1)S(1)}, u32[]{:S(2)}, u32[]{:S(2)}) collective-permute-start(bf16[256,1024]{1,0:T(8,128)(2,1)} %get-tuple-element.48), channel_id=1, source_target_pairs={{0,12},{1,13},{2,14},{3,15},{4,8},{5,9},{6,10},{7,11},{8,4},{9,5},... | collective-permute-start | bytes 1572872 | tf_op jit(solution)/shard_map/ppermute | solution.py:395
  67.2 1.9 %collective-permute-start.11 = (bf16[256,1024]{1,0:T(8,128)(2,1)}, bf16[256,1024]{1,0:T(8,128)(2,1)S(1)}, u32[]{:S(2)}, u32[]{:S(2)}) collective-permute-start(bf16[256,1024]{1,0:T(8,128)(2,1)} %get-tuple-element.50), channel_id=1, source_target_pairs={{0,1},{1,0},{2,3},{3,2},{4,5},{5,4},{6,7},{7,6},{8,9},{9,8},{10,11... | collective-permute-start | bytes 1572872 | tf_op jit(solution)/shard_map/ppermute | solution.py:395
  69.0 6.7 %keep.1 = (bf16[256,1152]{1,0:T(8,128)(2,1)}, bf16[256,1024]{1,0:T(8,128)(2,1)}, bf16[256,1024]{1,0:T(8,128)(2,1)}, bf16[256,1024]{1,0:T(8,128)(2,1)}, bf16[256,...) custom-call(bf16[1024,640]{1,0:T(8,128)(2,1)} %get-tuple-element.40.g_ref, ...), custom_call_target="tpu_custom_call" | custom-call | tf_op jit(solution)/shard_map/keep/pallas_call | solution.py:378
  75.8 0.9 collective-permute-done.17
  76.6 0.8 collective-permute-start.2
  77.5 1.2 add_convert_fusion.1
  78.8 3.0 %collective-permute-start.16 = (bf16[256,1024]{1,0:T(8,128)(2,1)S(1)}, bf16[256,1024]{1,0:T(8,128)(2,1)S(1)}, u32[]{:S(2)}, u32[]{:S(2)}) collective-permute-start(bf16[256,1024]{1,0:T(8,128)(2,1)S(1)} %copy-done.11), channel_id=1, source_target_pairs={{0,3},{1,2},{2,1},{3,0},{4,7},{5,6},{6,5},{7,4},{8,11},{9,10},{10,... | collective-permute-start | bytes 1572872 | tf_op jit(solution)/shard_map/ppermute | solution.py:395
  82.0 8.5 %collective-permute-done.7 = bf16[256,1024]{1,0:T(8,128)(2,1)S(1)} collective-permute-done((bf16[256,1024]{1,0:T(8,128)(2,1)}, bf16[256,1024]{1,0:T(8,128)(2,1)S(1)}, u32[]{:S(2)}, u32[]{:S(2)}) %collective-permute-start.7) | collective-permute-done | bytes 524320 | tf_op jit(solution)/shard_map/ppermute | solution.py:395
  90.8 0.9 collective-permute-done.2
  91.6 1.2 collective-permute-start.8
  93.0 4.0 %collective-permute-start.13 = (bf16[256,1024]{1,0:T(8,128)(2,1)S(1)}, bf16[256,1024]{1,0:T(8,128)(2,1)S(1)}, u32[]{:S(2)}, u32[]{:S(2)}) collective-permute-start(bf16[256,1024]{1,0:T(8,128)(2,1)S(1)} %add_convert_fusion.2), channel_id=1, source_target_pairs={{0,3},{1,2},{2,1},{3,0},{4,7},{5,6},{6,5},{7,4},{8,11},{9,10},{10,... | collective-permute-start | bytes 1572872 | tf_op jit(solution)/shard_map/ppermute | solution.py:395
  97.0 19.3 %collective-permute-done.8 = bf16[256,1024]{1,0:T(8,128)(2,1)S(1)} collective-permute-done((bf16[256,1024]{1,0:T(8,128)(2,1)S(1)}, bf16[256,1024]{1,0:T(8,128)(2,1)S(1)}, u32[]{:S(2)}, u32[]{:S(2)}) %collective-permute-start.8) | collective-permute-done | bytes 524320 | tf_op jit(solution)/shard_map/ppermute | solution.py:395
  116.3 1.6 %collective-permute-start.18 = (bf16[256,1024]{1,0:T(8,128)(2,1)S(1)}, bf16[256,1024]{1,0:T(8,128)(2,1)S(1)}, u32[]{:S(2)}, u32[]{:S(2)}) collective-permute-start(bf16[256,1024]{1,0:T(8,128)(2,1)S(1)} %add_convert_fusion.1), channel_id=1, source_target_pairs={{0,1},{1,0},{2,3},{3,2},{4,5},{5,4},{6,7},{7,6},{8,9},{9,8},{10,11... | collective-permute-start | bytes 1572872 | tf_op jit(solution)/shard_map/ppermute | solution.py:395
  119.8 0.9 collective-permute-start.14
  120.7 7.9 %collective-permute-done.18 = bf16[256,1024]{1,0:T(8,128)(2,1)S(1)} collective-permute-done((bf16[256,1024]{1,0:T(8,128)(2,1)S(1)}, bf16[256,1024]{1,0:T(8,128)(2,1)S(1)}, u32[]{:S(2)}, u32[]{:S(2)}) %collective-permute-start.18) | collective-permute-done | bytes 524320 | tf_op jit(solution)/shard_map/ppermute | solution.py:395
  129.5 5.7 %collective-permute-done.3 = bf16[256,1152]{1,0:T(8,128)(2,1)S(1)} collective-permute-done((bf16[256,1152]{1,0:T(8,128)(2,1)S(1)}, bf16[256,1152]{1,0:T(8,128)(2,1)S(1)}, u32[]{:S(2)}, u32[]{:S(2)}) %collective-permute-start.3) | collective-permute-done | bytes 589856 | tf_op jit(solution)/shard_map/ppermute | solution.py:395
  135.7 2.1 %collective-permute-start.10 = (bf16[64,1024]{1,0:T(8,128)(2,1)S(1)}, bf16[64,1024]{1,0:T(8,128)(2,1)S(1)}, u32[]{:S(2)}, u32[]{:S(2)}) collective-permute-start(bf16[64,1024]{1,0:T(8,128)(2,1)S(1)} %fusion.10), channel_id=1, source_target_pairs={{0,1},{1,0},{2,3},{3,2},{4,5},{5,4},{6,7},{7,6},{8,9},{9,8},{10,11... | collective-permute-start | bytes 393224 | tf_op jit(solution)/shard_map/ppermute | solution.py:395
  138.4 4.0 %collective-permute-done.4 = bf16[2,64,1152]{2,1,0:T(8,128)(2,1)S(1)} collective-permute-done((bf16[2,64,1152]{2,1,0:T(8,128)(2,1)S(1)}, bf16[2,64,1152]{2,1,0:T(8,128)(2,1)S(1)}, u32[]{:S(2)}, u32[]{:S(2)}) %collective-permute-start.4) | collective-permute-done | bytes 294944 | tf_op jit(solution)/shard_map/ppermute | solution.py:395
  142.4 0.8 collective-permute-start.5
  143.3 5.5 %collective-permute-done.5 = bf16[64,1152]{1,0:T(8,128)(2,1)S(1)} collective-permute-done((bf16[64,1152]{1,0:T(8,128)(2,1)S(1)}, bf16[64,1152]{1,0:T(8,128)(2,1)S(1)}, u32[]{:S(2)}, u32[]{:S(2)}) %collective-permute-start.5) | collective-permute-done | bytes 147488 | tf_op jit(solution)/shard_map/ppermute | solution.py:395
  149.2 0.8 pad_maximum_fusion
  (68 shorter events, 6.7 us)
Async XLA Ops:
  1.3 4.3 %collective-permute-start = (bf16[16,768]{1,0:T(8,128)(2,1)}, bf16[16,768]{1,0:T(8,128)(2,1)S(1)}, u32[]{:S(2)}, u32[]{:S(2)}) collective-permute-start(bf16[16,768]{1,0:T(8,128)(2,1)} %edge.1), channel_id=1, source_target_pairs={{0,16},{16,32},{32,48},{48,64},{64,80},{80,96},{96,112},{112,128},... | collective-permute-start | bytes 73736 | tf_op jit(solution)/shard_map/ppermute | solution.py:436
  35.4 12.1 %all-to-all-start.1 = ((bf16[16,32,128]{2,1,0:T(8,128)(2,1)}), bf16[16,32,128]{2,1,0:T(8,128)(2,1)S(1)}, u32[]{:S(2)}, u32[]{:S(2)}) async-start(bf16[16,32,128]{2,1,0:T(8,128)(2,1)} %prefix.1), calls=%async_computation.1 | async-start | bytes 262144 | tf_op jit(solution)/shard_map/all_to_all | solution.py:444
  60.7 16.0 %collective-permute-start.17 = (bf16[256,1024]{1,0:T(8,128)(2,1)}, bf16[256,1024]{1,0:T(8,128)(2,1)S(1)}, u32[]{:S(2)}, u32[]{:S(2)}) collective-permute-start(bf16[256,1024]{1,0:T(8,128)(2,1)} %get-tuple-element.56), channel_id=1, source_target_pairs={{0,3},{1,2},{2,1},{3,0},{4,7},{5,6},{6,5},{7,4},{8,11},{9,10},{10,... | collective-permute-start | bytes 1572872 | tf_op jit(solution)/shard_map/ppermute | solution.py:395
  63.8 15.0 %collective-permute-start.12 = (bf16[256,1024]{1,0:T(8,128)(2,1)}, bf16[256,1024]{1,0:T(8,128)(2,1)S(1)}, u32[]{:S(2)}, u32[]{:S(2)}) collective-permute-start(bf16[256,1024]{1,0:T(8,128)(2,1)} %get-tuple-element.52), channel_id=1, source_target_pairs={{0,1},{1,0},{2,3},{3,2},{4,5},{5,4},{6,7},{7,6},{8,9},{9,8},{10,11... | collective-permute-start | bytes 1572872 | tf_op jit(solution)/shard_map/ppermute | solution.py:395
  63.9 29.1 %collective-permute-start.6 = (bf16[256,1024]{1,0:T(8,128)(2,1)}, bf16[256,1024]{1,0:T(8,128)(2,1)S(1)}, u32[]{:S(2)}, u32[]{:S(2)}) collective-permute-start(bf16[256,1024]{1,0:T(8,128)(2,1)} %get-tuple-element.46), channel_id=1, source_target_pairs={{0,12},{1,13},{2,14},{3,15},{4,8},{5,9},{6,10},{7,11},{8,4},{9,5},... | collective-permute-start | bytes 1572872 | tf_op jit(solution)/shard_map/ppermute | solution.py:395
  64.4 26.2 %collective-permute-start.7 = (bf16[256,1024]{1,0:T(8,128)(2,1)}, bf16[256,1024]{1,0:T(8,128)(2,1)S(1)}, u32[]{:S(2)}, u32[]{:S(2)}) collective-permute-start(bf16[256,1024]{1,0:T(8,128)(2,1)} %get-tuple-element.48), channel_id=1, source_target_pairs={{0,12},{1,13},{2,14},{3,15},{4,8},{5,9},{6,10},{7,11},{8,4},{9,5},... | collective-permute-start | bytes 1572872 | tf_op jit(solution)/shard_map/ppermute | solution.py:395
  67.2 51.1 %collective-permute-start.11 = (bf16[256,1024]{1,0:T(8,128)(2,1)}, bf16[256,1024]{1,0:T(8,128)(2,1)S(1)}, u32[]{:S(2)}, u32[]{:S(2)}) collective-permute-start(bf16[256,1024]{1,0:T(8,128)(2,1)} %get-tuple-element.50), channel_id=1, source_target_pairs={{0,1},{1,0},{2,3},{3,2},{4,5},{5,4},{6,7},{7,6},{8,9},{9,8},{10,11... | collective-permute-start | bytes 1572872 | tf_op jit(solution)/shard_map/ppermute | solution.py:395
  69.0 7.6 %copy-start.10 = (bf16[256,1152]{1,0:T(8,128)(2,1)S(1)}, bf16[256,1152]{1,0:T(8,128)(2,1)}, u32[]{:S(2)}) copy-start(bf16[256,1152]{1,0:T(8,128)(2,1)} %get-tuple-element.44) | copy-start | bytes 1769476
  75.7 3.1 %copy-start.11 = (bf16[256,1024]{1,0:T(8,128)(2,1)S(1)}, bf16[256,1024]{1,0:T(8,128)(2,1)}, u32[]{:S(2)}) copy-start(bf16[256,1024]{1,0:T(8,128)(2,1)} %get-tuple-element.54) | copy-start | bytes 1572868
  75.7 6.0 %copy-start.4 = (bf16[256,1024]{1,0:T(8,128)(2,1)S(1)}, bf16[256,1024]{1,0:T(8,128)(2,1)}, u32[]{:S(2)}) copy-start(bf16[256,1024]{1,0:T(8,128)(2,1)} %get-tuple-element.51) | copy-start | bytes 1572868
  76.6 15.0 %collective-permute-start.2 = (bf16[256,1152]{1,0:T(8,128)(2,1)S(1)}, bf16[256,1152]{1,0:T(8,128)(2,1)S(1)}, u32[]{:S(2)}, u32[]{:S(2)}) collective-permute-start(bf16[256,1152]{1,0:T(8,128)(2,1)S(1)} %copy-done.10), channel_id=1, source_target_pairs={{0,4},{1,5},{2,6},{3,7},{4,0},{5,1},{6,2},{7,3},{8,12},{9,13},{10,... | collective-permute-start | bytes 1769480 | tf_op jit(solution)/shard_map/ppermute | solution.py:395
  78.7 11.8 %copy-start.9 = (bf16[256,1152]{1,0:T(8,128)(2,1)S(1)}, bf16[256,1152]{1,0:T(8,128)(2,1)}, u32[]{:S(2)}) copy-start(bf16[256,1152]{1,0:T(8,128)(2,1)} %get-tuple-element.42) | copy-start | bytes 1769476
  78.7 11.8 %copy-start.3 = (bf16[256,1024]{1,0:T(8,128)(2,1)S(1)}, bf16[256,1024]{1,0:T(8,128)(2,1)}, u32[]{:S(2)}) copy-start(bf16[256,1024]{1,0:T(8,128)(2,1)} %get-tuple-element.47) | copy-start | bytes 1572868
  78.8 41.0 %collective-permute-start.16 = (bf16[256,1024]{1,0:T(8,128)(2,1)S(1)}, bf16[256,1024]{1,0:T(8,128)(2,1)S(1)}, u32[]{:S(2)}, u32[]{:S(2)}) collective-permute-start(bf16[256,1024]{1,0:T(8,128)(2,1)S(1)} %copy-done.11), channel_id=1, source_target_pairs={{0,3},{1,2},{2,1},{3,0},{4,7},{5,6},{6,5},{7,4},{8,11},{9,10},{10,... | collective-permute-start | bytes 1572872 | tf_op jit(solution)/shard_map/ppermute | solution.py:395
  82.0 10.9 %copy-start.1 = (bf16[256,1152]{1,0:T(8,128)(2,1)S(1)}, bf16[256,1152]{1,0:T(8,128)(2,1)}, u32[]{:S(2)}) copy-start(bf16[256,1152]{1,0:T(8,128)(2,1)} %get-tuple-element.43) | copy-start | bytes 1769476
  90.5 39.0 %collective-permute-start.1 = (bf16[256,1152]{1,0:T(8,128)(2,1)S(1)}, bf16[256,1152]{1,0:T(8,128)(2,1)S(1)}, u32[]{:S(2)}, u32[]{:S(2)}) collective-permute-start(bf16[256,1152]{1,0:T(8,128)(2,1)S(1)} %copy-done.9), channel_id=1, source_target_pairs={{0,4},{1,5},{2,6},{3,7},{4,0},{5,1},{6,2},{7,3},{8,12},{9,13},{10,... | collective-permute-start | bytes 1769480 | tf_op jit(solution)/shard_map/ppermute | solution.py:395
  90.8 27.2 %copy-start.7 = (bf16[256,1024]{1,0:T(8,128)(2,1)S(1)}, bf16[256,1024]{1,0:T(8,128)(2,1)}, u32[]{:S(2)}) copy-start(bf16[256,1024]{1,0:T(8,128)(2,1)} %get-tuple-element.45) | copy-start | bytes 1572868
  91.6 24.7 %collective-permute-start.8 = (bf16[256,1024]{1,0:T(8,128)(2,1)S(1)}, bf16[256,1024]{1,0:T(8,128)(2,1)S(1)}, u32[]{:S(2)}, u32[]{:S(2)}) collective-permute-start(bf16[256,1024]{1,0:T(8,128)(2,1)S(1)} %add_convert_fusion.3), channel_id=1, source_target_pairs={{0,4},{1,5},{2,6},{3,7},{4,0},{5,1},{6,2},{7,3},{8,12},{9,13},{10,... | collective-permute-start | bytes 1572872 | tf_op jit(solution)/shard_map/ppermute | solution.py:395
  93.0 25.8 %collective-permute-start.13 = (bf16[256,1024]{1,0:T(8,128)(2,1)S(1)}, bf16[256,1024]{1,0:T(8,128)(2,1)S(1)}, u32[]{:S(2)}, u32[]{:S(2)}) collective-permute-start(bf16[256,1024]{1,0:T(8,128)(2,1)S(1)} %add_convert_fusion.2), channel_id=1, source_target_pairs={{0,3},{1,2},{2,1},{3,0},{4,7},{5,6},{6,5},{7,4},{8,11},{9,10},{10,... | collective-permute-start | bytes 1572872 | tf_op jit(solution)/shard_map/ppermute | solution.py:395
  116.3 12.3 %collective-permute-start.18 = (bf16[256,1024]{1,0:T(8,128)(2,1)S(1)}, bf16[256,1024]{1,0:T(8,128)(2,1)S(1)}, u32[]{:S(2)}, u32[]{:S(2)}) collective-permute-start(bf16[256,1024]{1,0:T(8,128)(2,1)S(1)} %add_convert_fusion.1), channel_id=1, source_target_pairs={{0,1},{1,0},{2,3},{3,2},{4,5},{5,4},{6,7},{7,6},{8,9},{9,8},{10,11... | collective-permute-start | bytes 1572872 | tf_op jit(solution)/shard_map/ppermute | solution.py:395
  118.2 1.2 copy-start.6
  118.3 17.0 %collective-permute-start.3 = (bf16[256,1152]{1,0:T(8,128)(2,1)S(1)}, bf16[256,1152]{1,0:T(8,128)(2,1)S(1)}, u32[]{:S(2)}, u32[]{:S(2)}) collective-permute-start(bf16[256,1152]{1,0:T(8,128)(2,1)S(1)} %add_convert_fusion), channel_id=1, source_target_pairs={{0,12},{1,13},{2,14},{3,15},{4,8},{5,9},{6,10},{7,11},{8,4},{9,5},... | collective-permute-start | bytes 1769480 | tf_op jit(solution)/shard_map/ppermute | solution.py:395
  118.8 16.8 %collective-permute-start.9 = (bf16[2,64,1024]{2,1,0:T(8,128)(2,1)S(1)}, bf16[2,64,1024]{2,1,0:T(8,128)(2,1)S(1)}, u32[]{:S(2)}, u32[]{:S(2)}) collective-permute-start(bf16[2,64,1024]{2,1,0:T(8,128)(2,1)S(1)} %pad_maximum_fusion.2), channel_id=1, source_target_pairs={{0,3},{1,2},{2,1},{3,0},{4,7},{5,6},{6,5},{7,4},{8,11},{9,10},{10,... | collective-permute-start | bytes 786440 | tf_op jit(solution)/shard_map/ppermute | solution.py:395
  119.7 8.9 %copy-start.5 = (bf16[256,1024]{1,0:T(8,128)(2,1)S(1)}, bf16[256,1024]{1,0:T(8,128)(2,1)}, u32[]{:S(2)}) copy-start(bf16[256,1024]{1,0:T(8,128)(2,1)} %get-tuple-element.53) | copy-start | bytes 1572868
  119.8 18.0 %collective-permute-start.14 = (bf16[2,64,1024]{2,1,0:T(8,128)(2,1)S(1)}, bf16[2,64,1024]{2,1,0:T(8,128)(2,1)S(1)}, u32[]{:S(2)}, u32[]{:S(2)}) collective-permute-start(bf16[2,64,1024]{2,1,0:T(8,128)(2,1)S(1)} %pad_maximum_fusion.3), channel_id=1, source_target_pairs={{0,4},{1,5},{2,6},{3,7},{4,0},{5,1},{6,2},{7,3},{8,12},{9,13},{10,... | collective-permute-start | bytes 786440 | tf_op jit(solution)/shard_map/ppermute | solution.py:395
  128.9 6.4 %copy-start = (bf16[256,1152]{1,0:T(8,128)(2,1)S(1)}, bf16[256,1152]{1,0:T(8,128)(2,1)}, u32[]{:S(2)}) copy-start(bf16[256,1152]{1,0:T(8,128)(2,1)} %get-tuple-element.41) | copy-start | bytes 1769476
  128.9 14.2 %collective-permute-start.19 = (bf16[2,64,1024]{2,1,0:T(8,128)(2,1)S(1)}, bf16[2,64,1024]{2,1,0:T(8,128)(2,1)S(1)}, u32[]{:S(2)}, u32[]{:S(2)}) collective-permute-start(bf16[2,64,1024]{2,1,0:T(8,128)(2,1)S(1)} %pad_maximum_fusion.4), channel_id=1, source_target_pairs={{0,12},{1,13},{2,14},{3,15},{4,8},{5,9},{6,10},{7,11},{8,4},{9,5},... | collective-permute-start | bytes 786440 | tf_op jit(solution)/shard_map/ppermute | solution.py:395
  135.5 6.8 %collective-permute-start.4 = (bf16[2,64,1152]{2,1,0:T(8,128)(2,1)S(1)}, bf16[2,64,1152]{2,1,0:T(8,128)(2,1)S(1)}, u32[]{:S(2)}, u32[]{:S(2)}) collective-permute-start(bf16[2,64,1152]{2,1,0:T(8,128)(2,1)S(1)} %pad_maximum_fusion.1), channel_id=1, source_target_pairs={{0,1},{1,0},{2,3},{3,2},{4,5},{5,4},{6,7},{7,6},{8,9},{9,8},{10,11... | collective-permute-start | bytes 884744 | tf_op jit(solution)/shard_map/ppermute | solution.py:395
  135.7 13.3 %collective-permute-start.10 = (bf16[64,1024]{1,0:T(8,128)(2,1)S(1)}, bf16[64,1024]{1,0:T(8,128)(2,1)S(1)}, u32[]{:S(2)}, u32[]{:S(2)}) collective-permute-start(bf16[64,1024]{1,0:T(8,128)(2,1)S(1)} %fusion.10), channel_id=1, source_target_pairs={{0,1},{1,0},{2,3},{3,2},{4,5},{5,4},{6,7},{7,6},{8,9},{9,8},{10,11... | collective-permute-start | bytes 393224 | tf_op jit(solution)/shard_map/ppermute | solution.py:395
  137.8 11.2 %collective-permute-start.15 = (bf16[64,1024]{1,0:T(8,128)(2,1)S(1)}, bf16[64,1024]{1,0:T(8,128)(2,1)S(1)}, u32[]{:S(2)}, u32[]{:S(2)}) collective-permute-start(bf16[64,1024]{1,0:T(8,128)(2,1)S(1)} %fusion.6), channel_id=1, source_target_pairs={{0,12},{1,13},{2,14},{3,15},{4,8},{5,9},{6,10},{7,11},{8,4},{9,5},... | collective-permute-start | bytes 393224 | tf_op jit(solution)/shard_map/ppermute | solution.py:395
  142.4 6.4 %collective-permute-start.5 = (bf16[64,1152]{1,0:T(8,128)(2,1)S(1)}, bf16[64,1152]{1,0:T(8,128)(2,1)S(1)}, u32[]{:S(2)}, u32[]{:S(2)}) collective-permute-start(bf16[64,1152]{1,0:T(8,128)(2,1)S(1)} %fusion), channel_id=1, source_target_pairs={{0,3},{1,2},{2,1},{3,0},{4,7},{5,6},{6,5},{7,4},{8,11},{9,10},{10,... | collective-permute-start | bytes 442376 | tf_op jit(solution)/shard_map/ppermute | solution.py:395
  143.2 5.8 %collective-permute-start.20 = (bf16[64,1024]{1,0:T(8,128)(2,1)S(1)}, bf16[64,1024]{1,0:T(8,128)(2,1)S(1)}, u32[]{:S(2)}, u32[]{:S(2)}) collective-permute-start(bf16[64,1024]{1,0:T(8,128)(2,1)S(1)} %fusion.2), channel_id=1, source_target_pairs={{0,4},{1,5},{2,6},{3,7},{4,0},{5,1},{6,2},{7,3},{8,12},{9,13},{10,... | collective-permute-start | bytes 393224 | tf_op jit(solution)/shard_map/ppermute | solution.py:395
  (2 other events, 1.3 us)
where the time goes:
time: 151 us; the launch traced here: 150 us
  waiting for transfers between devices  53.8 us (36%)
  Pallas kernels  39.7 us (26%)
  starting transfers between devices  30.5 us (20%)
  blocking collectives  20.1 us (13%)
  other arithmetic  4.26 us (3%)
    ppermute x20, waiting for transfers between devices, swap(): return lax.ppermute(values, 'head', [(h, h ^ mask) for h in range(16)])  52.8 us
    ppermute x20, starting transfers between devices, swap(): return lax.ppermute(values, 'head', [(h, h ^ mask) for h in range(16)])  25.2 us
    all_to_all x1, blocking collectives, layer(): pieces = prefix(lax.all_to_all(msg, 'seq', 0, 0))  20.1 us
    pallas_call x1, Pallas kernels, gate(): pl.pallas_call(gate_kernel, grid=(12,), in_specs=[rows(512), rows(256), r...  12.5 us
    pallas_call x1, Pallas kernels, inside(): pl.pallas_call(inside_kernel, grid=(1024 // Q,), in_specs=[pl.BlockSpec(m...  7.61 us
    pallas_call x1, Pallas kernels, block_states(): pl.pallas_call(state_kernel, grid=(1024 // Q,), in_specs=[rows(512), rows...  7.41 us
    pallas_call x1, Pallas kernels, keep(): pl.pallas_call(keep_kernel, grid=(4,), in_specs=[pl.BlockSpec((1024, 640)...  6.68 us
    all_to_all x1, starting transfers between devices, layer(): incoming = lax.all_to_all(pieces, 'seq', 0, 0)  3.51 us
  transfers between devices with their start and end apart: 22, of which 10 were waited for; matrix products, arithmetic and copies ran while one was open for 2% of the time, Pallas kernels for 11%

commit v1 on v0

--- a/solution.py
+++ b/solution.py
@@ -9,8 +9,13 @@
 INNER = 8192
 norm_eps = 1e-05
 Q = 128
+PARAMS = pltpu.CompilerParams(vmem_limit_bytes=24 * 2**20)
 bf16 = jnp.bfloat16
 f32 = jnp.float32
+
+
+def in_hbm(v):
+    return pltpu.with_memory_space_constraint(v, pltpu.HBM)
 
 
 def silu(v):
@@ -49,7 +54,8 @@
         out_specs=pl.BlockSpec((16, 768), lambda i: (0, 0)),
         out_shape=jax.ShapeDtypeStruct((16, 768), bf16),
         name="edge",
-    )(x_in, b_in, c_in)
+        compiler_params=PARAMS,
+    )(in_hbm(x_in), in_hbm(b_in), in_hbm(c_in))
 
 
 def pair_row(low, values, h):
@@ -90,6 +96,7 @@
         out_shape=[jax.ShapeDtypeStruct((8, 1024), f32)] * 2
         + [jax.ShapeDtypeStruct((1024, 16), bf16)] * 2,
         name="decays",
+        compiler_params=PARAMS,
     )(a_log, dt_raw.T)
 
 
@@ -177,10 +184,10 @@
         ],
         out_specs=[rows(512), rows(256), lanes, rows(512), full(16, 40, 128)],
         out_shape=[
-            jax.ShapeDtypeStruct((1024, 512), bf16),
+            pltpu.HBM((1024, 512), bf16),
             jax.ShapeDtypeStruct((1024, 256), bf16),
             jax.ShapeDtypeStruct((8, 1024), f32),
-            jax.ShapeDtypeStruct((1024, 512), bf16),
+            pltpu.HBM((1024, 512), bf16),
             jax.ShapeDtypeStruct((16, 40, 128), bf16),
         ],
         scratch_shapes=[
@@ -190,6 +197,7 @@
             pltpu.VMEM((8, Q), f32),
         ],
         name="states",
+        compiler_params=PARAMS,
     )(x_in, b_in, c_in, rim, run, late, conv_x, conv_bc)
 
 
@@ -230,7 +238,8 @@
         out_specs=rows(512),
         out_shape=jax.ShapeDtypeStruct((1024, 512), f32),
         name="inside",
-    )(d_skip, xc, bc, run, step)
+        compiler_params=PARAMS,
+    )(d_skip, in_hbm(xc), bc, run, step)
 
 
 def prefix_kernel(in_ref, out_ref):
@@ -245,7 +254,8 @@
 
 def prefix(msg):
     return pl.pallas_call(
-        prefix_kernel, out_shape=jax.ShapeDtypeStruct((16, 32, 128), bf16), name="prefix"
+        prefix_kernel, out_shape=jax.ShapeDtypeStruct((16, 32, 128), bf16), name="prefix",
+        compiler_params=PARAMS
     )(msg)
 
 
@@ -253,7 +263,7 @@
 WIDTHS = (1152, 1024, 1024, 1024)
 
 
-def projected(g_ref, w_ref, out, here, axis, picks):
+def projected(g_ref, w_ref, q, out, here, axis, picks):
     parts = []
     for pick in picks:
         for k in range(4):
@@ -261,16 +271,16 @@
             owner = jnp.bitwise_xor(here, mask)
             parts.append(g_ref[pl.ds(pl.multiple_of(owner * 64, 64), 64), :])
     rows = jnp.concatenate(parts, axis=0)
-    out[:, :1024] = dot(rows[:, :512], w_ref[...]).astype(bf16)
+    out[:, :1024] = dot(rows[:, :512], w_ref[:, q * 1024 : q * 1024 + 1024]).astype(bf16)
     if out.shape[1] > 1024:
         out[:, 1024:] = rows[:, 512:]
 
 
 def gate_kernel(
-    y_ref, bc_ref, grow_ref, before_ref, states_ref, z_ref, sin_ref, gain_ref, w_ref,
+    y_ref, bc_ref, grow_ref, before_ref, states_hbm, z_hbm, sin_ref, gain_ref, w_ref,
     *rest,
 ):
-    outs, (st, g, b0, b1, b2, b3, sems) = rest[:9], rest[9:]
+    outs, (st, g, w, zs, ss, b0, b1, b2, b3, sems) = rest[:9], rest[9:]
     i = pl.program_id(0)
     here = lax.axis_index("head")
     bufs = (b0, b1, b2, b3)
@@ -283,14 +293,32 @@
             bufs[q].at[part * 256 : part * 256 + 256], outs[n], sems.at[n]
         )
 
+    def w_copy(q):
+        cols = slice(1024 * q, 1024 * q + 1024)
+        return pltpu.make_async_copy(w_ref.at[:, cols], w.at[:, cols], sems.at[9 + q])
+
+    def in_copies(k):
+        part = pl.ds(pl.multiple_of(k * Q, Q), Q)
+        return (
+            pltpu.make_async_copy(z_hbm.at[part, :], zs.at[part, :], sems.at[13 + k]),
+            pltpu.make_async_copy(states_hbm.at[part, :], ss.at[part, :], sems.at[21 + k]),
+        )
+
     @pl.when(i == 0)
     def _():
+        for k in range(8):
+            for copy in in_copies(k):
+                copy.start()
+        for q in range(4):
+            w_copy(q).start()
         for j in range(16):
             group, p = j // 4, j % 4
             st[32 * group : 32 * group + 32, 128 * p : 128 * p + 128] = sin_ref[j].astype(f32)
 
     @pl.when(i < 8)
     def _():
+        for copy in in_copies(i):
+            copy.wait()
         before = jnp.exp(before_ref[...])
         low1 = lax.broadcasted_iota(jnp.int32, (1, 128), 1) < 64
         grow = dot(grow_ref[...], spread())
@@ -299,11 +327,11 @@
         rows = pl.ds(pl.multiple_of(i * Q, Q), Q)
         for p in range(4):
             cols = slice(128 * p, 128 * p + 128)
-            entering = states_ref[:, cols].astype(f32) + st[:, cols] * pair_row(
+            entering = ss[rows, cols].astype(f32) + st[:, cols] * pair_row(
                 low1, before, 2 * p
             )
             ssd = y_ref[:, cols] + grow[:, cols] * dot(c, entering.astype(bf16))
-            v = ssd * silu(z_ref[:, cols].astype(f32))
+            v = ssd * silu(zs[rows, cols].astype(f32))
             squares = squares + v * v
             g[rows, cols] = (v * gain_ref[:, cols]).astype(bf16)
         g[rows, 512:] = dot(squares.astype(bf16), jnp.ones((128, 128), bf16)).astype(bf16)
@@ -312,7 +340,8 @@
 
         @pl.when(i == 8 + q)
         def _(q=q, ax=ax, m=m):
-            projected(g, w_ref, bufs[q], here, ax, (2, m))
+            w_copy(q).wait()
+            projected(g, w, q, bufs[q], here, ax, (2, m))
             out_copy(q).start()
             out_copy(4 + q).start()
 
@@ -331,21 +360,29 @@
     rows = lambda n: pl.BlockSpec((Q, n), lambda i: (row(i), 0))
     full = lambda *s: pl.BlockSpec(s, lambda i: (0,) * len(s))
     lanes = pl.BlockSpec((8, Q), lambda i: (0, row(i)))
+    anywhere = pl.BlockSpec(memory_space=pl.ANY)
     return pl.pallas_call(
         gate_kernel,
         grid=(12,),
         in_specs=[
-            rows(512), rows(256), rows(16), lanes, rows(512), rows(512), full(16, 32, 128),
-            full(1, 512), pl.BlockSpec((512, 1024), lambda i: (0, jnp.maximum(i - 8, 0))),
+            rows(512), rows(256), rows(16), lanes, anywhere, anywhere, full(16, 32, 128),
+            full(1, 512), anywhere,
         ],
         out_specs=[pl.BlockSpec(memory_space=pl.ANY)] * 9,
         out_shape=[jax.ShapeDtypeStruct((256, n), bf16) for n in WIDTHS * 2]
         + [jax.ShapeDtypeStruct((1024, 640), bf16)],
-        scratch_shapes=[pltpu.VMEM((128, 512), f32), pltpu.VMEM((1024, 640), bf16)]
+        scratch_shapes=[
+            pltpu.VMEM((128, 512), f32),
+            pltpu.VMEM((1024, 640), bf16),
+            pltpu.VMEM((512, 4096), bf16),
+            pltpu.VMEM((1024, 512), bf16),
+            pltpu.VMEM((1024, 512), bf16),
+        ]
         + [pltpu.VMEM((512, n), bf16) for n in WIDTHS]
-        + [pltpu.SemaphoreType.DMA((9,))],
+        + [pltpu.SemaphoreType.DMA((29,))],
         name="gate",
-    )(y, bc, grow, before, states, z_gate, incoming, gain, w_out)
+        compiler_params=PARAMS,
+    )(y, bc, grow, before, in_hbm(states), in_hbm(z_gate), incoming, gain, in_hbm(w_out))
 
 
 def keep_kernel(g_ref, w_ref, *rest):
@@ -364,7 +401,7 @@
 
         @pl.when(i == q)
         def _(q=q, ax=ax, m=m):
-            projected(g_ref, w_ref, bufs[q], here, ax, (m ^ 2, 0))
+            projected(g_ref, w_ref, q, bufs[q], here, ax, (m ^ 2, 0))
             out_copy(q).start()
             out_copy(4 + q).start()
 
@@ -380,14 +417,15 @@
         grid=(4,),
         in_specs=[
             pl.BlockSpec((1024, 640), lambda i: (0, 0)),
-            pl.BlockSpec((512, 1024), lambda i: (0, i)),
+            pl.BlockSpec(memory_space=pltpu.VMEM),
         ],
         out_specs=[pl.BlockSpec(memory_space=pl.ANY)] * 8,
         out_shape=[jax.ShapeDtypeStruct((256, n), bf16) for n in WIDTHS * 2],
         scratch_shapes=[pltpu.VMEM((512, n), bf16) for n in WIDTHS]
         + [pltpu.SemaphoreType.DMA((8,))],
         name="keep",
-    )(g, w_out)
+        compiler_params=PARAMS,
+    )(g, pltpu.with_memory_space_constraint(w_out, pltpu.VMEM))
 
 
 def swap(values, axis, mask):
@@ -464,6 +502,4 @@
         P("head", None),
     )
     out_specs = P(("seq", "head"), None)
-    return jax.shard_map(
-        layer, mesh=mesh, in_specs=in_specs, out_specs=out_specs, check_vma=False
-    )
+    return jax.shard_map(layer, mesh=mesh, in_specs=in_specs, out_specs=out_specs, check_vma=False)

time: 151 us -> 141 us (0.934)
  the two profiles are of different devices: /device:TPU:6 before, /device:TPU:2 now
where the time goes in v1:
time: 141 us; the launch traced here: 138 us
  waiting for transfers between devices  50.7 us (36%)
  starting transfers between devices  36.9 us (26%)
  Pallas kernels  26.5 us (19%)
  blocking collectives  19.8 us (14%)
  other arithmetic  3.25 us (2%)
    ppermute x20, waiting for transfers between devices, swap(): return lax.ppermute(values, 'head', [(h, h ^ mask) for h in range(16)])  48.5 us
    ppermute x20, starting transfers between devices, swap(): return lax.ppermute(values, 'head', [(h, h ^ mask) for h in range(16)])  31.6 us
    all_to_all x1, blocking collectives, layer(): pieces = prefix(lax.all_to_all(msg, 'seq', 0, 0))  19.8 us
    pallas_call x1, Pallas kernels, gate(): pl.pallas_call(gate_kernel, grid=(12,), in_specs=[rows(512), rows(256), r...  8.32 us
    pallas_call x1, Pallas kernels, inside(): pl.pallas_call(inside_kernel, grid=(1024 // Q,), in_specs=[pl.BlockSpec(m...  6.38 us
    pallas_call x1, Pallas kernels, block_states(): pl.pallas_call(state_kernel, grid=(1024 // Q,), in_specs=[rows(512), rows...  5.17 us
    all_to_all x1, starting transfers between devices, layer(): incoming = lax.all_to_all(pieces, 'seq', 0, 0)  3.51 us
    pallas_call x1, Pallas kernels, keep(): pl.pallas_call(keep_kernel, grid=(4,), in_specs=[pl.BlockSpec((1024, 640)...  3.48 us
  transfers between devices with their start and end apart: 22, of which 11 were waited for; matrix products, arithmetic and copies ran while one was open for 2% of the time, Pallas kernels for 8%

profile of v1, /device:TPU:2, one launch (start us, length us, event | category | flops | bytes accessed | tf_op | source)
XLA Modules:
  0.0 138.4 jit_solution(3752095900752598984)
XLA Ops:
  0.9 1.7 %collective-permute-start = (bf16[16,768]{1,0:T(8,128)(2,1)S(1)}, bf16[16,768]{1,0:T(8,128)(2,1)S(1)}, u32[]{:S(2)}, u32[]{:S(2)}) collective-permute-start(bf16[16,768]{1,0:T(8,128)(2,1)S(1)} %edge.1), channel_id=1, source_target_pairs={{0,16},{16,32},{32,48},{48,64},{64,80},{80,96},{96,112},{112,128},... | collective-permute-start | bytes 73736 | tf_op jit(solution)/shard_map/ppermute | solution.py:474
  3.4 1.6 %decays.1 = (f32[8,1024]{1,0:T(8,128)S(1)}, f32[8,1024]{1,0:T(8,128)S(1)}, bf16[1024,16]{1,0:T(8,128)(2,1)S(1)}, bf16[1024,16]{1,0:T(8,128)(2,1)S(1)}) custom-call(f32[8]{0:T(128)S(1)} %copy-done.8, f32[8,1024]{1,0:T(8,128)S(1)} %bitcast.58), custom_call_target="tpu_custom_call" | custom-call | tf_op jit(solution)/shard_map/decays/pallas_call | solution.py:91
  5.0 5.2 %states.1 = (bf16[1024,512]{1,0:T(8,128)(2,1)}, bf16[1024,256]{1,0:T(8,128)(2,1)S(1)}, f32[8,1024]{1,0:T(8,128)S(1)}, bf16[1024,512]{1,0:T(8,128)(2,1)}, bf16[16,40,128]{2,1,0:T(8,128)(2,1)S(1)}) custom-call(bf16[1024,512]{1,0:T(8,128)(2,1)S(1)} %copy-done.1, bf16[1024,128]{1,0:T(8,128)(2,1)S(1)} %copy-done.2, bf16[1024,128]{1,0:T(8,128)(2,1)S(1)} %copy-done.3, ...), custom_call_target="tpu_custom_call" | custom-call | tf_op jit(solution)/shard_map/states/pallas_call | solution.py:178
  10.2 19.8 %all_to_all.10.in_ref = bf16[16,40,128]{2,1,0:T(8,128)(2,1)S(1)} all-to-all(bf16[16,40,128]{2,1,0:T(8,128)(2,1)S(1)} %get-tuple-element.39), channel_id=1, replica_groups=mesh['seq'=16,'head'=16] {'seq'}, dimensions={0} | all-to-all | bytes 327680 | tf_op jit(solution)/shard_map/all_to_all | solution.py:481
  30.7 3.5 %all-to-all-start.1 = ((bf16[16,32,128]{2,1,0:T(8,128)(2,1)}), bf16[16,32,128]{2,1,0:T(8,128)(2,1)S(1)}, u32[]{:S(2)}, u32[]{:S(2)}) async-start(bf16[16,32,128]{2,1,0:T(8,128)(2,1)} %prefix.1), calls=%async_computation.1 | async-start | bytes 262144 | tf_op jit(solution)/shard_map/all_to_all | solution.py:482
  34.2 6.4 %inside.1.y_ref = f32[1024,512]{1,0:T(8,128)S(1)} custom-call(f32[8]{0:T(128)S(1)} %copy-done.9, bf16[1024,512]{1,0:T(8,128)(2,1)} %get-tuple-element.33.xc_ref, bf16[1024,256]{1,0:T(8,128)(2,1)S(1)} %get-tuple-element.34.bc_ref, f32[8,1024]{1,0:T(8,128)S(1)} %get-tuple-element.31.run_ref, f32[8,1024]{1,0:T(8,128)S(1)} %get-tuple-element.35.step_ref), custom_call_target="tpu_custom_call" | custom-call | tf_op jit(solution)/shard_map/inside/pallas_call | solution.py:232
  40.6 2.2 %all-to-all-done.1.sin_ref = bf16[16,32,128]{2,1,0:T(8,128)(2,1)S(1)} async-done(((bf16[16,32,128]{2,1,0:T(8,128)(2,1)}), bf16[16,32,128]{2,1,0:T(8,128)(2,1)S(1)}, u32[]{:S(2)}, u32[]{:S(2)}) %all-to-all-start.1) | async-done | bytes 131104 | tf_op jit(solution)/shard_map/all_to_all | solution.py:482
  42.8 8.3 %gate.1 = (bf16[256,1152]{1,0:T(8,128)(2,1)S(1)}, bf16[256,1024]{1,0:T(8,128)(2,1)S(1)}, bf16[256,1024]{1,0:T(8,128)(2,1)S(1)}, bf16[256,1024]{1,0:T(8,128)(2,1)...) custom-call(f32[1024,512]{1,0:T(8,128)S(1)} %inside.1.y_ref, ...), custom_call_target="tpu_custom_call" | custom-call | tf_op jit(solution)/shard_map/gate/pallas_call | solution.py:364
  51.2 3.1 %collective-permute-start.17 = (bf16[256,1024]{1,0:T(8,128)(2,1)S(1)}, bf16[256,1024]{1,0:T(8,128)(2,1)S(1)}, u32[]{:S(2)}, u32[]{:S(2)}) collective-permute-start(bf16[256,1024]{1,0:T(8,128)(2,1)S(1)} %get-tuple-element.56), channel_id=1, source_target_pairs={{0,3},{1,2},{2,1},{3,0},{4,7},{5,6},{6,5},{7,4},{8,11},{9,10},{10,... | collective-permute-start | bytes 1572872 | tf_op jit(solution)/shard_map/ppermute | solution.py:433
  54.4 1.5 %collective-permute-start.6 = (bf16[256,1024]{1,0:T(8,128)(2,1)S(1)}, bf16[256,1024]{1,0:T(8,128)(2,1)S(1)}, u32[]{:S(2)}, u32[]{:S(2)}) collective-permute-start(bf16[256,1024]{1,0:T(8,128)(2,1)S(1)} %get-tuple-element.46), channel_id=1, source_target_pairs={{0,12},{1,13},{2,14},{3,15},{4,8},{5,9},{6,10},{7,11},{8,4},{9,5},... | collective-permute-start | bytes 1572872 | tf_op jit(solution)/shard_map/ppermute | solution.py:433
  56.4 1.9 %collective-permute-start.11 = (bf16[256,1024]{1,0:T(8,128)(2,1)S(1)}, bf16[256,1024]{1,0:T(8,128)(2,1)S(1)}, u32[]{:S(2)}, u32[]{:S(2)}) collective-permute-start(bf16[256,1024]{1,0:T(8,128)(2,1)S(1)} %get-tuple-element.50), channel_id=1, source_target_pairs={{0,1},{1,0},{2,3},{3,2},{4,5},{5,4},{6,7},{7,6},{8,9},{9,8},{10,11... | collective-permute-start | bytes 1572872 | tf_op jit(solution)/shard_map/ppermute | solution.py:433
  58.3 3.5 %keep.1 = (bf16[256,1152]{1,0:T(8,128)(2,1)S(1)}, bf16[256,1024]{1,0:T(8,128)(2,1)S(1)}, bf16[256,1024]{1,0:T(8,128)(2,1)S(1)}, bf16[256,1024]{1,0:T(8,128)(2,1)...) custom-call(bf16[1024,640]{1,0:T(8,128)(2,1)S(1)} %get-tuple-element, ...), custom_call_target="tpu_custom_call" | custom-call | tf_op jit(solution)/shard_map/keep/pallas_call | solution.py:415
  61.8 5.1 %collective-permute-done.17 = bf16[256,1024]{1,0:T(8,128)(2,1)S(1)} collective-permute-done((bf16[256,1024]{1,0:T(8,128)(2,1)S(1)}, bf16[256,1024]{1,0:T(8,128)(2,1)S(1)}, u32[]{:S(2)}, u32[]{:S(2)}) %collective-permute-start.17) | collective-permute-done | bytes 524320 | tf_op jit(solution)/shard_map/ppermute | solution.py:433
  67.6 1.4 %collective-permute-done.12 = bf16[256,1024]{1,0:T(8,128)(2,1)S(1)} collective-permute-done((bf16[256,1024]{1,0:T(8,128)(2,1)S(1)}, bf16[256,1024]{1,0:T(8,128)(2,1)S(1)}, u32[]{:S(2)}, u32[]{:S(2)}) %collective-permute-start.12) | collective-permute-done | bytes 524320 | tf_op jit(solution)/shard_map/ppermute | solution.py:433
  69.1 1.6 %collective-permute-start.16 = (bf16[256,1024]{1,0:T(8,128)(2,1)S(1)}, bf16[256,1024]{1,0:T(8,128)(2,1)S(1)}, u32[]{:S(2)}, u32[]{:S(2)}) collective-permute-start(bf16[256,1024]{1,0:T(8,128)(2,1)S(1)} %get-tuple-element.54), channel_id=1, source_target_pairs={{0,3},{1,2},{2,1},{3,0},{4,7},{5,6},{6,5},{7,4},{8,11},{9,10},{10,... | collective-permute-start | bytes 1572872 | tf_op jit(solution)/shard_map/ppermute | solution.py:433
  70.9 8.7 %collective-permute-done.7 = bf16[256,1024]{1,0:T(8,128)(2,1)S(1)} collective-permute-done((bf16[256,1024]{1,0:T(8,128)(2,1)S(1)}, bf16[256,1024]{1,0:T(8,128)(2,1)S(1)}, u32[]{:S(2)}, u32[]{:S(2)}) %collective-permute-start.7) | collective-permute-done | bytes 524320 | tf_op jit(solution)/shard_map/ppermute | solution.py:433
  79.6 1.7 %collective-permute-start.1 = (bf16[256,1152]{1,0:T(8,128)(2,1)S(1)}, bf16[256,1152]{1,0:T(8,128)(2,1)S(1)}, u32[]{:S(2)}, u32[]{:S(2)}) collective-permute-start(bf16[256,1152]{1,0:T(8,128)(2,1)S(1)} %get-tuple-element.42), channel_id=1, source_target_pairs={{0,4},{1,5},{2,6},{3,7},{4,0},{5,1},{6,2},{7,3},{8,12},{9,13},{10,... | collective-permute-start | bytes 1769480 | tf_op jit(solution)/shard_map/ppermute | solution.py:433
  82.6 4.4 %collective-permute-start.13 = (bf16[256,1024]{1,0:T(8,128)(2,1)S(1)}, bf16[256,1024]{1,0:T(8,128)(2,1)S(1)}, u32[]{:S(2)}, u32[]{:S(2)}) collective-permute-start(bf16[256,1024]{1,0:T(8,128)(2,1)S(1)} %add_convert_fusion.2), channel_id=1, source_target_pairs={{0,3},{1,2},{2,1},{3,0},{4,7},{5,6},{6,5},{7,4},{8,11},{9,10},{10,... | collective-permute-start | bytes 1572872 | tf_op jit(solution)/shard_map/ppermute | solution.py:433
  87.0 18.8 %collective-permute-done.8 = bf16[256,1024]{1,0:T(8,128)(2,1)S(1)} collective-permute-done((bf16[256,1024]{1,0:T(8,128)(2,1)S(1)}, bf16[256,1024]{1,0:T(8,128)(2,1)S(1)}, u32[]{:S(2)}, u32[]{:S(2)}) %collective-permute-start.8) | collective-permute-done | bytes 524320 | tf_op jit(solution)/shard_map/ppermute | solution.py:433
  105.8 1.2 collective-permute-start.18
  107.3 2.2 %collective-permute-start.3 = (bf16[256,1152]{1,0:T(8,128)(2,1)S(1)}, bf16[256,1152]{1,0:T(8,128)(2,1)S(1)}, u32[]{:S(2)}, u32[]{:S(2)}) collective-permute-start(bf16[256,1152]{1,0:T(8,128)(2,1)S(1)} %add_convert_fusion), channel_id=1, source_target_pairs={{0,12},{1,13},{2,14},{3,15},{4,8},{5,9},{6,10},{7,11},{8,4},{9,5},... | collective-permute-start | bytes 1769480 | tf_op jit(solution)/shard_map/ppermute | solution.py:433
  109.6 1.0 collective-permute-start.9
  111.0 1.9 %collective-permute-start.14 = (bf16[2,64,1024]{2,1,0:T(8,128)(2,1)S(1)}, bf16[2,64,1024]{2,1,0:T(8,128)(2,1)S(1)}, u32[]{:S(2)}, u32[]{:S(2)}) collective-permute-start(bf16[2,64,1024]{2,1,0:T(8,128)(2,1)S(1)} %pad_maximum_fusion.3), channel_id=1, source_target_pairs={{0,4},{1,5},{2,6},{3,7},{4,0},{5,1},{6,2},{7,3},{8,12},{9,13},{10,... | collective-permute-start | bytes 786440 | tf_op jit(solution)/shard_map/ppermute | solution.py:433
  112.9 5.6 %collective-permute-done.18 = bf16[256,1024]{1,0:T(8,128)(2,1)S(1)} collective-permute-done((bf16[256,1024]{1,0:T(8,128)(2,1)S(1)}, bf16[256,1024]{1,0:T(8,128)(2,1)S(1)}, u32[]{:S(2)}, u32[]{:S(2)}) %collective-permute-start.18) | collective-permute-done | bytes 524320 | tf_op jit(solution)/shard_map/ppermute | solution.py:433
  118.8 1.7 %collective-permute-start.19 = (bf16[2,64,1024]{2,1,0:T(8,128)(2,1)S(1)}, bf16[2,64,1024]{2,1,0:T(8,128)(2,1)S(1)}, u32[]{:S(2)}, u32[]{:S(2)}) collective-permute-start(bf16[2,64,1024]{2,1,0:T(8,128)(2,1)S(1)} %pad_maximum_fusion.4), channel_id=1, source_target_pairs={{0,12},{1,13},{2,14},{3,15},{4,8},{5,9},{6,10},{7,11},{8,4},{9,5},... | collective-permute-start | bytes 786440 | tf_op jit(solution)/shard_map/ppermute | solution.py:433
  120.5 2.7 %collective-permute-done.3 = bf16[256,1152]{1,0:T(8,128)(2,1)S(1)} collective-permute-done((bf16[256,1152]{1,0:T(8,128)(2,1)S(1)}, bf16[256,1152]{1,0:T(8,128)(2,1)S(1)}, u32[]{:S(2)}, u32[]{:S(2)}) %collective-permute-start.3) | collective-permute-done | bytes 589856 | tf_op jit(solution)/shard_map/ppermute | solution.py:433
  124.1 1.7 %collective-permute-start.10 = (bf16[64,1024]{1,0:T(8,128)(2,1)S(1)}, bf16[64,1024]{1,0:T(8,128)(2,1)S(1)}, u32[]{:S(2)}, u32[]{:S(2)}) collective-permute-start(bf16[64,1024]{1,0:T(8,128)(2,1)S(1)} %fusion.10), channel_id=1, source_target_pairs={{0,1},{1,0},{2,3},{3,2},{4,5},{5,4},{6,7},{7,6},{8,9},{9,8},{10,11... | collective-permute-start | bytes 393224 | tf_op jit(solution)/shard_map/ppermute | solution.py:433
  125.8 2.1 %collective-permute-start.15 = (bf16[64,1024]{1,0:T(8,128)(2,1)S(1)}, bf16[64,1024]{1,0:T(8,128)(2,1)S(1)}, u32[]{:S(2)}, u32[]{:S(2)}) collective-permute-start(bf16[64,1024]{1,0:T(8,128)(2,1)S(1)} %fusion.6), channel_id=1, source_target_pairs={{0,12},{1,13},{2,14},{3,15},{4,8},{5,9},{6,10},{7,11},{8,4},{9,5},... | collective-permute-start | bytes 393224 | tf_op jit(solution)/shard_map/ppermute | solution.py:433
  127.9 2.4 %collective-permute-done.4 = bf16[2,64,1152]{2,1,0:T(8,128)(2,1)S(1)} collective-permute-done((bf16[2,64,1152]{2,1,0:T(8,128)(2,1)S(1)}, bf16[2,64,1152]{2,1,0:T(8,128)(2,1)S(1)}, u32[]{:S(2)}, u32[]{:S(2)}) %collective-permute-start.4) | collective-permute-done | bytes 294944 | tf_op jit(solution)/shard_map/ppermute | solution.py:433
  130.4 1.8 %collective-permute-start.5 = (bf16[64,1152]{1,0:T(8,128)(2,1)S(1)}, bf16[64,1152]{1,0:T(8,128)(2,1)S(1)}, u32[]{:S(2)}, u32[]{:S(2)}) collective-permute-start(bf16[64,1152]{1,0:T(8,128)(2,1)S(1)} %fusion), channel_id=1, source_target_pairs={{0,3},{1,2},{2,1},{3,0},{4,7},{5,6},{6,5},{7,4},{8,11},{9,10},{10,... | collective-permute-start | bytes 442376 | tf_op jit(solution)/shard_map/ppermute | solution.py:433
  132.2 1.9 %collective-permute-start.20 = (bf16[64,1024]{1,0:T(8,128)(2,1)S(1)}, bf16[64,1024]{1,0:T(8,128)(2,1)S(1)}, u32[]{:S(2)}, u32[]{:S(2)}) collective-permute-start(bf16[64,1024]{1,0:T(8,128)(2,1)S(1)} %fusion.2), channel_id=1, source_target_pairs={{0,4},{1,5},{2,6},{3,7},{4,0},{5,1},{6,2},{7,3},{8,12},{9,13},{10,... | collective-permute-start | bytes 393224 | tf_op jit(solution)/shard_map/ppermute | solution.py:433
  134.1 2.7 %collective-permute-done.5 = bf16[64,1152]{1,0:T(8,128)(2,1)S(1)} collective-permute-done((bf16[64,1152]{1,0:T(8,128)(2,1)S(1)}, bf16[64,1152]{1,0:T(8,128)(2,1)S(1)}, u32[]{:S(2)}, u32[]{:S(2)}) %collective-permute-start.5) | collective-permute-done | bytes 147488 | tf_op jit(solution)/shard_map/ppermute | solution.py:433
  (64 shorter events, 8.6 us)
Async XLA Ops:
  0.0 5.0 %copy-start.3 = (bf16[1024,128]{1,0:T(8,128)(2,1)S(1)}, bf16[1024,128]{1,0:T(8,128)(2,1)}, u32[]{:S(2)}) copy-start(bf16[1024,128]{1,0:T(8,128)(2,1)} %c_ref.3) | copy-start | bytes 786436
  0.0 5.0 %copy-start.2 = (bf16[1024,128]{1,0:T(8,128)(2,1)S(1)}, bf16[1024,128]{1,0:T(8,128)(2,1)}, u32[]{:S(2)}) copy-start(bf16[1024,128]{1,0:T(8,128)(2,1)} %b_ref.3) | copy-start | bytes 786436
  0.0 5.0 %copy-start.1 = (bf16[1024,512]{1,0:T(8,128)(2,1)S(1)}, bf16[1024,512]{1,0:T(8,128)(2,1)}, u32[]{:S(2)}) copy-start(bf16[1024,512]{1,0:T(8,128)(2,1)} %x_ref.3) | copy-start | bytes 3145732
  0.0 2.6 %copy-start.8 = (f32[8]{0:T(128)S(1)}, f32[8]{0:T(128)}, u32[]{:S(2)}) copy-start(f32[8]{0:T(128)} %a_ref.1) | copy-start | bytes 100
  0.0 5.0 %copy-start.6 = (f32[4,256]{1,0:T(4,128)S(1)}, f32[4,256]{1,0:T(4,128)}, u32[]{:S(2)}) copy-start(f32[4,256]{1,0:T(4,128)} %wbc_ref.1) | copy-start | bytes 12292
  0.0 5.0 %copy-start.5 = (f32[4,512]{1,0:T(4,128)S(1)}, f32[4,512]{1,0:T(4,128)}, u32[]{:S(2)}) copy-start(f32[4,512]{1,0:T(4,128)} %wx_ref.1) | copy-start | bytes 24580
  0.9 4.1 %collective-permute-start = (bf16[16,768]{1,0:T(8,128)(2,1)S(1)}, bf16[16,768]{1,0:T(8,128)(2,1)S(1)}, u32[]{:S(2)}, u32[]{:S(2)}) collective-permute-start(bf16[16,768]{1,0:T(8,128)(2,1)S(1)} %edge.1), channel_id=1, source_target_pairs={{0,16},{16,32},{32,48},{48,64},{64,80},{80,96},{96,112},{112,128},... | collective-permute-start | bytes 73736 | tf_op jit(solution)/shard_map/ppermute | solution.py:474
  2.6 0.8 copy-start.4
  5.0 29.2 %copy-start.9 = (f32[8]{0:T(128)S(1)}, f32[8]{0:T(128)}, u32[]{:S(2)}) copy-start(f32[8]{0:T(128)} %skip_ref.1) | copy-start | bytes 100
  30.7 12.1 %all-to-all-start.1 = ((bf16[16,32,128]{2,1,0:T(8,128)(2,1)}), bf16[16,32,128]{2,1,0:T(8,128)(2,1)S(1)}, u32[]{:S(2)}, u32[]{:S(2)}) async-start(bf16[16,32,128]{2,1,0:T(8,128)(2,1)} %prefix.1), calls=%async_computation.1 | async-start | bytes 262144 | tf_op jit(solution)/shard_map/all_to_all | solution.py:482
  34.2 8.6 %copy-start.7 = (f32[512]{0:T(512)S(1)}, f32[512]{0:T(512)}, u32[]{:S(2)}) copy-start(f32[512]{0:T(512)} %param.20) | copy-start | bytes 6148
  42.8 15.5 %copy-start = (bf16[512,4096]{1,0:T(8,128)(2,1)S(1)}, bf16[512,4096]{1,0:T(8,128)(2,1)}, u32[]{:S(2)}) copy-start(bf16[512,4096]{1,0:T(8,128)(2,1)} %w_ref.3) | copy-start | bytes 12582916
  51.2 15.8 %collective-permute-start.17 = (bf16[256,1024]{1,0:T(8,128)(2,1)S(1)}, bf16[256,1024]{1,0:T(8,128)(2,1)S(1)}, u32[]{:S(2)}, u32[]{:S(2)}) collective-permute-start(bf16[256,1024]{1,0:T(8,128)(2,1)S(1)} %get-tuple-element.56), channel_id=1, source_target_pairs={{0,3},{1,2},{2,1},{3,0},{4,7},{5,6},{6,5},{7,4},{8,11},{9,10},{10,... | collective-permute-start | bytes 1572872 | tf_op jit(solution)/shard_map/ppermute | solution.py:433
  54.3 14.8 %collective-permute-start.12 = (bf16[256,1024]{1,0:T(8,128)(2,1)S(1)}, bf16[256,1024]{1,0:T(8,128)(2,1)S(1)}, u32[]{:S(2)}, u32[]{:S(2)}) collective-permute-start(bf16[256,1024]{1,0:T(8,128)(2,1)S(1)} %get-tuple-element.52), channel_id=1, source_target_pairs={{0,1},{1,0},{2,3},{3,2},{4,5},{5,4},{6,7},{7,6},{8,9},{9,8},{10,11... | collective-permute-start | bytes 1572872 | tf_op jit(solution)/shard_map/ppermute | solution.py:433
  54.4 28.2 %collective-permute-start.6 = (bf16[256,1024]{1,0:T(8,128)(2,1)S(1)}, bf16[256,1024]{1,0:T(8,128)(2,1)S(1)}, u32[]{:S(2)}, u32[]{:S(2)}) collective-permute-start(bf16[256,1024]{1,0:T(8,128)(2,1)S(1)} %get-tuple-element.46), channel_id=1, source_target_pairs={{0,12},{1,13},{2,14},{3,15},{4,8},{5,9},{6,10},{7,11},{8,4},{9,5},... | collective-permute-start | bytes 1572872 | tf_op jit(solution)/shard_map/ppermute | solution.py:433
  55.9 23.7 %collective-permute-start.7 = (bf16[256,1024]{1,0:T(8,128)(2,1)S(1)}, bf16[256,1024]{1,0:T(8,128)(2,1)S(1)}, u32[]{:S(2)}, u32[]{:S(2)}) collective-permute-start(bf16[256,1024]{1,0:T(8,128)(2,1)S(1)} %get-tuple-element.48), channel_id=1, source_target_pairs={{0,12},{1,13},{2,14},{3,15},{4,8},{5,9},{6,10},{7,11},{8,4},{9,5},... | collective-permute-start | bytes 1572872 | tf_op jit(solution)/shard_map/ppermute | solution.py:433
  56.4 50.9 %collective-permute-start.11 = (bf16[256,1024]{1,0:T(8,128)(2,1)S(1)}, bf16[256,1024]{1,0:T(8,128)(2,1)S(1)}, u32[]{:S(2)}, u32[]{:S(2)}) collective-permute-start(bf16[256,1024]{1,0:T(8,128)(2,1)S(1)} %get-tuple-element.50), channel_id=1, source_target_pairs={{0,1},{1,0},{2,3},{3,2},{4,5},{5,4},{6,7},{7,6},{8,9},{9,8},{10,11... | collective-permute-start | bytes 1572872 | tf_op jit(solution)/shard_map/ppermute | solution.py:433
  66.9 15.4 %collective-permute-start.2 = (bf16[256,1152]{1,0:T(8,128)(2,1)S(1)}, bf16[256,1152]{1,0:T(8,128)(2,1)S(1)}, u32[]{:S(2)}, u32[]{:S(2)}) collective-permute-start(bf16[256,1152]{1,0:T(8,128)(2,1)S(1)} %get-tuple-element.44), channel_id=1, source_target_pairs={{0,4},{1,5},{2,6},{3,7},{4,0},{5,1},{6,2},{7,3},{8,12},{9,13},{10,... | collective-permute-start | bytes 1769480 | tf_op jit(solution)/shard_map/ppermute | solution.py:433
  69.1 41.9 %collective-permute-start.16 = (bf16[256,1024]{1,0:T(8,128)(2,1)S(1)}, bf16[256,1024]{1,0:T(8,128)(2,1)S(1)}, u32[]{:S(2)}, u32[]{:S(2)}) collective-permute-start(bf16[256,1024]{1,0:T(8,128)(2,1)S(1)} %get-tuple-element.54), channel_id=1, source_target_pairs={{0,3},{1,2},{2,1},{3,0},{4,7},{5,6},{6,5},{7,4},{8,11},{9,10},{10,... | collective-permute-start | bytes 1572872 | tf_op jit(solution)/shard_map/ppermute | solution.py:433
  79.6 40.9 %collective-permute-start.1 = (bf16[256,1152]{1,0:T(8,128)(2,1)S(1)}, bf16[256,1152]{1,0:T(8,128)(2,1)S(1)}, u32[]{:S(2)}, u32[]{:S(2)}) collective-permute-start(bf16[256,1152]{1,0:T(8,128)(2,1)S(1)} %get-tuple-element.42), channel_id=1, source_target_pairs={{0,4},{1,5},{2,6},{3,7},{4,0},{5,1},{6,2},{7,3},{8,12},{9,13},{10,... | collective-permute-start | bytes 1769480 | tf_op jit(solution)/shard_map/ppermute | solution.py:433
  82.3 23.5 %collective-permute-start.8 = (bf16[256,1024]{1,0:T(8,128)(2,1)S(1)}, bf16[256,1024]{1,0:T(8,128)(2,1)S(1)}, u32[]{:S(2)}, u32[]{:S(2)}) collective-permute-start(bf16[256,1024]{1,0:T(8,128)(2,1)S(1)} %add_convert_fusion.3), channel_id=1, source_target_pairs={{0,4},{1,5},{2,6},{3,7},{4,0},{5,1},{6,2},{7,3},{8,12},{9,13},{10,... | collective-permute-start | bytes 1572872 | tf_op jit(solution)/shard_map/ppermute | solution.py:433
  82.6 27.0 %collective-permute-start.13 = (bf16[256,1024]{1,0:T(8,128)(2,1)S(1)}, bf16[256,1024]{1,0:T(8,128)(2,1)S(1)}, u32[]{:S(2)}, u32[]{:S(2)}) collective-permute-start(bf16[256,1024]{1,0:T(8,128)(2,1)S(1)} %add_convert_fusion.2), channel_id=1, source_target_pairs={{0,3},{1,2},{2,1},{3,0},{4,7},{5,6},{6,5},{7,4},{8,11},{9,10},{10,... | collective-permute-start | bytes 1572872 | tf_op jit(solution)/shard_map/ppermute | solution.py:433
  105.8 12.7 %collective-permute-start.18 = (bf16[256,1024]{1,0:T(8,128)(2,1)S(1)}, bf16[256,1024]{1,0:T(8,128)(2,1)S(1)}, u32[]{:S(2)}, u32[]{:S(2)}) collective-permute-start(bf16[256,1024]{1,0:T(8,128)(2,1)S(1)} %add_convert_fusion.1), channel_id=1, source_target_pairs={{0,1},{1,0},{2,3},{3,2},{4,5},{5,4},{6,7},{7,6},{8,9},{9,8},{10,11... | collective-permute-start | bytes 1572872 | tf_op jit(solution)/shard_map/ppermute | solution.py:433
  107.3 15.9 %collective-permute-start.3 = (bf16[256,1152]{1,0:T(8,128)(2,1)S(1)}, bf16[256,1152]{1,0:T(8,128)(2,1)S(1)}, u32[]{:S(2)}, u32[]{:S(2)}) collective-permute-start(bf16[256,1152]{1,0:T(8,128)(2,1)S(1)} %add_convert_fusion), channel_id=1, source_target_pairs={{0,12},{1,13},{2,14},{3,15},{4,8},{5,9},{6,10},{7,11},{8,4},{9,5},... | collective-permute-start | bytes 1769480 | tf_op jit(solution)/shard_map/ppermute | solution.py:433
  109.6 14.4 %collective-permute-start.9 = (bf16[2,64,1024]{2,1,0:T(8,128)(2,1)S(1)}, bf16[2,64,1024]{2,1,0:T(8,128)(2,1)S(1)}, u32[]{:S(2)}, u32[]{:S(2)}) collective-permute-start(bf16[2,64,1024]{2,1,0:T(8,128)(2,1)S(1)} %pad_maximum_fusion.2), channel_id=1, source_target_pairs={{0,3},{1,2},{2,1},{3,0},{4,7},{5,6},{6,5},{7,4},{8,11},{9,10},{10,... | collective-permute-start | bytes 786440 | tf_op jit(solution)/shard_map/ppermute | solution.py:433
  111.0 14.7 %collective-permute-start.14 = (bf16[2,64,1024]{2,1,0:T(8,128)(2,1)S(1)}, bf16[2,64,1024]{2,1,0:T(8,128)(2,1)S(1)}, u32[]{:S(2)}, u32[]{:S(2)}) collective-permute-start(bf16[2,64,1024]{2,1,0:T(8,128)(2,1)S(1)} %pad_maximum_fusion.3), channel_id=1, source_target_pairs={{0,4},{1,5},{2,6},{3,7},{4,0},{5,1},{6,2},{7,3},{8,12},{9,13},{10,... | collective-permute-start | bytes 786440 | tf_op jit(solution)/shard_map/ppermute | solution.py:433
  118.8 13.4 %collective-permute-start.19 = (bf16[2,64,1024]{2,1,0:T(8,128)(2,1)S(1)}, bf16[2,64,1024]{2,1,0:T(8,128)(2,1)S(1)}, u32[]{:S(2)}, u32[]{:S(2)}) collective-permute-start(bf16[2,64,1024]{2,1,0:T(8,128)(2,1)S(1)} %pad_maximum_fusion.4), channel_id=1, source_target_pairs={{0,12},{1,13},{2,14},{3,15},{4,8},{5,9},{6,10},{7,11},{8,4},{9,5},... | collective-permute-start | bytes 786440 | tf_op jit(solution)/shard_map/ppermute | solution.py:433
  123.5 6.8 %collective-permute-start.4 = (bf16[2,64,1152]{2,1,0:T(8,128)(2,1)S(1)}, bf16[2,64,1152]{2,1,0:T(8,128)(2,1)S(1)}, u32[]{:S(2)}, u32[]{:S(2)}) collective-permute-start(bf16[2,64,1152]{2,1,0:T(8,128)(2,1)S(1)} %pad_maximum_fusion.1), channel_id=1, source_target_pairs={{0,1},{1,0},{2,3},{3,2},{4,5},{5,4},{6,7},{7,6},{8,9},{9,8},{10,11... | collective-permute-start | bytes 884744 | tf_op jit(solution)/shard_map/ppermute | solution.py:433
  124.1 12.9 %collective-permute-start.10 = (bf16[64,1024]{1,0:T(8,128)(2,1)S(1)}, bf16[64,1024]{1,0:T(8,128)(2,1)S(1)}, u32[]{:S(2)}, u32[]{:S(2)}) collective-permute-start(bf16[64,1024]{1,0:T(8,128)(2,1)S(1)} %fusion.10), channel_id=1, source_target_pairs={{0,1},{1,0},{2,3},{3,2},{4,5},{5,4},{6,7},{7,6},{8,9},{9,8},{10,11... | collective-permute-start | bytes 393224 | tf_op jit(solution)/shard_map/ppermute | solution.py:433
  125.8 11.2 %collective-permute-start.15 = (bf16[64,1024]{1,0:T(8,128)(2,1)S(1)}, bf16[64,1024]{1,0:T(8,128)(2,1)S(1)}, u32[]{:S(2)}, u32[]{:S(2)}) collective-permute-start(bf16[64,1024]{1,0:T(8,128)(2,1)S(1)} %fusion.6), channel_id=1, source_target_pairs={{0,12},{1,13},{2,14},{3,15},{4,8},{5,9},{6,10},{7,11},{8,4},{9,5},... | collective-permute-start | bytes 393224 | tf_op jit(solution)/shard_map/ppermute | solution.py:433
  130.4 6.4 %collective-permute-start.5 = (bf16[64,1152]{1,0:T(8,128)(2,1)S(1)}, bf16[64,1152]{1,0:T(8,128)(2,1)S(1)}, u32[]{:S(2)}, u32[]{:S(2)}) collective-permute-start(bf16[64,1152]{1,0:T(8,128)(2,1)S(1)} %fusion), channel_id=1, source_target_pairs={{0,3},{1,2},{2,1},{3,0},{4,7},{5,6},{6,5},{7,4},{8,11},{9,10},{10,... | collective-permute-start | bytes 442376 | tf_op jit(solution)/shard_map/ppermute | solution.py:433
  132.2 5.1 %collective-permute-start.20 = (bf16[64,1024]{1,0:T(8,128)(2,1)S(1)}, bf16[64,1024]{1,0:T(8,128)(2,1)S(1)}, u32[]{:S(2)}, u32[]{:S(2)}) collective-permute-start(bf16[64,1024]{1,0:T(8,128)(2,1)S(1)} %fusion.2), channel_id=1, source_target_pairs={{0,4},{1,5},{2,6},{3,7},{4,0},{5,1},{6,2},{7,3},{8,12},{9,13},{10,... | collective-permute-start | bytes 393224 | tf_op jit(solution)/shard_map/ppermute | solution.py:433

commit v2 on v1

--- a/solution.py
+++ b/solution.py
@@ -109,10 +109,18 @@
 
 def state_kernel(
     x_ref, b_ref, c_ref, rim_ref, run_ref, late_ref, wx_ref, wbc_ref,
-    xc_ref, bc_ref, before_ref, states_ref, msg_ref,
-    xs, bs, st, tot,
+    xc_hbm, bc_ref, before_ref, states_hbm, msg_ref,
+    xs, bs, st, tot, xc_ref, states_ref, sems,
 ):
     i = pl.program_id(0)
+    here = pl.ds(pl.multiple_of(i * Q, Q), Q)
+
+    def out_copies(k):
+        part = pl.ds(pl.multiple_of(k * Q, Q), Q)
+        return (
+            pltpu.make_async_copy(xc_ref.at[part, :], xc_hbm.at[part, :], sems.at[k]),
+            pltpu.make_async_copy(states_ref.at[part, :], states_hbm.at[part, :], sems.at[8 + k]),
+        )
 
     @pl.when(i == 0)
     def _():
@@ -145,15 +153,17 @@
     b_t = jnp.transpose(b).astype(bf16)
     low1 = lax.broadcasted_iota(jnp.int32, (1, 128), 1) < 64
     late = dot(late_ref[...], spread())
-    states_ref[...] = st[...].astype(bf16)
+    states_ref[here, :] = st[...].astype(bf16)
     before_ref[...] = tot[...]
     for p in range(4):
         cols = slice(128 * p, 128 * p + 128)
         xp = conv(xs, wx_ref, cols)
-        xc_ref[:, cols] = xp.astype(bf16)
+        xc_ref[here, cols] = xp.astype(bf16)
         end = jnp.exp(pair_row(low1, fin, 2 * p))
         st[:, cols] = st[:, cols] * end + dot(b_t, (xp * late[:, cols]).astype(bf16))
     tot[...] = tot[...] + fin
+    for copy in out_copies(i):
+        copy.start()
 
     @pl.when(i == pl.num_programs(0) - 1)
     def _():
@@ -169,12 +179,16 @@
                     32 * group : 32 * group + 32, 128 * p : 128 * p + 128
                 ].astype(bf16)
                 msg_ref[j, 32:40, :] = tile
+        for k in range(8):
+            for copy in out_copies(k):
+                copy.wait()
 
 
 def block_states(x_in, b_in, c_in, rim, run, late, conv_x, conv_bc):
     rows = lambda n: pl.BlockSpec((Q, n), lambda i: (i, 0))
     full = lambda *s: pl.BlockSpec(s, lambda i: (0,) * len(s))
     lanes = pl.BlockSpec((8, Q), lambda i: (0, i))
+    anywhere = pl.BlockSpec(memory_space=pl.ANY)
     return pl.pallas_call(
         state_kernel,
         grid=(1024 // Q,),
@@ -182,7 +196,7 @@
             rows(512), rows(128), rows(128), full(16, 768), lanes, rows(16),
             full(4, 512), full(4, 256),
         ],
-        out_specs=[rows(512), rows(256), lanes, rows(512), full(16, 40, 128)],
+        out_specs=[anywhere, rows(256), lanes, anywhere, full(16, 40, 128)],
         out_shape=[
             pltpu.HBM((1024, 512), bf16),
             jax.ShapeDtypeStruct((1024, 256), bf16),
@@ -195,6 +209,9 @@
             pltpu.VMEM((Q + 8, 256), f32),
             pltpu.VMEM((128, 512), f32),
             pltpu.VMEM((8, Q), f32),
+            pltpu.VMEM((1024, 512), bf16),
+            pltpu.VMEM((1024, 512), bf16),
+            pltpu.SemaphoreType.DMA((16,)),
         ],
         name="states",
         compiler_params=PARAMS,
@@ -330,7 +347,7 @@
             entering = ss[rows, cols].astype(f32) + st[:, cols] * pair_row(
                 low1, before, 2 * p
             )
-            ssd = y_ref[:, cols] + grow[:, cols] * dot(c, entering.astype(bf16))
+            ssd = y_ref[rows, cols] + grow[:, cols] * dot(c, entering.astype(bf16))
             v = ssd * silu(zs[rows, cols].astype(f32))
             squares = squares + v * v
             g[rows, cols] = (v * gain_ref[:, cols]).astype(bf16)
@@ -365,7 +382,8 @@
         gate_kernel,
         grid=(12,),
         in_specs=[
-            rows(512), rows(256), rows(16), lanes, anywhere, anywhere, full(16, 32, 128),
+            pl.BlockSpec(memory_space=pltpu.VMEM), rows(256), rows(16), lanes, anywhere, anywhere,
+            full(16, 32, 128),
             full(1, 512), anywhere,
         ],
         out_specs=[pl.BlockSpec(memory_space=pl.ANY)] * 9,

time: 141 us -> 140 us (level)
  no operation moved by 1% of the time
where the time goes in v2:
time: 140 us; the launch traced here: 138 us
  waiting for transfers between devices  50.7 us (36%)
  starting transfers between devices  36.9 us (26%)
  Pallas kernels  25.7 us (18%)
  blocking collectives  19.8 us (14%)
  other arithmetic  3.25 us (2%)
    ppermute x20, waiting for transfers between devices, swap(): return lax.ppermute(values, 'head', [(h, h ^ mask) for h in range(16)])  48.5 us
    ppermute x20, starting transfers between devices, swap(): return lax.ppermute(values, 'head', [(h, h ^ mask) for h in range(16)])  31.7 us
    all_to_all x1, blocking collectives, layer(): pieces = prefix(lax.all_to_all(msg, 'seq', 0, 0))  19.8 us
    pallas_call x1, Pallas kernels, gate(): pl.pallas_call(gate_kernel, grid=(12,), in_specs=[pl.BlockSpec(memory_spa...  8.26 us
    pallas_call x1, Pallas kernels, inside(): pl.pallas_call(inside_kernel, grid=(1024 // Q,), in_specs=[pl.BlockSpec(m...  6.38 us
    pallas_call x1, Pallas kernels, block_states(): pl.pallas_call(state_kernel, grid=(1024 // Q,), in_specs=[rows(512), rows...  4.43 us
    all_to_all x1, starting transfers between devices, layer(): incoming = lax.all_to_all(pieces, 'seq', 0, 0)  3.51 us
    pallas_call x1, Pallas kernels, keep(): pl.pallas_call(keep_kernel, grid=(4,), in_specs=[pl.BlockSpec((1024, 640)...  3.48 us
  transfers between devices with their start and end apart: 22, of which 11 were waited for; matrix products, arithmetic and copies ran while one was open for 2% of the time, Pallas kernels for 8%

profile of v2, /device:TPU:2, one launch (start us, length us, event | category | flops | bytes accessed | tf_op | source)
XLA Modules:
  0.0 137.6 jit_solution(10375850928900060056)
XLA Ops:
  0.9 1.7 %collective-permute-start = (bf16[16,768]{1,0:T(8,128)(2,1)S(1)}, bf16[16,768]{1,0:T(8,128)(2,1)S(1)}, u32[]{:S(2)}, u32[]{:S(2)}) collective-permute-start(bf16[16,768]{1,0:T(8,128)(2,1)S(1)} %edge.1), channel_id=1, source_target_pairs={{0,16},{16,32},{32,48},{48,64},{64,80},{80,96},{96,112},{112,128},... | collective-permute-start | bytes 73736 | tf_op jit(solution)/shard_map/ppermute | solution.py:492
  3.4 1.6 %decays.1 = (f32[8,1024]{1,0:T(8,128)S(1)}, f32[8,1024]{1,0:T(8,128)S(1)}, bf16[1024,16]{1,0:T(8,128)(2,1)S(1)}, bf16[1024,16]{1,0:T(8,128)(2,1)S(1)}) custom-call(f32[8]{0:T(128)S(1)} %copy-done.8, f32[8,1024]{1,0:T(8,128)S(1)} %bitcast.58), custom_call_target="tpu_custom_call" | custom-call | tf_op jit(solution)/shard_map/decays/pallas_call | solution.py:91
  5.0 4.4 %states.1 = (bf16[1024,512]{1,0:T(8,128)(2,1)}, bf16[1024,256]{1,0:T(8,128)(2,1)S(1)}, f32[8,1024]{1,0:T(8,128)S(1)}, bf16[1024,512]{1,0:T(8,128)(2,1)}, bf16[16,40,128]{2,1,0:T(8,128)(2,1)S(1)}) custom-call(bf16[1024,512]{1,0:T(8,128)(2,1)S(1)} %copy-done.1, bf16[1024,128]{1,0:T(8,128)(2,1)S(1)} %copy-done.2, bf16[1024,128]{1,0:T(8,128)(2,1)S(1)} %copy-done.3, ...), custom_call_target="tpu_custom_call" | custom-call | tf_op jit(solution)/shard_map/states/pallas_call | solution.py:192
  9.5 19.8 %all_to_all.10.in_ref = bf16[16,40,128]{2,1,0:T(8,128)(2,1)S(1)} all-to-all(bf16[16,40,128]{2,1,0:T(8,128)(2,1)S(1)} %get-tuple-element.39), channel_id=1, replica_groups=mesh['seq'=16,'head'=16] {'seq'}, dimensions={0} | all-to-all | bytes 327680 | tf_op jit(solution)/shard_map/all_to_all | solution.py:499
  30.0 3.5 %all-to-all-start.1 = ((bf16[16,32,128]{2,1,0:T(8,128)(2,1)}), bf16[16,32,128]{2,1,0:T(8,128)(2,1)S(1)}, u32[]{:S(2)}, u32[]{:S(2)}) async-start(bf16[16,32,128]{2,1,0:T(8,128)(2,1)} %prefix.1), calls=%async_computation.1 | async-start | bytes 262144 | tf_op jit(solution)/shard_map/all_to_all | solution.py:500
  33.5 6.4 %inside.1.y_ref = f32[1024,512]{1,0:T(8,128)S(1)} custom-call(f32[8]{0:T(128)S(1)} %copy-done.9, bf16[1024,512]{1,0:T(8,128)(2,1)} %get-tuple-element.33.xc_ref, bf16[1024,256]{1,0:T(8,128)(2,1)S(1)} %get-tuple-element.34.bc_ref, f32[8,1024]{1,0:T(8,128)S(1)} %get-tuple-element.31.run_ref, f32[8,1024]{1,0:T(8,128)S(1)} %get-tuple-element.35.step_ref), custom_call_target="tpu_custom_call" | custom-call | tf_op jit(solution)/shard_map/inside/pallas_call | solution.py:249
  39.9 2.2 %all-to-all-done.1.sin_ref = bf16[16,32,128]{2,1,0:T(8,128)(2,1)S(1)} async-done(((bf16[16,32,128]{2,1,0:T(8,128)(2,1)}), bf16[16,32,128]{2,1,0:T(8,128)(2,1)S(1)}, u32[]{:S(2)}, u32[]{:S(2)}) %all-to-all-start.1) | async-done | bytes 131104 | tf_op jit(solution)/shard_map/all_to_all | solution.py:500
  42.1 8.3 %gate.1 = (bf16[256,1152]{1,0:T(8,128)(2,1)S(1)}, bf16[256,1024]{1,0:T(8,128)(2,1)S(1)}, bf16[256,1024]{1,0:T(8,128)(2,1)S(1)}, bf16[256,1024]{1,0:T(8,128)(2,1)...) custom-call(f32[1024,512]{1,0:T(8,128)S(1)} %inside.1.y_ref, ...), custom_call_target="tpu_custom_call" | custom-call | tf_op jit(solution)/shard_map/gate/pallas_call | solution.py:381
  50.4 3.1 %collective-permute-start.17 = (bf16[256,1024]{1,0:T(8,128)(2,1)S(1)}, bf16[256,1024]{1,0:T(8,128)(2,1)S(1)}, u32[]{:S(2)}, u32[]{:S(2)}) collective-permute-start(bf16[256,1024]{1,0:T(8,128)(2,1)S(1)} %get-tuple-element.56), channel_id=1, source_target_pairs={{0,3},{1,2},{2,1},{3,0},{4,7},{5,6},{6,5},{7,4},{8,11},{9,10},{10,... | collective-permute-start | bytes 1572872 | tf_op jit(solution)/shard_map/ppermute | solution.py:451
  53.6 1.5 %collective-permute-start.6 = (bf16[256,1024]{1,0:T(8,128)(2,1)S(1)}, bf16[256,1024]{1,0:T(8,128)(2,1)S(1)}, u32[]{:S(2)}, u32[]{:S(2)}) collective-permute-start(bf16[256,1024]{1,0:T(8,128)(2,1)S(1)} %get-tuple-element.46), channel_id=1, source_target_pairs={{0,12},{1,13},{2,14},{3,15},{4,8},{5,9},{6,10},{7,11},{8,4},{9,5},... | collective-permute-start | bytes 1572872 | tf_op jit(solution)/shard_map/ppermute | solution.py:451
  55.7 1.9 %collective-permute-start.11 = (bf16[256,1024]{1,0:T(8,128)(2,1)S(1)}, bf16[256,1024]{1,0:T(8,128)(2,1)S(1)}, u32[]{:S(2)}, u32[]{:S(2)}) collective-permute-start(bf16[256,1024]{1,0:T(8,128)(2,1)S(1)} %get-tuple-element.50), channel_id=1, source_target_pairs={{0,1},{1,0},{2,3},{3,2},{4,5},{5,4},{6,7},{7,6},{8,9},{9,8},{10,11... | collective-permute-start | bytes 1572872 | tf_op jit(solution)/shard_map/ppermute | solution.py:451
  57.6 3.5 %keep.1 = (bf16[256,1152]{1,0:T(8,128)(2,1)S(1)}, bf16[256,1024]{1,0:T(8,128)(2,1)S(1)}, bf16[256,1024]{1,0:T(8,128)(2,1)S(1)}, bf16[256,1024]{1,0:T(8,128)(2,1)...) custom-call(bf16[1024,640]{1,0:T(8,128)(2,1)S(1)} %get-tuple-element, ...), custom_call_target="tpu_custom_call" | custom-call | tf_op jit(solution)/shard_map/keep/pallas_call | solution.py:433
  61.0 5.1 %collective-permute-done.17 = bf16[256,1024]{1,0:T(8,128)(2,1)S(1)} collective-permute-done((bf16[256,1024]{1,0:T(8,128)(2,1)S(1)}, bf16[256,1024]{1,0:T(8,128)(2,1)S(1)}, u32[]{:S(2)}, u32[]{:S(2)}) %collective-permute-start.17) | collective-permute-done | bytes 524320 | tf_op jit(solution)/shard_map/ppermute | solution.py:451
  66.9 1.4 %collective-permute-done.12 = bf16[256,1024]{1,0:T(8,128)(2,1)S(1)} collective-permute-done((bf16[256,1024]{1,0:T(8,128)(2,1)S(1)}, bf16[256,1024]{1,0:T(8,128)(2,1)S(1)}, u32[]{:S(2)}, u32[]{:S(2)}) %collective-permute-start.12) | collective-permute-done | bytes 524320 | tf_op jit(solution)/shard_map/ppermute | solution.py:451
  68.3 1.6 %collective-permute-start.16 = (bf16[256,1024]{1,0:T(8,128)(2,1)S(1)}, bf16[256,1024]{1,0:T(8,128)(2,1)S(1)}, u32[]{:S(2)}, u32[]{:S(2)}) collective-permute-start(bf16[256,1024]{1,0:T(8,128)(2,1)S(1)} %get-tuple-element.54), channel_id=1, source_target_pairs={{0,3},{1,2},{2,1},{3,0},{4,7},{5,6},{6,5},{7,4},{8,11},{9,10},{10,... | collective-permute-start | bytes 1572872 | tf_op jit(solution)/shard_map/ppermute | solution.py:451
  70.1 8.7 %collective-permute-done.7 = bf16[256,1024]{1,0:T(8,128)(2,1)S(1)} collective-permute-done((bf16[256,1024]{1,0:T(8,128)(2,1)S(1)}, bf16[256,1024]{1,0:T(8,128)(2,1)S(1)}, u32[]{:S(2)}, u32[]{:S(2)}) %collective-permute-start.7) | collective-permute-done | bytes 524320 | tf_op jit(solution)/shard_map/ppermute | solution.py:451
  78.8 1.7 %collective-permute-start.1 = (bf16[256,1152]{1,0:T(8,128)(2,1)S(1)}, bf16[256,1152]{1,0:T(8,128)(2,1)S(1)}, u32[]{:S(2)}, u32[]{:S(2)}) collective-permute-start(bf16[256,1152]{1,0:T(8,128)(2,1)S(1)} %get-tuple-element.42), channel_id=1, source_target_pairs={{0,4},{1,5},{2,6},{3,7},{4,0},{5,1},{6,2},{7,3},{8,12},{9,13},{10,... | collective-permute-start | bytes 1769480 | tf_op jit(solution)/shard_map/ppermute | solution.py:451
  81.8 4.4 %collective-permute-start.13 = (bf16[256,1024]{1,0:T(8,128)(2,1)S(1)}, bf16[256,1024]{1,0:T(8,128)(2,1)S(1)}, u32[]{:S(2)}, u32[]{:S(2)}) collective-permute-start(bf16[256,1024]{1,0:T(8,128)(2,1)S(1)} %add_convert_fusion.2), channel_id=1, source_target_pairs={{0,3},{1,2},{2,1},{3,0},{4,7},{5,6},{6,5},{7,4},{8,11},{9,10},{10,... | collective-permute-start | bytes 1572872 | tf_op jit(solution)/shard_map/ppermute | solution.py:451
  86.3 18.8 %collective-permute-done.8 = bf16[256,1024]{1,0:T(8,128)(2,1)S(1)} collective-permute-done((bf16[256,1024]{1,0:T(8,128)(2,1)S(1)}, bf16[256,1024]{1,0:T(8,128)(2,1)S(1)}, u32[]{:S(2)}, u32[]{:S(2)}) %collective-permute-start.8) | collective-permute-done | bytes 524320 | tf_op jit(solution)/shard_map/ppermute | solution.py:451
  105.0 1.2 collective-permute-start.18
  106.6 2.2 %collective-permute-start.3 = (bf16[256,1152]{1,0:T(8,128)(2,1)S(1)}, bf16[256,1152]{1,0:T(8,128)(2,1)S(1)}, u32[]{:S(2)}, u32[]{:S(2)}) collective-permute-start(bf16[256,1152]{1,0:T(8,128)(2,1)S(1)} %add_convert_fusion), channel_id=1, source_target_pairs={{0,12},{1,13},{2,14},{3,15},{4,8},{5,9},{6,10},{7,11},{8,4},{9,5},... | collective-permute-start | bytes 1769480 | tf_op jit(solution)/shard_map/ppermute | solution.py:451
  108.8 1.0 collective-permute-start.9
  110.2 1.9 %collective-permute-start.14 = (bf16[2,64,1024]{2,1,0:T(8,128)(2,1)S(1)}, bf16[2,64,1024]{2,1,0:T(8,128)(2,1)S(1)}, u32[]{:S(2)}, u32[]{:S(2)}) collective-permute-start(bf16[2,64,1024]{2,1,0:T(8,128)(2,1)S(1)} %pad_maximum_fusion.3), channel_id=1, source_target_pairs={{0,4},{1,5},{2,6},{3,7},{4,0},{5,1},{6,2},{7,3},{8,12},{9,13},{10,... | collective-permute-start | bytes 786440 | tf_op jit(solution)/shard_map/ppermute | solution.py:451
  112.2 5.5 %collective-permute-done.18 = bf16[256,1024]{1,0:T(8,128)(2,1)S(1)} collective-permute-done((bf16[256,1024]{1,0:T(8,128)(2,1)S(1)}, bf16[256,1024]{1,0:T(8,128)(2,1)S(1)}, u32[]{:S(2)}, u32[]{:S(2)}) %collective-permute-start.18) | collective-permute-done | bytes 524320 | tf_op jit(solution)/shard_map/ppermute | solution.py:451
  118.1 1.7 %collective-permute-start.19 = (bf16[2,64,1024]{2,1,0:T(8,128)(2,1)S(1)}, bf16[2,64,1024]{2,1,0:T(8,128)(2,1)S(1)}, u32[]{:S(2)}, u32[]{:S(2)}) collective-permute-start(bf16[2,64,1024]{2,1,0:T(8,128)(2,1)S(1)} %pad_maximum_fusion.4), channel_id=1, source_target_pairs={{0,12},{1,13},{2,14},{3,15},{4,8},{5,9},{6,10},{7,11},{8,4},{9,5},... | collective-permute-start | bytes 786440 | tf_op jit(solution)/shard_map/ppermute | solution.py:451
  119.7 2.7 %collective-permute-done.3 = bf16[256,1152]{1,0:T(8,128)(2,1)S(1)} collective-permute-done((bf16[256,1152]{1,0:T(8,128)(2,1)S(1)}, bf16[256,1152]{1,0:T(8,128)(2,1)S(1)}, u32[]{:S(2)}, u32[]{:S(2)}) %collective-permute-start.3) | collective-permute-done | bytes 589856 | tf_op jit(solution)/shard_map/ppermute | solution.py:451
  123.3 1.7 %collective-permute-start.10 = (bf16[64,1024]{1,0:T(8,128)(2,1)S(1)}, bf16[64,1024]{1,0:T(8,128)(2,1)S(1)}, u32[]{:S(2)}, u32[]{:S(2)}) collective-permute-start(bf16[64,1024]{1,0:T(8,128)(2,1)S(1)} %fusion.10), channel_id=1, source_target_pairs={{0,1},{1,0},{2,3},{3,2},{4,5},{5,4},{6,7},{7,6},{8,9},{9,8},{10,11... | collective-permute-start | bytes 393224 | tf_op jit(solution)/shard_map/ppermute | solution.py:451
  125.0 2.1 %collective-permute-start.15 = (bf16[64,1024]{1,0:T(8,128)(2,1)S(1)}, bf16[64,1024]{1,0:T(8,128)(2,1)S(1)}, u32[]{:S(2)}, u32[]{:S(2)}) collective-permute-start(bf16[64,1024]{1,0:T(8,128)(2,1)S(1)} %fusion.6), channel_id=1, source_target_pairs={{0,12},{1,13},{2,14},{3,15},{4,8},{5,9},{6,10},{7,11},{8,4},{9,5},... | collective-permute-start | bytes 393224 | tf_op jit(solution)/shard_map/ppermute | solution.py:451
  127.1 2.4 %collective-permute-done.4 = bf16[2,64,1152]{2,1,0:T(8,128)(2,1)S(1)} collective-permute-done((bf16[2,64,1152]{2,1,0:T(8,128)(2,1)S(1)}, bf16[2,64,1152]{2,1,0:T(8,128)(2,1)S(1)}, u32[]{:S(2)}, u32[]{:S(2)}) %collective-permute-start.4) | collective-permute-done | bytes 294944 | tf_op jit(solution)/shard_map/ppermute | solution.py:451
  129.6 1.8 %collective-permute-start.5 = (bf16[64,1152]{1,0:T(8,128)(2,1)S(1)}, bf16[64,1152]{1,0:T(8,128)(2,1)S(1)}, u32[]{:S(2)}, u32[]{:S(2)}) collective-permute-start(bf16[64,1152]{1,0:T(8,128)(2,1)S(1)} %fusion), channel_id=1, source_target_pairs={{0,3},{1,2},{2,1},{3,0},{4,7},{5,6},{6,5},{7,4},{8,11},{9,10},{10,... | collective-permute-start | bytes 442376 | tf_op jit(solution)/shard_map/ppermute | solution.py:451
  131.4 1.9 %collective-permute-start.20 = (bf16[64,1024]{1,0:T(8,128)(2,1)S(1)}, bf16[64,1024]{1,0:T(8,128)(2,1)S(1)}, u32[]{:S(2)}, u32[]{:S(2)}) collective-permute-start(bf16[64,1024]{1,0:T(8,128)(2,1)S(1)} %fusion.2), channel_id=1, source_target_pairs={{0,4},{1,5},{2,6},{3,7},{4,0},{5,1},{6,2},{7,3},{8,12},{9,13},{10,... | collective-permute-start | bytes 393224 | tf_op jit(solution)/shard_map/ppermute | solution.py:451
  133.3 2.7 %collective-permute-done.5 = bf16[64,1152]{1,0:T(8,128)(2,1)S(1)} collective-permute-done((bf16[64,1152]{1,0:T(8,128)(2,1)S(1)}, bf16[64,1152]{1,0:T(8,128)(2,1)S(1)}, u32[]{:S(2)}, u32[]{:S(2)}) %collective-permute-start.5) | collective-permute-done | bytes 147488 | tf_op jit(solution)/shard_map/ppermute | solution.py:451
  (64 shorter events, 8.6 us)
Async XLA Ops:
  0.0 5.0 %copy-start.3 = (bf16[1024,128]{1,0:T(8,128)(2,1)S(1)}, bf16[1024,128]{1,0:T(8,128)(2,1)}, u32[]{:S(2)}) copy-start(bf16[1024,128]{1,0:T(8,128)(2,1)} %c_ref.3) | copy-start | bytes 786436
  0.0 5.0 %copy-start.2 = (bf16[1024,128]{1,0:T(8,128)(2,1)S(1)}, bf16[1024,128]{1,0:T(8,128)(2,1)}, u32[]{:S(2)}) copy-start(bf16[1024,128]{1,0:T(8,128)(2,1)} %b_ref.3) | copy-start | bytes 786436
  0.0 5.0 %copy-start.1 = (bf16[1024,512]{1,0:T(8,128)(2,1)S(1)}, bf16[1024,512]{1,0:T(8,128)(2,1)}, u32[]{:S(2)}) copy-start(bf16[1024,512]{1,0:T(8,128)(2,1)} %x_ref.3) | copy-start | bytes 3145732
  0.0 2.6 %copy-start.8 = (f32[8]{0:T(128)S(1)}, f32[8]{0:T(128)}, u32[]{:S(2)}) copy-start(f32[8]{0:T(128)} %a_ref.1) | copy-start | bytes 100
  0.0 5.0 %copy-start.6 = (f32[4,256]{1,0:T(4,128)S(1)}, f32[4,256]{1,0:T(4,128)}, u32[]{:S(2)}) copy-start(f32[4,256]{1,0:T(4,128)} %wbc_ref.1) | copy-start | bytes 12292
  0.0 5.0 %copy-start.5 = (f32[4,512]{1,0:T(4,128)S(1)}, f32[4,512]{1,0:T(4,128)}, u32[]{:S(2)}) copy-start(f32[4,512]{1,0:T(4,128)} %wx_ref.1) | copy-start | bytes 24580
  0.9 4.1 %collective-permute-start = (bf16[16,768]{1,0:T(8,128)(2,1)S(1)}, bf16[16,768]{1,0:T(8,128)(2,1)S(1)}, u32[]{:S(2)}, u32[]{:S(2)}) collective-permute-start(bf16[16,768]{1,0:T(8,128)(2,1)S(1)} %edge.1), channel_id=1, source_target_pairs={{0,16},{16,32},{32,48},{48,64},{64,80},{80,96},{96,112},{112,128},... | collective-permute-start | bytes 73736 | tf_op jit(solution)/shard_map/ppermute | solution.py:492
  2.6 0.8 copy-start.4
  5.0 28.5 %copy-start.9 = (f32[8]{0:T(128)S(1)}, f32[8]{0:T(128)}, u32[]{:S(2)}) copy-start(f32[8]{0:T(128)} %skip_ref.1) | copy-start | bytes 100
  30.0 12.1 %all-to-all-start.1 = ((bf16[16,32,128]{2,1,0:T(8,128)(2,1)}), bf16[16,32,128]{2,1,0:T(8,128)(2,1)S(1)}, u32[]{:S(2)}, u32[]{:S(2)}) async-start(bf16[16,32,128]{2,1,0:T(8,128)(2,1)} %prefix.1), calls=%async_computation.1 | async-start | bytes 262144 | tf_op jit(solution)/shard_map/all_to_all | solution.py:500
  33.5 8.6 %copy-start.7 = (f32[512]{0:T(512)S(1)}, f32[512]{0:T(512)}, u32[]{:S(2)}) copy-start(f32[512]{0:T(512)} %param.20) | copy-start | bytes 6148
  42.1 15.4 %copy-start = (bf16[512,4096]{1,0:T(8,128)(2,1)S(1)}, bf16[512,4096]{1,0:T(8,128)(2,1)}, u32[]{:S(2)}) copy-start(bf16[512,4096]{1,0:T(8,128)(2,1)} %w_ref.3) | copy-start | bytes 12582916
  50.4 15.8 %collective-permute-start.17 = (bf16[256,1024]{1,0:T(8,128)(2,1)S(1)}, bf16[256,1024]{1,0:T(8,128)(2,1)S(1)}, u32[]{:S(2)}, u32[]{:S(2)}) collective-permute-start(bf16[256,1024]{1,0:T(8,128)(2,1)S(1)} %get-tuple-element.56), channel_id=1, source_target_pairs={{0,3},{1,2},{2,1},{3,0},{4,7},{5,6},{6,5},{7,4},{8,11},{9,10},{10,... | collective-permute-start | bytes 1572872 | tf_op jit(solution)/shard_map/ppermute | solution.py:451
  53.5 14.8 %collective-permute-start.12 = (bf16[256,1024]{1,0:T(8,128)(2,1)S(1)}, bf16[256,1024]{1,0:T(8,128)(2,1)S(1)}, u32[]{:S(2)}, u32[]{:S(2)}) collective-permute-start(bf16[256,1024]{1,0:T(8,128)(2,1)S(1)} %get-tuple-element.52), channel_id=1, source_target_pairs={{0,1},{1,0},{2,3},{3,2},{4,5},{5,4},{6,7},{7,6},{8,9},{9,8},{10,11... | collective-permute-start | bytes 1572872 | tf_op jit(solution)/shard_map/ppermute | solution.py:451
  53.6 28.2 %collective-permute-start.6 = (bf16[256,1024]{1,0:T(8,128)(2,1)S(1)}, bf16[256,1024]{1,0:T(8,128)(2,1)S(1)}, u32[]{:S(2)}, u32[]{:S(2)}) collective-permute-start(bf16[256,1024]{1,0:T(8,128)(2,1)S(1)} %get-tuple-element.46), channel_id=1, source_target_pairs={{0,12},{1,13},{2,14},{3,15},{4,8},{5,9},{6,10},{7,11},{8,4},{9,5},... | collective-permute-start | bytes 1572872 | tf_op jit(solution)/shard_map/ppermute | solution.py:451
  55.1 23.7 %collective-permute-start.7 = (bf16[256,1024]{1,0:T(8,128)(2,1)S(1)}, bf16[256,1024]{1,0:T(8,128)(2,1)S(1)}, u32[]{:S(2)}, u32[]{:S(2)}) collective-permute-start(bf16[256,1024]{1,0:T(8,128)(2,1)S(1)} %get-tuple-element.48), channel_id=1, source_target_pairs={{0,12},{1,13},{2,14},{3,15},{4,8},{5,9},{6,10},{7,11},{8,4},{9,5},... | collective-permute-start | bytes 1572872 | tf_op jit(solution)/shard_map/ppermute | solution.py:451
  55.7 50.9 %collective-permute-start.11 = (bf16[256,1024]{1,0:T(8,128)(2,1)S(1)}, bf16[256,1024]{1,0:T(8,128)(2,1)S(1)}, u32[]{:S(2)}, u32[]{:S(2)}) collective-permute-start(bf16[256,1024]{1,0:T(8,128)(2,1)S(1)} %get-tuple-element.50), channel_id=1, source_target_pairs={{0,1},{1,0},{2,3},{3,2},{4,5},{5,4},{6,7},{7,6},{8,9},{9,8},{10,11... | collective-permute-start | bytes 1572872 | tf_op jit(solution)/shard_map/ppermute | solution.py:451
  66.1 15.4 %collective-permute-start.2 = (bf16[256,1152]{1,0:T(8,128)(2,1)S(1)}, bf16[256,1152]{1,0:T(8,128)(2,1)S(1)}, u32[]{:S(2)}, u32[]{:S(2)}) collective-permute-start(bf16[256,1152]{1,0:T(8,128)(2,1)S(1)} %get-tuple-element.44), channel_id=1, source_target_pairs={{0,4},{1,5},{2,6},{3,7},{4,0},{5,1},{6,2},{7,3},{8,12},{9,13},{10,... | collective-permute-start | bytes 1769480 | tf_op jit(solution)/shard_map/ppermute | solution.py:451
  68.3 41.9 %collective-permute-start.16 = (bf16[256,1024]{1,0:T(8,128)(2,1)S(1)}, bf16[256,1024]{1,0:T(8,128)(2,1)S(1)}, u32[]{:S(2)}, u32[]{:S(2)}) collective-permute-start(bf16[256,1024]{1,0:T(8,128)(2,1)S(1)} %get-tuple-element.54), channel_id=1, source_target_pairs={{0,3},{1,2},{2,1},{3,0},{4,7},{5,6},{6,5},{7,4},{8,11},{9,10},{10,... | collective-permute-start | bytes 1572872 | tf_op jit(solution)/shard_map/ppermute | solution.py:451
  78.8 40.9 %collective-permute-start.1 = (bf16[256,1152]{1,0:T(8,128)(2,1)S(1)}, bf16[256,1152]{1,0:T(8,128)(2,1)S(1)}, u32[]{:S(2)}, u32[]{:S(2)}) collective-permute-start(bf16[256,1152]{1,0:T(8,128)(2,1)S(1)} %get-tuple-element.42), channel_id=1, source_target_pairs={{0,4},{1,5},{2,6},{3,7},{4,0},{5,1},{6,2},{7,3},{8,12},{9,13},{10,... | collective-permute-start | bytes 1769480 | tf_op jit(solution)/shard_map/ppermute | solution.py:451
  81.6 23.5 %collective-permute-start.8 = (bf16[256,1024]{1,0:T(8,128)(2,1)S(1)}, bf16[256,1024]{1,0:T(8,128)(2,1)S(1)}, u32[]{:S(2)}, u32[]{:S(2)}) collective-permute-start(bf16[256,1024]{1,0:T(8,128)(2,1)S(1)} %add_convert_fusion.3), channel_id=1, source_target_pairs={{0,4},{1,5},{2,6},{3,7},{4,0},{5,1},{6,2},{7,3},{8,12},{9,13},{10,... | collective-permute-start | bytes 1572872 | tf_op jit(solution)/shard_map/ppermute | solution.py:451
  81.8 27.0 %collective-permute-start.13 = (bf16[256,1024]{1,0:T(8,128)(2,1)S(1)}, bf16[256,1024]{1,0:T(8,128)(2,1)S(1)}, u32[]{:S(2)}, u32[]{:S(2)}) collective-permute-start(bf16[256,1024]{1,0:T(8,128)(2,1)S(1)} %add_convert_fusion.2), channel_id=1, source_target_pairs={{0,3},{1,2},{2,1},{3,0},{4,7},{5,6},{6,5},{7,4},{8,11},{9,10},{10,... | collective-permute-start | bytes 1572872 | tf_op jit(solution)/shard_map/ppermute | solution.py:451
  105.0 12.7 %collective-permute-start.18 = (bf16[256,1024]{1,0:T(8,128)(2,1)S(1)}, bf16[256,1024]{1,0:T(8,128)(2,1)S(1)}, u32[]{:S(2)}, u32[]{:S(2)}) collective-permute-start(bf16[256,1024]{1,0:T(8,128)(2,1)S(1)} %add_convert_fusion.1), channel_id=1, source_target_pairs={{0,1},{1,0},{2,3},{3,2},{4,5},{5,4},{6,7},{7,6},{8,9},{9,8},{10,11... | collective-permute-start | bytes 1572872 | tf_op jit(solution)/shard_map/ppermute | solution.py:451
  106.6 15.9 %collective-permute-start.3 = (bf16[256,1152]{1,0:T(8,128)(2,1)S(1)}, bf16[256,1152]{1,0:T(8,128)(2,1)S(1)}, u32[]{:S(2)}, u32[]{:S(2)}) collective-permute-start(bf16[256,1152]{1,0:T(8,128)(2,1)S(1)} %add_convert_fusion), channel_id=1, source_target_pairs={{0,12},{1,13},{2,14},{3,15},{4,8},{5,9},{6,10},{7,11},{8,4},{9,5},... | collective-permute-start | bytes 1769480 | tf_op jit(solution)/shard_map/ppermute | solution.py:451
  108.8 14.4 %collective-permute-start.9 = (bf16[2,64,1024]{2,1,0:T(8,128)(2,1)S(1)}, bf16[2,64,1024]{2,1,0:T(8,128)(2,1)S(1)}, u32[]{:S(2)}, u32[]{:S(2)}) collective-permute-start(bf16[2,64,1024]{2,1,0:T(8,128)(2,1)S(1)} %pad_maximum_fusion.2), channel_id=1, source_target_pairs={{0,3},{1,2},{2,1},{3,0},{4,7},{5,6},{6,5},{7,4},{8,11},{9,10},{10,... | collective-permute-start | bytes 786440 | tf_op jit(solution)/shard_map/ppermute | solution.py:451
  110.2 14.8 %collective-permute-start.14 = (bf16[2,64,1024]{2,1,0:T(8,128)(2,1)S(1)}, bf16[2,64,1024]{2,1,0:T(8,128)(2,1)S(1)}, u32[]{:S(2)}, u32[]{:S(2)}) collective-permute-start(bf16[2,64,1024]{2,1,0:T(8,128)(2,1)S(1)} %pad_maximum_fusion.3), channel_id=1, source_target_pairs={{0,4},{1,5},{2,6},{3,7},{4,0},{5,1},{6,2},{7,3},{8,12},{9,13},{10,... | collective-permute-start | bytes 786440 | tf_op jit(solution)/shard_map/ppermute | solution.py:451
  118.1 13.4 %collective-permute-start.19 = (bf16[2,64,1024]{2,1,0:T(8,128)(2,1)S(1)}, bf16[2,64,1024]{2,1,0:T(8,128)(2,1)S(1)}, u32[]{:S(2)}, u32[]{:S(2)}) collective-permute-start(bf16[2,64,1024]{2,1,0:T(8,128)(2,1)S(1)} %pad_maximum_fusion.4), channel_id=1, source_target_pairs={{0,12},{1,13},{2,14},{3,15},{4,8},{5,9},{6,10},{7,11},{8,4},{9,5},... | collective-permute-start | bytes 786440 | tf_op jit(solution)/shard_map/ppermute | solution.py:451
  122.7 6.8 %collective-permute-start.4 = (bf16[2,64,1152]{2,1,0:T(8,128)(2,1)S(1)}, bf16[2,64,1152]{2,1,0:T(8,128)(2,1)S(1)}, u32[]{:S(2)}, u32[]{:S(2)}) collective-permute-start(bf16[2,64,1152]{2,1,0:T(8,128)(2,1)S(1)} %pad_maximum_fusion.1), channel_id=1, source_target_pairs={{0,1},{1,0},{2,3},{3,2},{4,5},{5,4},{6,7},{7,6},{8,9},{9,8},{10,11... | collective-permute-start | bytes 884744 | tf_op jit(solution)/shard_map/ppermute | solution.py:451
  123.3 12.9 %collective-permute-start.10 = (bf16[64,1024]{1,0:T(8,128)(2,1)S(1)}, bf16[64,1024]{1,0:T(8,128)(2,1)S(1)}, u32[]{:S(2)}, u32[]{:S(2)}) collective-permute-start(bf16[64,1024]{1,0:T(8,128)(2,1)S(1)} %fusion.10), channel_id=1, source_target_pairs={{0,1},{1,0},{2,3},{3,2},{4,5},{5,4},{6,7},{7,6},{8,9},{9,8},{10,11... | collective-permute-start | bytes 393224 | tf_op jit(solution)/shard_map/ppermute | solution.py:451
  125.0 11.2 %collective-permute-start.15 = (bf16[64,1024]{1,0:T(8,128)(2,1)S(1)}, bf16[64,1024]{1,0:T(8,128)(2,1)S(1)}, u32[]{:S(2)}, u32[]{:S(2)}) collective-permute-start(bf16[64,1024]{1,0:T(8,128)(2,1)S(1)} %fusion.6), channel_id=1, source_target_pairs={{0,12},{1,13},{2,14},{3,15},{4,8},{5,9},{6,10},{7,11},{8,4},{9,5},... | collective-permute-start | bytes 393224 | tf_op jit(solution)/shard_map/ppermute | solution.py:451
  129.6 6.4 %collective-permute-start.5 = (bf16[64,1152]{1,0:T(8,128)(2,1)S(1)}, bf16[64,1152]{1,0:T(8,128)(2,1)S(1)}, u32[]{:S(2)}, u32[]{:S(2)}) collective-permute-start(bf16[64,1152]{1,0:T(8,128)(2,1)S(1)} %fusion), channel_id=1, source_target_pairs={{0,3},{1,2},{2,1},{3,0},{4,7},{5,6},{6,5},{7,4},{8,11},{9,10},{10,... | collective-permute-start | bytes 442376 | tf_op jit(solution)/shard_map/ppermute | solution.py:451
  131.4 5.1 %collective-permute-start.20 = (bf16[64,1024]{1,0:T(8,128)(2,1)S(1)}, bf16[64,1024]{1,0:T(8,128)(2,1)S(1)}, u32[]{:S(2)}, u32[]{:S(2)}) collective-permute-start(bf16[64,1024]{1,0:T(8,128)(2,1)S(1)} %fusion.2), channel_id=1, source_target_pairs={{0,4},{1,5},{2,6},{3,7},{4,0},{5,1},{6,2},{7,3},{8,12},{9,13},{10,... | collective-permute-start | bytes 393224 | tf_op jit(solution)/shard_map/ppermute | solution.py:451

commit v3 on v2

--- a/solution.py
+++ b/solution.py
@@ -1,3 +1,5 @@
+import functools
+
 import jax
 import jax.numpy as jnp
 from jax import lax
@@ -280,50 +282,66 @@
 WIDTHS = (1152, 1024, 1024, 1024)
 
 
-def projected(g_ref, w_ref, q, out, here, axis, picks):
+FIRST = (8, 9, 10, 11, 2, 6, 14)
+REST = (0, 1, 3, 4, 5, 7, 12, 13, 15)
+
+
+def projected(g_ref, w_ref, q, out, axis, picks, place=None):
     parts = []
     for pick in picks:
         for k in range(4):
             mask = pick * 4 + k if axis == 0 else k * 4 + pick
-            owner = jnp.bitwise_xor(here, mask)
-            parts.append(g_ref[pl.ds(pl.multiple_of(owner * 64, 64), 64), :])
+            at = 64 * (mask if place is None else place.index(mask))
+            parts.append(g_ref[at : at + 64, :])
     rows = jnp.concatenate(parts, axis=0)
     out[:, :1024] = dot(rows[:, :512], w_ref[:, q * 1024 : q * 1024 + 1024]).astype(bf16)
     if out.shape[1] > 1024:
         out[:, 1024:] = rows[:, 512:]
 
 
-def gate_kernel(
-    y_ref, bc_ref, grow_ref, before_ref, states_hbm, z_hbm, sin_ref, gain_ref, w_ref,
-    *rest,
-):
-    outs, (st, g, w, zs, ss, b0, b1, b2, b3, sems) = rest[:9], rest[9:]
+def gate_kernel(masks, name, y_ref, bc_ref, grow_ref, before_ref, states_hbm, z_hbm, sin_ref, gain_ref, w_ref, *rest):
+    count = len(masks)
+    far = name == "gate_far"
+    if far:
+        outs, (st, g, w, zs, ss, b0, b1, b2, b3, sems) = rest[:5], rest[5:]
+    else:
+        g_before, outs = rest[0], rest[1:6]
+        st, g, w, zs, ss, b0, b1, b2, b3, sems = rest[6:]
     i = pl.program_id(0)
     here = lax.axis_index("head")
     bufs = (b0, b1, b2, b3)
 
+    def mask_of(k):
+        mask = jnp.int32(masks[0])
+        for n in range(1, count):
+            mask = jnp.where(k == n, masks[n], mask)
+        return mask
+
     def out_copy(n):
-        if n == 8:
-            return pltpu.make_async_copy(g, outs[8], sems.at[8])
-        q, part = n % 4, n // 4
-        return pltpu.make_async_copy(
-            bufs[q].at[part * 256 : part * 256 + 256], outs[n], sems.at[n]
-        )
+        return pltpu.make_async_copy(g if n == 4 else bufs[n], outs[n], sems.at[n])
 
     def w_copy(q):
         cols = slice(1024 * q, 1024 * q + 1024)
-        return pltpu.make_async_copy(w_ref.at[:, cols], w.at[:, cols], sems.at[9 + q])
+        return pltpu.make_async_copy(w_ref.at[:, cols], w.at[:, cols], sems.at[5 + q])
 
     def in_copies(k):
-        part = pl.ds(pl.multiple_of(k * Q, Q), Q)
+        owner = jnp.bitwise_xor(here, mask_of(k))
+        rows = pl.ds(pl.multiple_of(owner * 64, 64), 64)
+        chunk = pl.ds(pl.multiple_of(owner // 2 * Q, Q), Q)
         return (
-            pltpu.make_async_copy(z_hbm.at[part, :], zs.at[part, :], sems.at[13 + k]),
-            pltpu.make_async_copy(states_hbm.at[part, :], ss.at[part, :], sems.at[21 + k]),
+            pltpu.make_async_copy(
+                z_hbm.at[rows, :], zs.at[pl.ds(pl.multiple_of(k * 64, 64), 64), :], sems.at[9 + k]
+            ),
+            pltpu.make_async_copy(
+                states_hbm.at[chunk, :],
+                ss.at[pl.ds(pl.multiple_of(k * Q, Q), Q), :],
+                sems.at[18 + k],
+            ),
         )
 
     @pl.when(i == 0)
     def _():
-        for k in range(8):
+        for k in range(count):
             for copy in in_copies(k):
                 copy.start()
         for q in range(4):
@@ -331,83 +349,89 @@
         for j in range(16):
             group, p = j // 4, j % 4
             st[32 * group : 32 * group + 32, 128 * p : 128 * p + 128] = sin_ref[j].astype(f32)
-
-    @pl.when(i < 8)
+        if not far:
+            for n, mask in enumerate(FIRST):
+                g[64 * mask : 64 * mask + 64, :] = g_before[64 * n : 64 * n + 64, :]
+
+    @pl.when(i < count)
     def _():
         for copy in in_copies(i):
             copy.wait()
-        before = jnp.exp(before_ref[...])
+        mask = mask_of(i)
+        owner = jnp.bitwise_xor(here, mask)
+        rows = pl.ds(pl.multiple_of(owner * 64, 64), 64)
+        lanes = pl.ds(pl.multiple_of(owner // 2 * Q, Q), Q)
+        mine = pl.ds(pl.multiple_of(i * 64, 64), 64)
+        target = mine if far else pl.ds(pl.multiple_of(mask * 64, 64), 64)
+        chunk = pl.ds(pl.multiple_of(i * Q, Q), Q)
+        before = jnp.exp(before_ref[:, lanes])
         low1 = lax.broadcasted_iota(jnp.int32, (1, 128), 1) < 64
-        grow = dot(grow_ref[...], spread())
-        c = bc_ref[:, 128:]
-        squares = jnp.zeros((Q, 128), f32)
-        rows = pl.ds(pl.multiple_of(i * Q, Q), Q)
+        grow = dot(grow_ref[rows, :], spread())
+        c = bc_ref[rows, 128:]
+        squares = jnp.zeros((64, 128), f32)
         for p in range(4):
             cols = slice(128 * p, 128 * p + 128)
-            entering = ss[rows, cols].astype(f32) + st[:, cols] * pair_row(
-                low1, before, 2 * p
-            )
+            entering = ss[chunk, cols].astype(f32) + st[:, cols] * pair_row(low1, before, 2 * p)
             ssd = y_ref[rows, cols] + grow[:, cols] * dot(c, entering.astype(bf16))
-            v = ssd * silu(zs[rows, cols].astype(f32))
+            v = ssd * silu(zs[mine, cols].astype(f32))
             squares = squares + v * v
-            g[rows, cols] = (v * gain_ref[:, cols]).astype(bf16)
-        g[rows, 512:] = dot(squares.astype(bf16), jnp.ones((128, 128), bf16)).astype(bf16)
+            g[target, cols] = (v * gain_ref[:, cols]).astype(bf16)
+        g[target, 512:] = dot(squares.astype(bf16), jnp.ones((128, 128), bf16)).astype(bf16)
 
     for q, (ax, m, _) in enumerate(SETS):
 
-        @pl.when(i == 8 + q)
+        @pl.when(i == count + q)
         def _(q=q, ax=ax, m=m):
             w_copy(q).wait()
-            projected(g, w, q, bufs[q], here, ax, (2, m))
+            if far:
+                projected(g, w, q, bufs[q], ax, (2,), FIRST)
+            else:
+                projected(g, w, q, bufs[q], ax, (m,))
             out_copy(q).start()
-            out_copy(4 + q).start()
-
-    @pl.when(i == 8)
-    def _():
-        out_copy(8).start()
-
-    @pl.when(i == 11)
-    def _():
-        for n in range(9):
+
+    @pl.when(i == count)
+    def _():
+        out_copy(4).start()
+
+    @pl.when(i == count + 3)
+    def _():
+        for n in range(5):
             out_copy(n).wait()
 
 
-def gate(y, bc, grow, before, states, z_gate, incoming, gain, w_out):
-    row = lambda i: jnp.minimum(i, 7)
-    rows = lambda n: pl.BlockSpec((Q, n), lambda i: (row(i), 0))
-    full = lambda *s: pl.BlockSpec(s, lambda i: (0,) * len(s))
-    lanes = pl.BlockSpec((8, Q), lambda i: (0, row(i)))
+def gate(name, masks, y, bc, grow, before, states, z_gate, incoming, gain, w_out, *g_before):
     anywhere = pl.BlockSpec(memory_space=pl.ANY)
-    return pl.pallas_call(
-        gate_kernel,
-        grid=(12,),
-        in_specs=[
-            pl.BlockSpec(memory_space=pltpu.VMEM), rows(256), rows(16), lanes, anywhere, anywhere,
-            full(16, 32, 128),
-            full(1, 512), anywhere,
-        ],
-        out_specs=[pl.BlockSpec(memory_space=pl.ANY)] * 9,
-        out_shape=[jax.ShapeDtypeStruct((256, n), bf16) for n in WIDTHS * 2]
-        + [jax.ShapeDtypeStruct((1024, 640), bf16)],
+    near = pl.BlockSpec(memory_space=pltpu.VMEM)
+    count = len(masks)
+    g_rows = 1024 if g_before else count * 64
+    return pl.pallas_call(
+        functools.partial(gate_kernel, masks, name),
+        grid=(count + 4,),
+        in_specs=[near, near, near, near, anywhere, anywhere, near, near, anywhere]
+        + [near] * len(g_before),
+        out_specs=[anywhere] * 5,
+        out_shape=[jax.ShapeDtypeStruct((256, n), bf16) for n in WIDTHS]
+        + [jax.ShapeDtypeStruct((g_rows, 640), bf16)],
         scratch_shapes=[
             pltpu.VMEM((128, 512), f32),
-            pltpu.VMEM((1024, 640), bf16),
+            pltpu.VMEM((g_rows, 640), bf16),
             pltpu.VMEM((512, 4096), bf16),
-            pltpu.VMEM((1024, 512), bf16),
-            pltpu.VMEM((1024, 512), bf16),
+            pltpu.VMEM((count * 64, 512), bf16),
+            pltpu.VMEM((count * Q, 512), bf16),
         ]
-        + [pltpu.VMEM((512, n), bf16) for n in WIDTHS]
-        + [pltpu.SemaphoreType.DMA((29,))],
-        name="gate",
+        + [pltpu.VMEM((256, n), bf16) for n in WIDTHS]
+        + [pltpu.SemaphoreType.DMA((27,))],
         compiler_params=PARAMS,
-    )(y, bc, grow, before, in_hbm(states), in_hbm(z_gate), incoming, gain, in_hbm(w_out))
+    )(
+        y, bc, grow, before, in_hbm(states), in_hbm(z_gate), incoming, gain, in_hbm(w_out),
+        *g_before,
+    )
 
 
 def keep_kernel(g_ref, w_ref, *rest):
     outs, (b0, b1, b2, b3, sems) = rest[:8], rest[8:]
     bufs = (b0, b1, b2, b3)
     i = pl.program_id(0)
-    here = lax.axis_index("head")
 
     def out_copy(n):
         q, part = n % 4, n // 4
@@ -419,7 +443,7 @@
 
         @pl.when(i == q)
         def _(q=q, ax=ax, m=m):
-            projected(g_ref, w_ref, q, bufs[q], here, ax, (m ^ 2, 0))
+            projected(g_ref, w_ref, q, bufs[q], ax, (m ^ 2, 0))
             out_copy(q).start()
             out_copy(4 + q).start()
 
@@ -434,7 +458,7 @@
         keep_kernel,
         grid=(4,),
         in_specs=[
-            pl.BlockSpec((1024, 640), lambda i: (0, 0)),
+            pl.BlockSpec(memory_space=pltpu.VMEM),
             pl.BlockSpec(memory_space=pltpu.VMEM),
         ],
         out_specs=[pl.BlockSpec(memory_space=pl.ANY)] * 8,
@@ -458,13 +482,15 @@
     return total
 
 
-def summed_to_owners(g, sends, w_out):
+def summed_to_owners(gated, w_out):
+    *sends, g_first = gate("gate_far", FIRST, *gated)
     far = []
     for q, (ax, m, _) in enumerate(SETS):
         far.append(swap(sends[q], ax, m))
+    *sends, g = gate("gate_near", REST, *gated, g_first)
     near = []
     for q, (ax, m, _) in enumerate(SETS):
-        near.append(swap(sends[4 + q], ax, m))
+        near.append(swap(sends[q], ax, m))
     kept = keep(g, w_out)
     passed, own = kept[:4], kept[4:]
     second = [
@@ -499,10 +525,8 @@
     pieces = prefix(lax.all_to_all(msg, "seq", 0, 0))
     incoming = lax.all_to_all(pieces, "seq", 0, 0)
     y = inside(xc, bc, run, step, d_skip)
-    *sends, g = gate(
-        y, bc, grow, before, states, z_gate, incoming, norm_gain[None, :], w_out
-    )
-    return summed_to_owners(g, sends, w_out)
+    gated = (y, bc, grow, before, states, z_gate, incoming, norm_gain[None, :], w_out)
+    return summed_to_owners(gated, w_out)
 
 
 def solution(mesh):

time: 140 us -> 144 us (1.029)
  Pallas kernels: 25.7 us -> 29.5 us
  waiting for transfers between devices: 50.7 us -> 53 us
  starting transfers between devices: 36.9 us -> 34.7 us
    pallas_call x2 -> x3, Pallas kernels: 11.7 us -> 15.6 us  [the longest x2 12.1 us: gate(): pl.pallas_call(functools.partial(gate_kernel, masks, name), grid=(count +...]
    ppermute x20, waiting for transfers between devices: 48.5 us -> 50.8 us  [swap(): return lax.ppermute(values, 'head', [(h, h ^ mask) for h in range(16)])]
    ppermute x20, starting transfers between devices: 31.7 us -> 29.5 us  [swap(): return lax.ppermute(values, 'head', [(h, h ^ mask) for h in range(16)])]
  transfers between devices with their start and end apart: 22 -> 22, of which waited for: 11 -> 7; matrix products, arithmetic and copies ran while one was open for 2% -> 2% of each run, Pallas kernels for 8% -> 13%
where the time goes in v3:
time: 144 us; the launch traced here: 142 us
  waiting for transfers between devices  53 us (37%)
  starting transfers between devices  34.7 us (24%)
  Pallas kernels  29.5 us (20%)
  blocking collectives  19.8 us (14%)
  other arithmetic  3.27 us (2%)
    ppermute x20, waiting for transfers between devices, swap(): return lax.ppermute(values, 'head', [(h, h ^ mask) for h in range(16)])  50.8 us
    ppermute x20, starting transfers between devices, swap(): return lax.ppermute(values, 'head', [(h, h ^ mask) for h in range(16)])  29.5 us
    all_to_all x1, blocking collectives, layer(): pieces = prefix(lax.all_to_all(msg, 'seq', 0, 0))  19.8 us
    pallas_call x2, Pallas kernels, gate(): pl.pallas_call(functools.partial(gate_kernel, masks, name), grid=(count +...  12.1 us
    pallas_call x1, Pallas kernels, inside(): pl.pallas_call(inside_kernel, grid=(1024 // Q,), in_specs=[pl.BlockSpec(m...  6.38 us
    pallas_call x1, Pallas kernels, block_states(): pl.pallas_call(state_kernel, grid=(1024 // Q,), in_specs=[rows(512), rows...  4.45 us
    all_to_all x1, starting transfers between devices, layer(): incoming = lax.all_to_all(pieces, 'seq', 0, 0)  3.51 us
    pallas_call x1, Pallas kernels, keep(): pl.pallas_call(keep_kernel, grid=(4,), in_specs=[pl.BlockSpec(memory_spac...  3.48 us
  transfers between devices with their start and end apart: 22, of which 7 were waited for; matrix products, arithmetic and copies ran while one was open for 2% of the time, Pallas kernels for 13%

profile of v3, /device:TPU:2, one launch (start us, length us, event | category | flops | bytes accessed | tf_op | source)
XLA Modules:
  0.0 141.6 jit_solution(1962003350699592474)
XLA Ops:
  0.0 0.9 edge.1
  0.9 1.7 %collective-permute-start = (bf16[16,768]{1,0:T(8,128)(2,1)S(1)}, bf16[16,768]{1,0:T(8,128)(2,1)S(1)}, u32[]{:S(2)}, u32[]{:S(2)}) collective-permute-start(bf16[16,768]{1,0:T(8,128)(2,1)S(1)} %edge.1), channel_id=1, source_target_pairs={{0,16},{16,32},{32,48},{48,64},{64,80},{80,96},{96,112},{112,128},... | collective-permute-start | bytes 73736 | tf_op jit(solution)/shard_map/ppermute | solution.py:518
  3.4 1.6 %decays.1 = (f32[8,1024]{1,0:T(8,128)S(1)}, f32[8,1024]{1,0:T(8,128)S(1)}, bf16[1024,16]{1,0:T(8,128)(2,1)S(1)}, bf16[1024,16]{1,0:T(8,128)(2,1)S(1)}) custom-call(f32[8]{0:T(128)S(1)} %copy-done.8, f32[8,1024]{1,0:T(8,128)S(1)} %bitcast.58), custom_call_target="tpu_custom_call" | custom-call | tf_op jit(solution)/shard_map/decays/pallas_call | solution.py:93
  5.0 4.4 %states.1 = (bf16[1024,512]{1,0:T(8,128)(2,1)}, bf16[1024,256]{1,0:T(8,128)(2,1)S(1)}, f32[8,1024]{1,0:T(8,128)S(1)}, bf16[1024,512]{1,0:T(8,128)(2,1)}, bf16[16,40,128]{2,1,0:T(8,128)(2,1)S(1)}) custom-call(bf16[1024,512]{1,0:T(8,128)(2,1)S(1)} %copy-done.1, bf16[1024,128]{1,0:T(8,128)(2,1)S(1)} %copy-done.2, bf16[1024,128]{1,0:T(8,128)(2,1)S(1)} %copy-done.3, ...), custom_call_target="tpu_custom_call" | custom-call | tf_op jit(solution)/shard_map/states/pallas_call | solution.py:194
  9.5 19.8 %all_to_all.10.in_ref = bf16[16,40,128]{2,1,0:T(8,128)(2,1)S(1)} all-to-all(bf16[16,40,128]{2,1,0:T(8,128)(2,1)S(1)} %get-tuple-element.40), channel_id=1, replica_groups=mesh['seq'=16,'head'=16] {'seq'}, dimensions={0} | all-to-all | bytes 327680 | tf_op jit(solution)/shard_map/all_to_all | solution.py:525
  30.0 3.5 %all-to-all-start.1 = ((bf16[16,32,128]{2,1,0:T(8,128)(2,1)}), bf16[16,32,128]{2,1,0:T(8,128)(2,1)S(1)}, u32[]{:S(2)}, u32[]{:S(2)}) async-start(bf16[16,32,128]{2,1,0:T(8,128)(2,1)} %prefix.1), calls=%async_computation.1 | async-start | bytes 262144 | tf_op jit(solution)/shard_map/all_to_all | solution.py:526
  33.5 6.4 %inside.1.y_ref = f32[1024,512]{1,0:T(8,128)S(1)} custom-call(f32[8]{0:T(128)S(1)} %copy-done.9, bf16[1024,512]{1,0:T(8,128)(2,1)} %get-tuple-element.34.xc_ref, bf16[1024,256]{1,0:T(8,128)(2,1)S(1)} %get-tuple-element.35.bc_ref, f32[8,1024]{1,0:T(8,128)S(1)} %get-tuple-element.32.run_ref, f32[8,1024]{1,0:T(8,128)S(1)} %get-tuple-element.36.step_ref), custom_call_target="tpu_custom_call" | custom-call | tf_op jit(solution)/shard_map/inside/pallas_call | solution.py:251
  39.9 2.2 %all-to-all-done.1.sin_ref = bf16[16,32,128]{2,1,0:T(8,128)(2,1)S(1)} async-done(((bf16[16,32,128]{2,1,0:T(8,128)(2,1)}), bf16[16,32,128]{2,1,0:T(8,128)(2,1)S(1)}, u32[]{:S(2)}, u32[]{:S(2)}) %all-to-all-start.1) | async-done | bytes 131104 | tf_op jit(solution)/shard_map/all_to_all | solution.py:526
  42.1 5.7 %shard_map.109 = (bf16[256,1152]{1,0:T(8,128)(2,1)S(1)}, bf16[256,1024]{1,0:T(8,128)(2,1)S(1)}, bf16[256,1024]{1,0:T(8,128)(2,1)S(1)}, bf16[256,1024]{1,0:T(8,128)(2,1)S(1)}, bf16[448,640]{1,0:T(8,128)(2,1)S(1)}) custom-call(f32[1024,512]{1,0:T(8,128)S(1)} %inside.1.y_ref, bf16[1024,256]{1,0:T(8,128)(2,1)S(1)} %get-tuple-element.35.bc_ref, ...), custom_call_target="tpu_custom_call" | custom-call | tf_op jit(solution)/shard_map/pallas_call | solution.py:407
  47.8 3.1 %collective-permute-start.17 = (bf16[256,1024]{1,0:T(8,128)(2,1)S(1)}, bf16[256,1024]{1,0:T(8,128)(2,1)S(1)}, u32[]{:S(2)}, u32[]{:S(2)}) collective-permute-start(bf16[256,1024]{1,0:T(8,128)(2,1)S(1)} %get-tuple-element.58), channel_id=1, source_target_pairs={{0,3},{1,2},{2,1},{3,0},{4,7},{5,6},{6,5},{7,4},{8,11},{9,10},{10,... | collective-permute-start | bytes 1572872 | tf_op jit(solution)/shard_map/ppermute | solution.py:475
  51.1 6.4 %shard_map.110 = (bf16[256,1152]{1,0:T(8,128)(2,1)S(1)}, bf16[256,1024]{1,0:T(8,128)(2,1)S(1)}, bf16[256,1024]{1,0:T(8,128)(2,1)S(1)}, bf16[256,1024]{1,0:T(8,128)(2,1)S(1)}, bf16[1024,640]{1,0:T(8,128)(2,1)S(1)}) custom-call(f32[1024,512]{1,0:T(8,128)S(1)} %inside.1.y_ref, bf16[1024,256]{1,0:T(8,128)(2,1)S(1)} %get-tuple-element.35.bc_ref, ...), custom_call_target="tpu_custom_call" | custom-call | tf_op jit(solution)/shard_map/pallas_call | solution.py:407
  57.5 1.6 %collective-permute-start.6 = (bf16[256,1024]{1,0:T(8,128)(2,1)S(1)}, bf16[256,1024]{1,0:T(8,128)(2,1)S(1)}, u32[]{:S(2)}, u32[]{:S(2)}) collective-permute-start(bf16[256,1024]{1,0:T(8,128)(2,1)S(1)} %get-tuple-element.48), channel_id=1, source_target_pairs={{0,12},{1,13},{2,14},{3,15},{4,8},{5,9},{6,10},{7,11},{8,4},{9,5},... | collective-permute-start | bytes 1572872 | tf_op jit(solution)/shard_map/ppermute | solution.py:475
  59.1 1.9 %collective-permute-start.11 = (bf16[256,1024]{1,0:T(8,128)(2,1)S(1)}, bf16[256,1024]{1,0:T(8,128)(2,1)S(1)}, u32[]{:S(2)}, u32[]{:S(2)}) collective-permute-start(bf16[256,1024]{1,0:T(8,128)(2,1)S(1)} %get-tuple-element.52), channel_id=1, source_target_pairs={{0,1},{1,0},{2,3},{3,2},{4,5},{5,4},{6,7},{7,6},{8,9},{9,8},{10,11... | collective-permute-start | bytes 1572872 | tf_op jit(solution)/shard_map/ppermute | solution.py:475
  61.5 3.5 %keep.1 = (bf16[256,1152]{1,0:T(8,128)(2,1)S(1)}, bf16[256,1024]{1,0:T(8,128)(2,1)S(1)}, bf16[256,1024]{1,0:T(8,128)(2,1)S(1)}, bf16[256,1024]{1,0:T(8,128)(2,1)...) custom-call(bf16[1024,640]{1,0:T(8,128)(2,1)S(1)} %get-tuple-element, ...), custom_call_target="tpu_custom_call" | custom-call | tf_op jit(solution)/shard_map/keep/pallas_call | solution.py:457
  65.0 1.8 %collective-permute-start.2 = (bf16[256,1152]{1,0:T(8,128)(2,1)S(1)}, bf16[256,1152]{1,0:T(8,128)(2,1)S(1)}, u32[]{:S(2)}, u32[]{:S(2)}) collective-permute-start(bf16[256,1152]{1,0:T(8,128)(2,1)S(1)} %get-tuple-element.46), channel_id=1, source_target_pairs={{0,4},{1,5},{2,6},{3,7},{4,0},{5,1},{6,2},{7,3},{8,12},{9,13},{10,... | collective-permute-start | bytes 1769480 | tf_op jit(solution)/shard_map/ppermute | solution.py:475
  67.6 15.2 %collective-permute-done.7 = bf16[256,1024]{1,0:T(8,128)(2,1)S(1)} collective-permute-done((bf16[256,1024]{1,0:T(8,128)(2,1)S(1)}, bf16[256,1024]{1,0:T(8,128)(2,1)S(1)}, u32[]{:S(2)}, u32[]{:S(2)}) %collective-permute-start.7) | collective-permute-done | bytes 524320 | tf_op jit(solution)/shard_map/ppermute | solution.py:475
  82.8 1.7 %collective-permute-start.1 = (bf16[256,1152]{1,0:T(8,128)(2,1)S(1)}, bf16[256,1152]{1,0:T(8,128)(2,1)S(1)}, u32[]{:S(2)}, u32[]{:S(2)}) collective-permute-start(bf16[256,1152]{1,0:T(8,128)(2,1)S(1)} %get-tuple-element.44), channel_id=1, source_target_pairs={{0,4},{1,5},{2,6},{3,7},{4,0},{5,1},{6,2},{7,3},{8,12},{9,13},{10,... | collective-permute-start | bytes 1769480 | tf_op jit(solution)/shard_map/ppermute | solution.py:475
  85.3 1.0 collective-permute-start.13
  86.3 22.3 %collective-permute-done.8 = bf16[256,1024]{1,0:T(8,128)(2,1)S(1)} collective-permute-done((bf16[256,1024]{1,0:T(8,128)(2,1)S(1)}, bf16[256,1024]{1,0:T(8,128)(2,1)S(1)}, u32[]{:S(2)}, u32[]{:S(2)}) %collective-permute-start.8) | collective-permute-done | bytes 524320 | tf_op jit(solution)/shard_map/ppermute | solution.py:475
  108.6 1.6 %collective-permute-start.18 = (bf16[256,1024]{1,0:T(8,128)(2,1)S(1)}, bf16[256,1024]{1,0:T(8,128)(2,1)S(1)}, u32[]{:S(2)}, u32[]{:S(2)}) collective-permute-start(bf16[256,1024]{1,0:T(8,128)(2,1)S(1)} %add_convert_fusion.1), channel_id=1, source_target_pairs={{0,1},{1,0},{2,3},{3,2},{4,5},{5,4},{6,7},{7,6},{8,9},{9,8},{10,11... | collective-permute-start | bytes 1572872 | tf_op jit(solution)/shard_map/ppermute | solution.py:475
  110.5 2.2 %collective-permute-start.3 = (bf16[256,1152]{1,0:T(8,128)(2,1)S(1)}, bf16[256,1152]{1,0:T(8,128)(2,1)S(1)}, u32[]{:S(2)}, u32[]{:S(2)}) collective-permute-start(bf16[256,1152]{1,0:T(8,128)(2,1)S(1)} %add_convert_fusion), channel_id=1, source_target_pairs={{0,12},{1,13},{2,14},{3,15},{4,8},{5,9},{6,10},{7,11},{8,4},{9,5},... | collective-permute-start | bytes 1769480 | tf_op jit(solution)/shard_map/ppermute | solution.py:475
  113.7 2.4 %collective-permute-start.14 = (bf16[2,64,1024]{2,1,0:T(8,128)(2,1)S(1)}, bf16[2,64,1024]{2,1,0:T(8,128)(2,1)S(1)}, u32[]{:S(2)}, u32[]{:S(2)}) collective-permute-start(bf16[2,64,1024]{2,1,0:T(8,128)(2,1)S(1)} %pad_maximum_fusion.3), channel_id=1, source_target_pairs={{0,4},{1,5},{2,6},{3,7},{4,0},{5,1},{6,2},{7,3},{8,12},{9,13},{10,... | collective-permute-start | bytes 786440 | tf_op jit(solution)/shard_map/ppermute | solution.py:475
  116.1 4.7 %collective-permute-done.18 = bf16[256,1024]{1,0:T(8,128)(2,1)S(1)} collective-permute-done((bf16[256,1024]{1,0:T(8,128)(2,1)S(1)}, bf16[256,1024]{1,0:T(8,128)(2,1)S(1)}, u32[]{:S(2)}, u32[]{:S(2)}) %collective-permute-start.18) | collective-permute-done | bytes 524320 | tf_op jit(solution)/shard_map/ppermute | solution.py:475
  121.2 2.5 %collective-permute-start.19 = (bf16[2,64,1024]{2,1,0:T(8,128)(2,1)S(1)}, bf16[2,64,1024]{2,1,0:T(8,128)(2,1)S(1)}, u32[]{:S(2)}, u32[]{:S(2)}) collective-permute-start(bf16[2,64,1024]{2,1,0:T(8,128)(2,1)S(1)} %pad_maximum_fusion.4), channel_id=1, source_target_pairs={{0,12},{1,13},{2,14},{3,15},{4,8},{5,9},{6,10},{7,11},{8,4},{9,5},... | collective-permute-start | bytes 786440 | tf_op jit(solution)/shard_map/ppermute | solution.py:475
  123.7 3.0 %collective-permute-done.3 = bf16[256,1152]{1,0:T(8,128)(2,1)S(1)} collective-permute-done((bf16[256,1152]{1,0:T(8,128)(2,1)S(1)}, bf16[256,1152]{1,0:T(8,128)(2,1)S(1)}, u32[]{:S(2)}, u32[]{:S(2)}) %collective-permute-start.3) | collective-permute-done | bytes 589856 | tf_op jit(solution)/shard_map/ppermute | solution.py:475
  127.1 2.1 %collective-permute-start.10 = (bf16[64,1024]{1,0:T(8,128)(2,1)S(1)}, bf16[64,1024]{1,0:T(8,128)(2,1)S(1)}, u32[]{:S(2)}, u32[]{:S(2)}) collective-permute-start(bf16[64,1024]{1,0:T(8,128)(2,1)S(1)} %fusion.10), channel_id=1, source_target_pairs={{0,1},{1,0},{2,3},{3,2},{4,5},{5,4},{6,7},{7,6},{8,9},{9,8},{10,11... | collective-permute-start | bytes 393224 | tf_op jit(solution)/shard_map/ppermute | solution.py:475
  129.3 1.8 %collective-permute-start.15 = (bf16[64,1024]{1,0:T(8,128)(2,1)S(1)}, bf16[64,1024]{1,0:T(8,128)(2,1)S(1)}, u32[]{:S(2)}, u32[]{:S(2)}) collective-permute-start(bf16[64,1024]{1,0:T(8,128)(2,1)S(1)} %fusion.6), channel_id=1, source_target_pairs={{0,12},{1,13},{2,14},{3,15},{4,8},{5,9},{6,10},{7,11},{8,4},{9,5},... | collective-permute-start | bytes 393224 | tf_op jit(solution)/shard_map/ppermute | solution.py:475
  131.1 2.7 %collective-permute-done.4 = bf16[2,64,1152]{2,1,0:T(8,128)(2,1)S(1)} collective-permute-done((bf16[2,64,1152]{2,1,0:T(8,128)(2,1)S(1)}, bf16[2,64,1152]{2,1,0:T(8,128)(2,1)S(1)}, u32[]{:S(2)}, u32[]{:S(2)}) %collective-permute-start.4) | collective-permute-done | bytes 294944 | tf_op jit(solution)/shard_map/ppermute | solution.py:475
  133.8 0.9 collective-permute-start.5
  134.7 2.7 %collective-permute-start.20 = (bf16[64,1024]{1,0:T(8,128)(2,1)S(1)}, bf16[64,1024]{1,0:T(8,128)(2,1)S(1)}, u32[]{:S(2)}, u32[]{:S(2)}) collective-permute-start(bf16[64,1024]{1,0:T(8,128)(2,1)S(1)} %fusion.2), channel_id=1, source_target_pairs={{0,4},{1,5},{2,6},{3,7},{4,0},{5,1},{6,2},{7,3},{8,12},{9,13},{10,... | collective-permute-start | bytes 393224 | tf_op jit(solution)/shard_map/ppermute | solution.py:475
  137.5 2.8 %collective-permute-done.5 = bf16[64,1152]{1,0:T(8,128)(2,1)S(1)} collective-permute-done((bf16[64,1152]{1,0:T(8,128)(2,1)S(1)}, bf16[64,1152]{1,0:T(8,128)(2,1)S(1)}, u32[]{:S(2)}, u32[]{:S(2)}) %collective-permute-start.5) | collective-permute-done | bytes 147488 | tf_op jit(solution)/shard_map/ppermute | solution.py:475
  140.7 0.8 pad_maximum_fusion
  (65 shorter events, 6.0 us)
Async XLA Ops:
  0.0 5.0 %copy-start.3 = (bf16[1024,128]{1,0:T(8,128)(2,1)S(1)}, bf16[1024,128]{1,0:T(8,128)(2,1)}, u32[]{:S(2)}) copy-start(bf16[1024,128]{1,0:T(8,128)(2,1)} %c_ref.3) | copy-start | bytes 786436
  0.0 5.0 %copy-start.2 = (bf16[1024,128]{1,0:T(8,128)(2,1)S(1)}, bf16[1024,128]{1,0:T(8,128)(2,1)}, u32[]{:S(2)}) copy-start(bf16[1024,128]{1,0:T(8,128)(2,1)} %b_ref.3) | copy-start | bytes 786436
  0.0 5.0 %copy-start.1 = (bf16[1024,512]{1,0:T(8,128)(2,1)S(1)}, bf16[1024,512]{1,0:T(8,128)(2,1)}, u32[]{:S(2)}) copy-start(bf16[1024,512]{1,0:T(8,128)(2,1)} %x_ref.3) | copy-start | bytes 3145732
  0.0 2.6 %copy-start.8 = (f32[8]{0:T(128)S(1)}, f32[8]{0:T(128)}, u32[]{:S(2)}) copy-start(f32[8]{0:T(128)} %a_ref.1) | copy-start | bytes 100
  0.0 5.0 %copy-start.7 = (f32[4,256]{1,0:T(4,128)S(1)}, f32[4,256]{1,0:T(4,128)}, u32[]{:S(2)}) copy-start(f32[4,256]{1,0:T(4,128)} %wbc_ref.1) | copy-start | bytes 12292
  0.0 5.0 %copy-start.5 = (f32[4,512]{1,0:T(4,128)S(1)}, f32[4,512]{1,0:T(4,128)}, u32[]{:S(2)}) copy-start(f32[4,512]{1,0:T(4,128)} %wx_ref.1) | copy-start | bytes 24580
  0.9 4.1 %collective-permute-start = (bf16[16,768]{1,0:T(8,128)(2,1)S(1)}, bf16[16,768]{1,0:T(8,128)(2,1)S(1)}, u32[]{:S(2)}, u32[]{:S(2)}) collective-permute-start(bf16[16,768]{1,0:T(8,128)(2,1)S(1)} %edge.1), channel_id=1, source_target_pairs={{0,16},{16,32},{32,48},{48,64},{64,80},{80,96},{96,112},{112,128},... | collective-permute-start | bytes 73736 | tf_op jit(solution)/shard_map/ppermute | solution.py:518
  2.6 0.8 copy-start.4
  5.0 28.5 %copy-start.9 = (f32[8]{0:T(128)S(1)}, f32[8]{0:T(128)}, u32[]{:S(2)}) copy-start(f32[8]{0:T(128)} %skip_ref.1) | copy-start | bytes 100
  30.0 12.1 %all-to-all-start.1 = ((bf16[16,32,128]{2,1,0:T(8,128)(2,1)}), bf16[16,32,128]{2,1,0:T(8,128)(2,1)S(1)}, u32[]{:S(2)}, u32[]{:S(2)}) async-start(bf16[16,32,128]{2,1,0:T(8,128)(2,1)} %prefix.1), calls=%async_computation.1 | async-start | bytes 262144 | tf_op jit(solution)/shard_map/all_to_all | solution.py:526
  33.5 8.6 %copy-start.6 = (f32[512]{0:T(512)S(1)}, f32[512]{0:T(512)}, u32[]{:S(2)}) copy-start(f32[512]{0:T(512)} %param.20) | copy-start | bytes 6148
  47.8 17.2 %collective-permute-start.17 = (bf16[256,1024]{1,0:T(8,128)(2,1)S(1)}, bf16[256,1024]{1,0:T(8,128)(2,1)S(1)}, u32[]{:S(2)}, u32[]{:S(2)}) collective-permute-start(bf16[256,1024]{1,0:T(8,128)(2,1)S(1)} %get-tuple-element.58), channel_id=1, source_target_pairs={{0,3},{1,2},{2,1},{3,0},{4,7},{5,6},{6,5},{7,4},{8,11},{9,10},{10,... | collective-permute-start | bytes 1572872 | tf_op jit(solution)/shard_map/ppermute | solution.py:475
  50.9 16.1 %collective-permute-start.12 = (bf16[256,1024]{1,0:T(8,128)(2,1)S(1)}, bf16[256,1024]{1,0:T(8,128)(2,1)S(1)}, u32[]{:S(2)}, u32[]{:S(2)}) collective-permute-start(bf16[256,1024]{1,0:T(8,128)(2,1)S(1)} %get-tuple-element.54), channel_id=1, source_target_pairs={{0,1},{1,0},{2,3},{3,2},{4,5},{5,4},{6,7},{7,6},{8,9},{9,8},{10,11... | collective-permute-start | bytes 1572872 | tf_op jit(solution)/shard_map/ppermute | solution.py:475
  51.1 10.4 %copy-start = (bf16[512,4096]{1,0:T(8,128)(2,1)S(1)}, bf16[512,4096]{1,0:T(8,128)(2,1)}, u32[]{:S(2)}) copy-start(bf16[512,4096]{1,0:T(8,128)(2,1)} %w_ref.5) | copy-start | bytes 12582916
  57.5 27.8 %collective-permute-start.6 = (bf16[256,1024]{1,0:T(8,128)(2,1)S(1)}, bf16[256,1024]{1,0:T(8,128)(2,1)S(1)}, u32[]{:S(2)}, u32[]{:S(2)}) collective-permute-start(bf16[256,1024]{1,0:T(8,128)(2,1)S(1)} %get-tuple-element.48), channel_id=1, source_target_pairs={{0,12},{1,13},{2,14},{3,15},{4,8},{5,9},{6,10},{7,11},{8,4},{9,5},... | collective-permute-start | bytes 1572872 | tf_op jit(solution)/shard_map/ppermute | solution.py:475
  59.1 51.4 %collective-permute-start.11 = (bf16[256,1024]{1,0:T(8,128)(2,1)S(1)}, bf16[256,1024]{1,0:T(8,128)(2,1)S(1)}, u32[]{:S(2)}, u32[]{:S(2)}) collective-permute-start(bf16[256,1024]{1,0:T(8,128)(2,1)S(1)} %get-tuple-element.52), channel_id=1, source_target_pairs={{0,1},{1,0},{2,3},{3,2},{4,5},{5,4},{6,7},{7,6},{8,9},{9,8},{10,11... | collective-permute-start | bytes 1572872 | tf_op jit(solution)/shard_map/ppermute | solution.py:475
  61.0 21.8 %collective-permute-start.7 = (bf16[256,1024]{1,0:T(8,128)(2,1)S(1)}, bf16[256,1024]{1,0:T(8,128)(2,1)S(1)}, u32[]{:S(2)}, u32[]{:S(2)}) collective-permute-start(bf16[256,1024]{1,0:T(8,128)(2,1)S(1)} %get-tuple-element.50), channel_id=1, source_target_pairs={{0,12},{1,13},{2,14},{3,15},{4,8},{5,9},{6,10},{7,11},{8,4},{9,5},... | collective-permute-start | bytes 1572872 | tf_op jit(solution)/shard_map/ppermute | solution.py:475
  65.0 19.7 %collective-permute-start.2 = (bf16[256,1152]{1,0:T(8,128)(2,1)S(1)}, bf16[256,1152]{1,0:T(8,128)(2,1)S(1)}, u32[]{:S(2)}, u32[]{:S(2)}) collective-permute-start(bf16[256,1152]{1,0:T(8,128)(2,1)S(1)} %get-tuple-element.46), channel_id=1, source_target_pairs={{0,4},{1,5},{2,6},{3,7},{4,0},{5,1},{6,2},{7,3},{8,12},{9,13},{10,... | collective-permute-start | bytes 1769480 | tf_op jit(solution)/shard_map/ppermute | solution.py:475
  67.0 46.6 %collective-permute-start.16 = (bf16[256,1024]{1,0:T(8,128)(2,1)S(1)}, bf16[256,1024]{1,0:T(8,128)(2,1)S(1)}, u32[]{:S(2)}, u32[]{:S(2)}) collective-permute-start(bf16[256,1024]{1,0:T(8,128)(2,1)S(1)} %get-tuple-element.56), channel_id=1, source_target_pairs={{0,3},{1,2},{2,1},{3,0},{4,7},{5,6},{6,5},{7,4},{8,11},{9,10},{10,... | collective-permute-start | bytes 1572872 | tf_op jit(solution)/shard_map/ppermute | solution.py:475
  82.8 40.9 %collective-permute-start.1 = (bf16[256,1152]{1,0:T(8,128)(2,1)S(1)}, bf16[256,1152]{1,0:T(8,128)(2,1)S(1)}, u32[]{:S(2)}, u32[]{:S(2)}) collective-permute-start(bf16[256,1152]{1,0:T(8,128)(2,1)S(1)} %get-tuple-element.44), channel_id=1, source_target_pairs={{0,4},{1,5},{2,6},{3,7},{4,0},{5,1},{6,2},{7,3},{8,12},{9,13},{10,... | collective-permute-start | bytes 1769480 | tf_op jit(solution)/shard_map/ppermute | solution.py:475
  84.7 23.8 %collective-permute-start.8 = (bf16[256,1024]{1,0:T(8,128)(2,1)S(1)}, bf16[256,1024]{1,0:T(8,128)(2,1)S(1)}, u32[]{:S(2)}, u32[]{:S(2)}) collective-permute-start(bf16[256,1024]{1,0:T(8,128)(2,1)S(1)} %add_convert_fusion.3), channel_id=1, source_target_pairs={{0,4},{1,5},{2,6},{3,7},{4,0},{5,1},{6,2},{7,3},{8,12},{9,13},{10,... | collective-permute-start | bytes 1572872 | tf_op jit(solution)/shard_map/ppermute | solution.py:475
  85.3 27.5 %collective-permute-start.13 = (bf16[256,1024]{1,0:T(8,128)(2,1)S(1)}, bf16[256,1024]{1,0:T(8,128)(2,1)S(1)}, u32[]{:S(2)}, u32[]{:S(2)}) collective-permute-start(bf16[256,1024]{1,0:T(8,128)(2,1)S(1)} %add_convert_fusion.2), channel_id=1, source_target_pairs={{0,3},{1,2},{2,1},{3,0},{4,7},{5,6},{6,5},{7,4},{8,11},{9,10},{10,... | collective-permute-start | bytes 1572872 | tf_op jit(solution)/shard_map/ppermute | solution.py:475
  108.6 12.3 %collective-permute-start.18 = (bf16[256,1024]{1,0:T(8,128)(2,1)S(1)}, bf16[256,1024]{1,0:T(8,128)(2,1)S(1)}, u32[]{:S(2)}, u32[]{:S(2)}) collective-permute-start(bf16[256,1024]{1,0:T(8,128)(2,1)S(1)} %add_convert_fusion.1), channel_id=1, source_target_pairs={{0,1},{1,0},{2,3},{3,2},{4,5},{5,4},{6,7},{7,6},{8,9},{9,8},{10,11... | collective-permute-start | bytes 1572872 | tf_op jit(solution)/shard_map/ppermute | solution.py:475
  110.5 16.2 %collective-permute-start.3 = (bf16[256,1152]{1,0:T(8,128)(2,1)S(1)}, bf16[256,1152]{1,0:T(8,128)(2,1)S(1)}, u32[]{:S(2)}, u32[]{:S(2)}) collective-permute-start(bf16[256,1152]{1,0:T(8,128)(2,1)S(1)} %add_convert_fusion), channel_id=1, source_target_pairs={{0,12},{1,13},{2,14},{3,15},{4,8},{5,9},{6,10},{7,11},{8,4},{9,5},... | collective-permute-start | bytes 1769480 | tf_op jit(solution)/shard_map/ppermute | solution.py:475
  112.8 14.3 %collective-permute-start.9 = (bf16[2,64,1024]{2,1,0:T(8,128)(2,1)S(1)}, bf16[2,64,1024]{2,1,0:T(8,128)(2,1)S(1)}, u32[]{:S(2)}, u32[]{:S(2)}) collective-permute-start(bf16[2,64,1024]{2,1,0:T(8,128)(2,1)S(1)} %pad_maximum_fusion.2), channel_id=1, source_target_pairs={{0,3},{1,2},{2,1},{3,0},{4,7},{5,6},{6,5},{7,4},{8,11},{9,10},{10,... | collective-permute-start | bytes 786440 | tf_op jit(solution)/shard_map/ppermute | solution.py:475
  113.7 15.6 %collective-permute-start.14 = (bf16[2,64,1024]{2,1,0:T(8,128)(2,1)S(1)}, bf16[2,64,1024]{2,1,0:T(8,128)(2,1)S(1)}, u32[]{:S(2)}, u32[]{:S(2)}) collective-permute-start(bf16[2,64,1024]{2,1,0:T(8,128)(2,1)S(1)} %pad_maximum_fusion.3), channel_id=1, source_target_pairs={{0,4},{1,5},{2,6},{3,7},{4,0},{5,1},{6,2},{7,3},{8,12},{9,13},{10,... | collective-permute-start | bytes 786440 | tf_op jit(solution)/shard_map/ppermute | solution.py:475
  121.2 13.5 %collective-permute-start.19 = (bf16[2,64,1024]{2,1,0:T(8,128)(2,1)S(1)}, bf16[2,64,1024]{2,1,0:T(8,128)(2,1)S(1)}, u32[]{:S(2)}, u32[]{:S(2)}) collective-permute-start(bf16[2,64,1024]{2,1,0:T(8,128)(2,1)S(1)} %pad_maximum_fusion.4), channel_id=1, source_target_pairs={{0,12},{1,13},{2,14},{3,15},{4,8},{5,9},{6,10},{7,11},{8,4},{9,5},... | collective-permute-start | bytes 786440 | tf_op jit(solution)/shard_map/ppermute | solution.py:475
  127.0 6.8 %collective-permute-start.4 = (bf16[2,64,1152]{2,1,0:T(8,128)(2,1)S(1)}, bf16[2,64,1152]{2,1,0:T(8,128)(2,1)S(1)}, u32[]{:S(2)}, u32[]{:S(2)}) collective-permute-start(bf16[2,64,1152]{2,1,0:T(8,128)(2,1)S(1)} %pad_maximum_fusion.1), channel_id=1, source_target_pairs={{0,1},{1,0},{2,3},{3,2},{4,5},{5,4},{6,7},{7,6},{8,9},{9,8},{10,11... | collective-permute-start | bytes 884744 | tf_op jit(solution)/shard_map/ppermute | solution.py:475
  127.1 13.3 %collective-permute-start.10 = (bf16[64,1024]{1,0:T(8,128)(2,1)S(1)}, bf16[64,1024]{1,0:T(8,128)(2,1)S(1)}, u32[]{:S(2)}, u32[]{:S(2)}) collective-permute-start(bf16[64,1024]{1,0:T(8,128)(2,1)S(1)} %fusion.10), channel_id=1, source_target_pairs={{0,1},{1,0},{2,3},{3,2},{4,5},{5,4},{6,7},{7,6},{8,9},{9,8},{10,11... | collective-permute-start | bytes 393224 | tf_op jit(solution)/shard_map/ppermute | solution.py:475
  129.3 11.2 %collective-permute-start.15 = (bf16[64,1024]{1,0:T(8,128)(2,1)S(1)}, bf16[64,1024]{1,0:T(8,128)(2,1)S(1)}, u32[]{:S(2)}, u32[]{:S(2)}) collective-permute-start(bf16[64,1024]{1,0:T(8,128)(2,1)S(1)} %fusion.6), channel_id=1, source_target_pairs={{0,12},{1,13},{2,14},{3,15},{4,8},{5,9},{6,10},{7,11},{8,4},{9,5},... | collective-permute-start | bytes 393224 | tf_op jit(solution)/shard_map/ppermute | solution.py:475
  133.8 6.4 %collective-permute-start.5 = (bf16[64,1152]{1,0:T(8,128)(2,1)S(1)}, bf16[64,1152]{1,0:T(8,128)(2,1)S(1)}, u32[]{:S(2)}, u32[]{:S(2)}) collective-permute-start(bf16[64,1152]{1,0:T(8,128)(2,1)S(1)} %fusion), channel_id=1, source_target_pairs={{0,3},{1,2},{2,1},{3,0},{4,7},{5,6},{6,5},{7,4},{8,11},{9,10},{10,... | collective-permute-start | bytes 442376 | tf_op jit(solution)/shard_map/ppermute | solution.py:475
  134.7 5.7 %collective-permute-start.20 = (bf16[64,1024]{1,0:T(8,128)(2,1)S(1)}, bf16[64,1024]{1,0:T(8,128)(2,1)S(1)}, u32[]{:S(2)}, u32[]{:S(2)}) collective-permute-start(bf16[64,1024]{1,0:T(8,128)(2,1)S(1)} %fusion.2), channel_id=1, source_target_pairs={{0,4},{1,5},{2,6},{3,7},{4,0},{5,1},{6,2},{7,3},{8,12},{9,13},{10,... | collective-permute-start | bytes 393224 | tf_op jit(solution)/shard_map/ppermute | solution.py:475

commit v4 on v3

--- a/solution.py
+++ b/solution.py
@@ -496,20 +496,20 @@
     second = [
         swap(added(a, b).astype(bf16), ax, m ^ 2) for a, b, (ax, m, q) in zip(passed, far, SETS)
     ]
-    later = []
-    for (ax, m, q), a, b, c in zip(SETS, own, near, second):
-        total = added(a, b, c).reshape(4, 64, -1)
-        away = jnp.stack([total[m], total[2]]).astype(bf16)
-        later.append((total[0], total[m ^ 2], swap(away, 1 - ax, m)))
-    last = []
-    for (ax, m, q), (first, second, got) in zip(SETS, later):
-        last.append(
-            (
-                added(first, got[0]),
-                swap(added(second, got[1]).astype(bf16), 1 - ax, m ^ 2),
-            )
-        )
-    parts = [added(a, b) for a, b in last]
+    total = [added(a, b, c).reshape(4, 64, -1) for a, b, c in zip(own, near, second)]
+
+    def swaps(values, masks):
+        out = []
+        for q, (ax, m, _) in enumerate(SETS):
+            out.append(swap(values[q].astype(bf16), 1 - ax, masks[q]))
+        return out
+
+    near_to = [m for _, m, _ in SETS]
+    pass_to = [m ^ 2 for m in near_to]
+    later_far = swaps([t[2] for t in total], near_to)
+    later_near = swaps([t[m] for t, m in zip(total, near_to)], near_to)
+    last = swaps([added(t[m], a) for t, m, a in zip(total, pass_to, later_far)], pass_to)
+    parts = [added(t[0], a, b) for t, a, b in zip(total, later_near, last)]
     scale = lax.rsqrt(parts[0][:, 1024:1025] / INNER + norm_eps)
     return jnp.concatenate([v[:, :1024] * scale for v in parts], axis=1).astype(bf16)
 

time: 144 us -> 150 us (1.042); the launches traced: 142 us -> 149 us
  waiting for transfers between devices: 53 us -> 57.8 us
  starting transfers between devices: 34.7 us -> 37.6 us
    ppermute x20 -> x24, waiting for transfers between devices: 50.8 us -> 55.6 us  [swap(): return lax.ppermute(values, 'head', [(h, h ^ mask) for h in range(16)])]
    ppermute x20 -> x24, starting transfers between devices: 29.5 us -> 32.3 us  [swap(): return lax.ppermute(values, 'head', [(h, h ^ mask) for h in range(16)])]
  transfers between devices with their start and end apart: 22 -> 26, of which waited for: 7 -> 10; matrix products, arithmetic and copies ran while one was open for 2% -> 1% of each run, Pallas kernels for 13% -> 12%
where the time goes in v4:
time: 150 us; the launch traced here: 149 us
  waiting for transfers between devices  57.8 us (39%)
  starting transfers between devices  37.6 us (25%)
  Pallas kernels  29.5 us (20%)
  blocking collectives  19.8 us (13%)
  other arithmetic  3.14 us (2%)
    ppermute x24, waiting for transfers between devices, swap(): return lax.ppermute(values, 'head', [(h, h ^ mask) for h in range(16)])  55.6 us
    ppermute x24, starting transfers between devices, swap(): return lax.ppermute(values, 'head', [(h, h ^ mask) for h in range(16)])  32.3 us
    all_to_all x1, blocking collectives, layer(): pieces = prefix(lax.all_to_all(msg, 'seq', 0, 0))  19.8 us
    pallas_call x2, Pallas kernels, gate(): pl.pallas_call(functools.partial(gate_kernel, masks, name), grid=(count +...  12.1 us
    pallas_call x1, Pallas kernels, inside(): pl.pallas_call(inside_kernel, grid=(1024 // Q,), in_specs=[pl.BlockSpec(m...  6.38 us
    pallas_call x1, Pallas kernels, block_states(): pl.pallas_call(state_kernel, grid=(1024 // Q,), in_specs=[rows(512), rows...  4.45 us
    all_to_all x1, starting transfers between devices, layer(): incoming = lax.all_to_all(pieces, 'seq', 0, 0)  3.51 us
    pallas_call x1, Pallas kernels, keep(): pl.pallas_call(keep_kernel, grid=(4,), in_specs=[pl.BlockSpec(memory_spac...  3.48 us
  transfers between devices with their start and end apart: 26, of which 10 were waited for; matrix products, arithmetic and copies ran while one was open for 1% of the time, Pallas kernels for 12%

profile of v4, /device:TPU:2, one launch (start us, length us, event | category | flops | bytes accessed | tf_op | source)
XLA Modules:
  0.0 149.1 jit_solution(7026834093687719191)
XLA Ops:
  0.9 1.7 %collective-permute-start = (bf16[16,768]{1,0:T(8,128)(2,1)S(1)}, bf16[16,768]{1,0:T(8,128)(2,1)S(1)}, u32[]{:S(2)}, u32[]{:S(2)}) collective-permute-start(bf16[16,768]{1,0:T(8,128)(2,1)S(1)} %edge.1), channel_id=1, source_target_pairs={{0,16},{16,32},{32,48},{48,64},{64,80},{80,96},{96,112},{112,128},... | collective-permute-start | bytes 73736 | tf_op jit(solution)/shard_map/ppermute | solution.py:518
  3.4 1.6 %decays.1 = (f32[8,1024]{1,0:T(8,128)S(1)}, f32[8,1024]{1,0:T(8,128)S(1)}, bf16[1024,16]{1,0:T(8,128)(2,1)S(1)}, bf16[1024,16]{1,0:T(8,128)(2,1)S(1)}) custom-call(f32[8]{0:T(128)S(1)} %copy-done.8, f32[8,1024]{1,0:T(8,128)S(1)} %bitcast.2), custom_call_target="tpu_custom_call" | custom-call | tf_op jit(solution)/shard_map/decays/pallas_call | solution.py:93
  5.0 4.4 %states.1 = (bf16[1024,512]{1,0:T(8,128)(2,1)}, bf16[1024,256]{1,0:T(8,128)(2,1)S(1)}, f32[8,1024]{1,0:T(8,128)S(1)}, bf16[1024,512]{1,0:T(8,128)(2,1)}, bf16[16,40,128]{2,1,0:T(8,128)(2,1)S(1)}) custom-call(bf16[1024,512]{1,0:T(8,128)(2,1)S(1)} %copy-done.1, bf16[1024,128]{1,0:T(8,128)(2,1)S(1)} %copy-done.2, bf16[1024,128]{1,0:T(8,128)(2,1)S(1)} %copy-done.3, ...), custom_call_target="tpu_custom_call" | custom-call | tf_op jit(solution)/shard_map/states/pallas_call | solution.py:194
  9.5 19.8 %all_to_all.10.in_ref = bf16[16,40,128]{2,1,0:T(8,128)(2,1)S(1)} all-to-all(bf16[16,40,128]{2,1,0:T(8,128)(2,1)S(1)} %get-tuple-element.40), channel_id=1, replica_groups=mesh['seq'=16,'head'=16] {'seq'}, dimensions={0} | all-to-all | bytes 327680 | tf_op jit(solution)/shard_map/all_to_all | solution.py:525
  30.0 3.5 %all-to-all-start.1 = ((bf16[16,32,128]{2,1,0:T(8,128)(2,1)}), bf16[16,32,128]{2,1,0:T(8,128)(2,1)S(1)}, u32[]{:S(2)}, u32[]{:S(2)}) async-start(bf16[16,32,128]{2,1,0:T(8,128)(2,1)} %prefix.1), calls=%async_computation.1 | async-start | bytes 262144 | tf_op jit(solution)/shard_map/all_to_all | solution.py:526
  33.5 6.4 %inside.1.y_ref = f32[1024,512]{1,0:T(8,128)S(1)} custom-call(f32[8]{0:T(128)S(1)} %copy-done.9, bf16[1024,512]{1,0:T(8,128)(2,1)} %get-tuple-element.34.xc_ref, bf16[1024,256]{1,0:T(8,128)(2,1)S(1)} %get-tuple-element.35.bc_ref, f32[8,1024]{1,0:T(8,128)S(1)} %get-tuple-element.32.run_ref, f32[8,1024]{1,0:T(8,128)S(1)} %get-tuple-element.36.step_ref), custom_call_target="tpu_custom_call" | custom-call | tf_op jit(solution)/shard_map/inside/pallas_call | solution.py:251
  39.9 2.2 %all-to-all-done.1.sin_ref = bf16[16,32,128]{2,1,0:T(8,128)(2,1)S(1)} async-done(((bf16[16,32,128]{2,1,0:T(8,128)(2,1)}), bf16[16,32,128]{2,1,0:T(8,128)(2,1)S(1)}, u32[]{:S(2)}, u32[]{:S(2)}) %all-to-all-start.1) | async-done | bytes 131104 | tf_op jit(solution)/shard_map/all_to_all | solution.py:526
  42.1 5.7 %shard_map.109 = (bf16[256,1152]{1,0:T(8,128)(2,1)S(1)}, bf16[256,1024]{1,0:T(8,128)(2,1)S(1)}, bf16[256,1024]{1,0:T(8,128)(2,1)S(1)}, bf16[256,1024]{1,0:T(8,128)(2,1)S(1)}, bf16[448,640]{1,0:T(8,128)(2,1)S(1)}) custom-call(f32[1024,512]{1,0:T(8,128)S(1)} %inside.1.y_ref, bf16[1024,256]{1,0:T(8,128)(2,1)S(1)} %get-tuple-element.35.bc_ref, ...), custom_call_target="tpu_custom_call" | custom-call | tf_op jit(solution)/shard_map/pallas_call | solution.py:407
  47.8 3.1 %collective-permute-start.20 = (bf16[256,1024]{1,0:T(8,128)(2,1)S(1)}, bf16[256,1024]{1,0:T(8,128)(2,1)S(1)}, u32[]{:S(2)}, u32[]{:S(2)}) collective-permute-start(bf16[256,1024]{1,0:T(8,128)(2,1)S(1)} %get-tuple-element.58), channel_id=1, source_target_pairs={{0,3},{1,2},{2,1},{3,0},{4,7},{5,6},{6,5},{7,4},{8,11},{9,10},{10,... | collective-permute-start | bytes 1572872 | tf_op jit(solution)/shard_map/ppermute | solution.py:475
  51.1 6.4 %shard_map.110 = (bf16[256,1152]{1,0:T(8,128)(2,1)S(1)}, bf16[256,1024]{1,0:T(8,128)(2,1)S(1)}, bf16[256,1024]{1,0:T(8,128)(2,1)S(1)}, bf16[256,1024]{1,0:T(8,128)(2,1)S(1)}, bf16[1024,640]{1,0:T(8,128)(2,1)S(1)}) custom-call(f32[1024,512]{1,0:T(8,128)S(1)} %inside.1.y_ref, bf16[1024,256]{1,0:T(8,128)(2,1)S(1)} %get-tuple-element.35.bc_ref, ...), custom_call_target="tpu_custom_call" | custom-call | tf_op jit(solution)/shard_map/pallas_call | solution.py:407
  57.5 1.6 %collective-permute-start.7 = (bf16[256,1024]{1,0:T(8,128)(2,1)S(1)}, bf16[256,1024]{1,0:T(8,128)(2,1)S(1)}, u32[]{:S(2)}, u32[]{:S(2)}) collective-permute-start(bf16[256,1024]{1,0:T(8,128)(2,1)S(1)} %get-tuple-element.48), channel_id=1, source_target_pairs={{0,12},{1,13},{2,14},{3,15},{4,8},{5,9},{6,10},{7,11},{8,4},{9,5},... | collective-permute-start | bytes 1572872 | tf_op jit(solution)/shard_map/ppermute | solution.py:475
  59.1 1.9 %collective-permute-start.13 = (bf16[256,1024]{1,0:T(8,128)(2,1)S(1)}, bf16[256,1024]{1,0:T(8,128)(2,1)S(1)}, u32[]{:S(2)}, u32[]{:S(2)}) collective-permute-start(bf16[256,1024]{1,0:T(8,128)(2,1)S(1)} %get-tuple-element.52), channel_id=1, source_target_pairs={{0,1},{1,0},{2,3},{3,2},{4,5},{5,4},{6,7},{7,6},{8,9},{9,8},{10,11... | collective-permute-start | bytes 1572872 | tf_op jit(solution)/shard_map/ppermute | solution.py:475
  61.5 3.5 %keep.1 = (bf16[256,1152]{1,0:T(8,128)(2,1)S(1)}, bf16[256,1024]{1,0:T(8,128)(2,1)S(1)}, bf16[256,1024]{1,0:T(8,128)(2,1)S(1)}, bf16[256,1024]{1,0:T(8,128)(2,1)...) custom-call(bf16[1024,640]{1,0:T(8,128)(2,1)S(1)} %get-tuple-element, ...), custom_call_target="tpu_custom_call" | custom-call | tf_op jit(solution)/shard_map/keep/pallas_call | solution.py:457
  65.0 1.8 %collective-permute-start.2 = (bf16[256,1152]{1,0:T(8,128)(2,1)S(1)}, bf16[256,1152]{1,0:T(8,128)(2,1)S(1)}, u32[]{:S(2)}, u32[]{:S(2)}) collective-permute-start(bf16[256,1152]{1,0:T(8,128)(2,1)S(1)} %get-tuple-element.46), channel_id=1, source_target_pairs={{0,4},{1,5},{2,6},{3,7},{4,0},{5,1},{6,2},{7,3},{8,12},{9,13},{10,... | collective-permute-start | bytes 1769480 | tf_op jit(solution)/shard_map/ppermute | solution.py:475
  67.5 15.2 %collective-permute-done.8 = bf16[256,1024]{1,0:T(8,128)(2,1)S(1)} collective-permute-done((bf16[256,1024]{1,0:T(8,128)(2,1)S(1)}, bf16[256,1024]{1,0:T(8,128)(2,1)S(1)}, u32[]{:S(2)}, u32[]{:S(2)}) %collective-permute-start.8) | collective-permute-done | bytes 524320 | tf_op jit(solution)/shard_map/ppermute | solution.py:475
  82.8 1.7 %collective-permute-start.1 = (bf16[256,1152]{1,0:T(8,128)(2,1)S(1)}, bf16[256,1152]{1,0:T(8,128)(2,1)S(1)}, u32[]{:S(2)}, u32[]{:S(2)}) collective-permute-start(bf16[256,1152]{1,0:T(8,128)(2,1)S(1)} %get-tuple-element.44), channel_id=1, source_target_pairs={{0,4},{1,5},{2,6},{3,7},{4,0},{5,1},{6,2},{7,3},{8,12},{9,13},{10,... | collective-permute-start | bytes 1769480 | tf_op jit(solution)/shard_map/ppermute | solution.py:475
  86.3 22.3 %collective-permute-done.9 = bf16[256,1024]{1,0:T(8,128)(2,1)S(1)} collective-permute-done((bf16[256,1024]{1,0:T(8,128)(2,1)S(1)}, bf16[256,1024]{1,0:T(8,128)(2,1)S(1)}, u32[]{:S(2)}, u32[]{:S(2)}) %collective-permute-start.9) | collective-permute-done | bytes 524320 | tf_op jit(solution)/shard_map/ppermute | solution.py:475
  108.5 1.6 %collective-permute-start.21 = (bf16[256,1024]{1,0:T(8,128)(2,1)S(1)}, bf16[256,1024]{1,0:T(8,128)(2,1)S(1)}, u32[]{:S(2)}, u32[]{:S(2)}) collective-permute-start(bf16[256,1024]{1,0:T(8,128)(2,1)S(1)} %add_convert_fusion.1), channel_id=1, source_target_pairs={{0,1},{1,0},{2,3},{3,2},{4,5},{5,4},{6,7},{7,6},{8,9},{9,8},{10,11... | collective-permute-start | bytes 1572872 | tf_op jit(solution)/shard_map/ppermute | solution.py:475
  110.5 2.2 %collective-permute-start.3 = (bf16[256,1152]{1,0:T(8,128)(2,1)S(1)}, bf16[256,1152]{1,0:T(8,128)(2,1)S(1)}, u32[]{:S(2)}, u32[]{:S(2)}) collective-permute-start(bf16[256,1152]{1,0:T(8,128)(2,1)S(1)} %add_convert_fusion), channel_id=1, source_target_pairs={{0,12},{1,13},{2,14},{3,15},{4,8},{5,9},{6,10},{7,11},{8,4},{9,5},... | collective-permute-start | bytes 1769480 | tf_op jit(solution)/shard_map/ppermute | solution.py:475
  113.6 2.8 %collective-permute-start.11 = (bf16[64,1024]{1,0:T(8,128)(2,1)S(1)}, bf16[64,1024]{1,0:T(8,128)(2,1)S(1)}, u32[]{:S(2)}, u32[]{:S(2)}) collective-permute-start(bf16[64,1024]{1,0:T(8,128)(2,1)S(1)} %get-tuple-element.70), channel_id=1, source_target_pairs={{0,3},{1,2},{2,1},{3,0},{4,7},{5,6},{6,5},{7,4},{8,11},{9,10},{10,... | collective-permute-start | bytes 393224 | tf_op jit(solution)/shard_map/ppermute | solution.py:475
  116.4 4.4 %collective-permute-done.21 = bf16[256,1024]{1,0:T(8,128)(2,1)S(1)} collective-permute-done((bf16[256,1024]{1,0:T(8,128)(2,1)S(1)}, bf16[256,1024]{1,0:T(8,128)(2,1)S(1)}, u32[]{:S(2)}, u32[]{:S(2)}) %collective-permute-start.21) | collective-permute-done | bytes 524320 | tf_op jit(solution)/shard_map/ppermute | solution.py:475
  120.8 1.7 %collective-permute-start.16 = (bf16[64,1024]{1,0:T(8,128)(2,1)S(1)}, bf16[64,1024]{1,0:T(8,128)(2,1)S(1)}, u32[]{:S(2)}, u32[]{:S(2)}) collective-permute-start(bf16[64,1024]{1,0:T(8,128)(2,1)S(1)} %get-tuple-element.71), channel_id=1, source_target_pairs={{0,4},{1,5},{2,6},{3,7},{4,0},{5,1},{6,2},{7,3},{8,12},{9,13},{10,... | collective-permute-start | bytes 393224 | tf_op jit(solution)/shard_map/ppermute | solution.py:475
  123.3 1.3 collective-permute-done.3
  124.5 1.7 %collective-permute-start.22 = (bf16[64,1024]{1,0:T(8,128)(2,1)S(1)}, bf16[64,1024]{1,0:T(8,128)(2,1)S(1)}, u32[]{:S(2)}, u32[]{:S(2)}) collective-permute-start(bf16[64,1024]{1,0:T(8,128)(2,1)S(1)} %get-tuple-element.73), channel_id=1, source_target_pairs={{0,12},{1,13},{2,14},{3,15},{4,8},{5,9},{6,10},{7,11},{8,4},{9,5},... | collective-permute-start | bytes 393224 | tf_op jit(solution)/shard_map/ppermute | solution.py:475
  126.9 1.0 collective-permute-done.17
  127.9 1.5 collective-permute-start.5
  129.4 5.2 %collective-permute-done.5 = bf16[64,1152]{1,0:T(8,128)(2,1)S(1)} collective-permute-done((bf16[64,1152]{1,0:T(8,128)(2,1)S(1)}, bf16[64,1152]{1,0:T(8,128)(2,1)S(1)}, u32[]{:S(2)}, u32[]{:S(2)}) %collective-permute-start.5) | collective-permute-done | bytes 147488 | tf_op jit(solution)/shard_map/ppermute | solution.py:475
  134.7 1.5 collective-permute-start.4
  137.1 2.7 %collective-permute-done.4 = bf16[64,1152]{1,0:T(8,128)(2,1)S(1)} collective-permute-done((bf16[64,1152]{1,0:T(8,128)(2,1)S(1)}, bf16[64,1152]{1,0:T(8,128)(2,1)S(1)}, u32[]{:S(2)}, u32[]{:S(2)}) %collective-permute-start.4) | collective-permute-done | bytes 147488 | tf_op jit(solution)/shard_map/ppermute | solution.py:475
  139.8 2.2 %collective-permute-start.18 = (bf16[64,1024]{1,0:T(8,128)(2,1)S(1)}, bf16[64,1024]{1,0:T(8,128)(2,1)S(1)}, u32[]{:S(2)}, u32[]{:S(2)}) collective-permute-start(bf16[64,1024]{1,0:T(8,128)(2,1)S(1)} %fusion.6), channel_id=1, source_target_pairs={{0,12},{1,13},{2,14},{3,15},{4,8},{5,9},{6,10},{7,11},{8,4},{9,5},... | collective-permute-start | bytes 393224 | tf_op jit(solution)/shard_map/ppermute | solution.py:475
  142.6 2.5 %collective-permute-start.24 = (bf16[64,1024]{1,0:T(8,128)(2,1)S(1)}, bf16[64,1024]{1,0:T(8,128)(2,1)S(1)}, u32[]{:S(2)}, u32[]{:S(2)}) collective-permute-start(bf16[64,1024]{1,0:T(8,128)(2,1)S(1)} %fusion.2), channel_id=1, source_target_pairs={{0,4},{1,5},{2,6},{3,7},{4,0},{5,1},{6,2},{7,3},{8,12},{9,13},{10,... | collective-permute-start | bytes 393224 | tf_op jit(solution)/shard_map/ppermute | solution.py:475
  145.3 2.7 %collective-permute-done.24 = bf16[64,1024]{1,0:T(8,128)(2,1)S(1)} collective-permute-done((bf16[64,1024]{1,0:T(8,128)(2,1)S(1)}, bf16[64,1024]{1,0:T(8,128)(2,1)S(1)}, u32[]{:S(2)}, u32[]{:S(2)}) %collective-permute-start.24) | collective-permute-done | bytes 131104 | tf_op jit(solution)/shard_map/ppermute | solution.py:475
  (69 shorter events, 10.8 us)
Async XLA Ops:
  0.0 5.0 %copy-start.1 = (bf16[1024,512]{1,0:T(8,128)(2,1)S(1)}, bf16[1024,512]{1,0:T(8,128)(2,1)}, u32[]{:S(2)}) copy-start(bf16[1024,512]{1,0:T(8,128)(2,1)} %x_ref.3) | copy-start | bytes 3145732
  0.0 5.0 %copy-start.7 = (f32[4,256]{1,0:T(4,128)S(1)}, f32[4,256]{1,0:T(4,128)}, u32[]{:S(2)}) copy-start(f32[4,256]{1,0:T(4,128)} %wbc_ref.1) | copy-start | bytes 12292
  0.0 5.0 %copy-start.5 = (f32[4,512]{1,0:T(4,128)S(1)}, f32[4,512]{1,0:T(4,128)}, u32[]{:S(2)}) copy-start(f32[4,512]{1,0:T(4,128)} %wx_ref.1) | copy-start | bytes 24580
  0.9 4.1 %collective-permute-start = (bf16[16,768]{1,0:T(8,128)(2,1)S(1)}, bf16[16,768]{1,0:T(8,128)(2,1)S(1)}, u32[]{:S(2)}, u32[]{:S(2)}) collective-permute-start(bf16[16,768]{1,0:T(8,128)(2,1)S(1)} %edge.1), channel_id=1, source_target_pairs={{0,16},{16,32},{32,48},{48,64},{64,80},{80,96},{96,112},{112,128},... | collective-permute-start | bytes 73736 | tf_op jit(solution)/shard_map/ppermute | solution.py:518
  5.0 28.5 %copy-start.9 = (f32[8]{0:T(128)S(1)}, f32[8]{0:T(128)}, u32[]{:S(2)}) copy-start(f32[8]{0:T(128)} %skip_ref.1) | copy-start | bytes 100
  30.0 12.1 %all-to-all-start.1 = ((bf16[16,32,128]{2,1,0:T(8,128)(2,1)}), bf16[16,32,128]{2,1,0:T(8,128)(2,1)S(1)}, u32[]{:S(2)}, u32[]{:S(2)}) async-start(bf16[16,32,128]{2,1,0:T(8,128)(2,1)} %prefix.1), calls=%async_computation.1 | async-start | bytes 262144 | tf_op jit(solution)/shard_map/all_to_all | solution.py:526
  33.5 8.6 %copy-start.6 = (f32[512]{0:T(512)S(1)}, f32[512]{0:T(512)}, u32[]{:S(2)}) copy-start(f32[512]{0:T(512)} %param.20) | copy-start | bytes 6148
  47.8 17.2 %collective-permute-start.20 = (bf16[256,1024]{1,0:T(8,128)(2,1)S(1)}, bf16[256,1024]{1,0:T(8,128)(2,1)S(1)}, u32[]{:S(2)}, u32[]{:S(2)}) collective-permute-start(bf16[256,1024]{1,0:T(8,128)(2,1)S(1)} %get-tuple-element.58), channel_id=1, source_target_pairs={{0,3},{1,2},{2,1},{3,0},{4,7},{5,6},{6,5},{7,4},{8,11},{9,10},{10,... | collective-permute-start | bytes 1572872 | tf_op jit(solution)/shard_map/ppermute | solution.py:475
  50.9 16.1 %collective-permute-start.14 = (bf16[256,1024]{1,0:T(8,128)(2,1)S(1)}, bf16[256,1024]{1,0:T(8,128)(2,1)S(1)}, u32[]{:S(2)}, u32[]{:S(2)}) collective-permute-start(bf16[256,1024]{1,0:T(8,128)(2,1)S(1)} %get-tuple-element.54), channel_id=1, source_target_pairs={{0,1},{1,0},{2,3},{3,2},{4,5},{5,4},{6,7},{7,6},{8,9},{9,8},{10,11... | collective-permute-start | bytes 1572872 | tf_op jit(solution)/shard_map/ppermute | solution.py:475
  51.1 10.4 %copy-start = (bf16[512,4096]{1,0:T(8,128)(2,1)S(1)}, bf16[512,4096]{1,0:T(8,128)(2,1)}, u32[]{:S(2)}) copy-start(bf16[512,4096]{1,0:T(8,128)(2,1)} %w_ref.5) | copy-start | bytes 12582916
  57.5 27.8 %collective-permute-start.7 = (bf16[256,1024]{1,0:T(8,128)(2,1)S(1)}, bf16[256,1024]{1,0:T(8,128)(2,1)S(1)}, u32[]{:S(2)}, u32[]{:S(2)}) collective-permute-start(bf16[256,1024]{1,0:T(8,128)(2,1)S(1)} %get-tuple-element.48), channel_id=1, source_target_pairs={{0,12},{1,13},{2,14},{3,15},{4,8},{5,9},{6,10},{7,11},{8,4},{9,5},... | collective-permute-start | bytes 1572872 | tf_op jit(solution)/shard_map/ppermute | solution.py:475
  59.1 51.4 %collective-permute-start.13 = (bf16[256,1024]{1,0:T(8,128)(2,1)S(1)}, bf16[256,1024]{1,0:T(8,128)(2,1)S(1)}, u32[]{:S(2)}, u32[]{:S(2)}) collective-permute-start(bf16[256,1024]{1,0:T(8,128)(2,1)S(1)} %get-tuple-element.52), channel_id=1, source_target_pairs={{0,1},{1,0},{2,3},{3,2},{4,5},{5,4},{6,7},{7,6},{8,9},{9,8},{10,11... | collective-permute-start | bytes 1572872 | tf_op jit(solution)/shard_map/ppermute | solution.py:475
  61.0 21.8 %collective-permute-start.8 = (bf16[256,1024]{1,0:T(8,128)(2,1)S(1)}, bf16[256,1024]{1,0:T(8,128)(2,1)S(1)}, u32[]{:S(2)}, u32[]{:S(2)}) collective-permute-start(bf16[256,1024]{1,0:T(8,128)(2,1)S(1)} %get-tuple-element.50), channel_id=1, source_target_pairs={{0,12},{1,13},{2,14},{3,15},{4,8},{5,9},{6,10},{7,11},{8,4},{9,5},... | collective-permute-start | bytes 1572872 | tf_op jit(solution)/shard_map/ppermute | solution.py:475
  65.0 19.7 %collective-permute-start.2 = (bf16[256,1152]{1,0:T(8,128)(2,1)S(1)}, bf16[256,1152]{1,0:T(8,128)(2,1)S(1)}, u32[]{:S(2)}, u32[]{:S(2)}) collective-permute-start(bf16[256,1152]{1,0:T(8,128)(2,1)S(1)} %get-tuple-element.46), channel_id=1, source_target_pairs={{0,4},{1,5},{2,6},{3,7},{4,0},{5,1},{6,2},{7,3},{8,12},{9,13},{10,... | collective-permute-start | bytes 1769480 | tf_op jit(solution)/shard_map/ppermute | solution.py:475
  67.0 46.6 %collective-permute-start.19 = (bf16[256,1024]{1,0:T(8,128)(2,1)S(1)}, bf16[256,1024]{1,0:T(8,128)(2,1)S(1)}, u32[]{:S(2)}, u32[]{:S(2)}) collective-permute-start(bf16[256,1024]{1,0:T(8,128)(2,1)S(1)} %get-tuple-element.56), channel_id=1, source_target_pairs={{0,3},{1,2},{2,1},{3,0},{4,7},{5,6},{6,5},{7,4},{8,11},{9,10},{10,... | collective-permute-start | bytes 1572872 | tf_op jit(solution)/shard_map/ppermute | solution.py:475
  82.8 40.1 %collective-permute-start.1 = (bf16[256,1152]{1,0:T(8,128)(2,1)S(1)}, bf16[256,1152]{1,0:T(8,128)(2,1)S(1)}, u32[]{:S(2)}, u32[]{:S(2)}) collective-permute-start(bf16[256,1152]{1,0:T(8,128)(2,1)S(1)} %get-tuple-element.44), channel_id=1, source_target_pairs={{0,4},{1,5},{2,6},{3,7},{4,0},{5,1},{6,2},{7,3},{8,12},{9,13},{10,... | collective-permute-start | bytes 1769480 | tf_op jit(solution)/shard_map/ppermute | solution.py:475
  84.7 23.8 %collective-permute-start.9 = (bf16[256,1024]{1,0:T(8,128)(2,1)S(1)}, bf16[256,1024]{1,0:T(8,128)(2,1)S(1)}, u32[]{:S(2)}, u32[]{:S(2)}) collective-permute-start(bf16[256,1024]{1,0:T(8,128)(2,1)S(1)} %add_convert_fusion.3), channel_id=1, source_target_pairs={{0,4},{1,5},{2,6},{3,7},{4,0},{5,1},{6,2},{7,3},{8,12},{9,13},{10,... | collective-permute-start | bytes 1572872 | tf_op jit(solution)/shard_map/ppermute | solution.py:475
  85.3 27.5 %collective-permute-start.15 = (bf16[256,1024]{1,0:T(8,128)(2,1)S(1)}, bf16[256,1024]{1,0:T(8,128)(2,1)S(1)}, u32[]{:S(2)}, u32[]{:S(2)}) collective-permute-start(bf16[256,1024]{1,0:T(8,128)(2,1)S(1)} %add_convert_fusion.2), channel_id=1, source_target_pairs={{0,3},{1,2},{2,1},{3,0},{4,7},{5,6},{6,5},{7,4},{8,11},{9,10},{10,... | collective-permute-start | bytes 1572872 | tf_op jit(solution)/shard_map/ppermute | solution.py:475
  108.5 12.3 %collective-permute-start.21 = (bf16[256,1024]{1,0:T(8,128)(2,1)S(1)}, bf16[256,1024]{1,0:T(8,128)(2,1)S(1)}, u32[]{:S(2)}, u32[]{:S(2)}) collective-permute-start(bf16[256,1024]{1,0:T(8,128)(2,1)S(1)} %add_convert_fusion.1), channel_id=1, source_target_pairs={{0,1},{1,0},{2,3},{3,2},{4,5},{5,4},{6,7},{7,6},{8,9},{9,8},{10,11... | collective-permute-start | bytes 1572872 | tf_op jit(solution)/shard_map/ppermute | solution.py:475
  110.5 14.0 %collective-permute-start.3 = (bf16[256,1152]{1,0:T(8,128)(2,1)S(1)}, bf16[256,1152]{1,0:T(8,128)(2,1)S(1)}, u32[]{:S(2)}, u32[]{:S(2)}) collective-permute-start(bf16[256,1152]{1,0:T(8,128)(2,1)S(1)} %add_convert_fusion), channel_id=1, source_target_pairs={{0,12},{1,13},{2,14},{3,15},{4,8},{5,9},{6,10},{7,11},{8,4},{9,5},... | collective-permute-start | bytes 1769480 | tf_op jit(solution)/shard_map/ppermute | solution.py:475
  112.7 24.3 %collective-permute-start.10 = (bf16[64,1024]{1,0:T(8,128)(2,1)S(1)}, bf16[64,1024]{1,0:T(8,128)(2,1)S(1)}, u32[]{:S(2)}, u32[]{:S(2)}) collective-permute-start(bf16[64,1024]{1,0:T(8,128)(2,1)S(1)} %get-tuple-element.69), channel_id=1, source_target_pairs={{0,3},{1,2},{2,1},{3,0},{4,7},{5,6},{6,5},{7,4},{8,11},{9,10},{10,... | collective-permute-start | bytes 393224 | tf_op jit(solution)/shard_map/ppermute | solution.py:475
  113.6 12.9 %collective-permute-start.11 = (bf16[64,1024]{1,0:T(8,128)(2,1)S(1)}, bf16[64,1024]{1,0:T(8,128)(2,1)S(1)}, u32[]{:S(2)}, u32[]{:S(2)}) collective-permute-start(bf16[64,1024]{1,0:T(8,128)(2,1)S(1)} %get-tuple-element.70), channel_id=1, source_target_pairs={{0,3},{1,2},{2,1},{3,0},{4,7},{5,6},{6,5},{7,4},{8,11},{9,10},{10,... | collective-permute-start | bytes 393224 | tf_op jit(solution)/shard_map/ppermute | solution.py:475
  120.8 24.5 %collective-permute-start.16 = (bf16[64,1024]{1,0:T(8,128)(2,1)S(1)}, bf16[64,1024]{1,0:T(8,128)(2,1)S(1)}, u32[]{:S(2)}, u32[]{:S(2)}) collective-permute-start(bf16[64,1024]{1,0:T(8,128)(2,1)S(1)} %get-tuple-element.71), channel_id=1, source_target_pairs={{0,4},{1,5},{2,6},{3,7},{4,0},{5,1},{6,2},{7,3},{8,12},{9,13},{10,... | collective-permute-start | bytes 393224 | tf_op jit(solution)/shard_map/ppermute | solution.py:475
  122.9 5.1 %collective-permute-start.17 = (bf16[64,1024]{1,0:T(8,128)(2,1)S(1)}, bf16[64,1024]{1,0:T(8,128)(2,1)S(1)}, u32[]{:S(2)}, u32[]{:S(2)}) collective-permute-start(bf16[64,1024]{1,0:T(8,128)(2,1)S(1)} %get-tuple-element.72), channel_id=1, source_target_pairs={{0,4},{1,5},{2,6},{3,7},{4,0},{5,1},{6,2},{7,3},{8,12},{9,13},{10,... | collective-permute-start | bytes 393224 | tf_op jit(solution)/shard_map/ppermute | solution.py:475
  124.5 20.8 %collective-permute-start.22 = (bf16[64,1024]{1,0:T(8,128)(2,1)S(1)}, bf16[64,1024]{1,0:T(8,128)(2,1)S(1)}, u32[]{:S(2)}, u32[]{:S(2)}) collective-permute-start(bf16[64,1024]{1,0:T(8,128)(2,1)S(1)} %get-tuple-element.73), channel_id=1, source_target_pairs={{0,12},{1,13},{2,14},{3,15},{4,8},{5,9},{6,10},{7,11},{8,4},{9,5},... | collective-permute-start | bytes 393224 | tf_op jit(solution)/shard_map/ppermute | solution.py:475
  126.5 9.7 %collective-permute-start.23 = (bf16[64,1024]{1,0:T(8,128)(2,1)S(1)}, bf16[64,1024]{1,0:T(8,128)(2,1)S(1)}, u32[]{:S(2)}, u32[]{:S(2)}) collective-permute-start(bf16[64,1024]{1,0:T(8,128)(2,1)S(1)} %get-tuple-element.74), channel_id=1, source_target_pairs={{0,12},{1,13},{2,14},{3,15},{4,8},{5,9},{6,10},{7,11},{8,4},{9,5},... | collective-permute-start | bytes 393224 | tf_op jit(solution)/shard_map/ppermute | solution.py:475
  127.9 6.7 %collective-permute-start.5 = (bf16[64,1152]{1,0:T(8,128)(2,1)S(1)}, bf16[64,1152]{1,0:T(8,128)(2,1)S(1)}, u32[]{:S(2)}, u32[]{:S(2)}) collective-permute-start(bf16[64,1152]{1,0:T(8,128)(2,1)S(1)} %get-tuple-element.68), channel_id=1, source_target_pairs={{0,1},{1,0},{2,3},{3,2},{4,5},{5,4},{6,7},{7,6},{8,9},{9,8},{10,11... | collective-permute-start | bytes 442376 | tf_op jit(solution)/shard_map/ppermute | solution.py:475
  134.7 5.1 %collective-permute-start.4 = (bf16[64,1152]{1,0:T(8,128)(2,1)S(1)}, bf16[64,1152]{1,0:T(8,128)(2,1)S(1)}, u32[]{:S(2)}, u32[]{:S(2)}) collective-permute-start(bf16[64,1152]{1,0:T(8,128)(2,1)S(1)} %get-tuple-element.67), channel_id=1, source_target_pairs={{0,1},{1,0},{2,3},{3,2},{4,5},{5,4},{6,7},{7,6},{8,9},{9,8},{10,11... | collective-permute-start | bytes 442376 | tf_op jit(solution)/shard_map/ppermute | solution.py:475
  136.2 6.4 %collective-permute-start.6 = (bf16[64,1152]{1,0:T(8,128)(2,1)S(1)}, bf16[64,1152]{1,0:T(8,128)(2,1)S(1)}, u32[]{:S(2)}, u32[]{:S(2)}) collective-permute-start(bf16[64,1152]{1,0:T(8,128)(2,1)S(1)} %fusion), channel_id=1, source_target_pairs={{0,3},{1,2},{2,1},{3,0},{4,7},{5,6},{6,5},{7,4},{8,11},{9,10},{10,... | collective-permute-start | bytes 442376 | tf_op jit(solution)/shard_map/ppermute | solution.py:475
  137.0 8.3 %collective-permute-start.12 = (bf16[64,1024]{1,0:T(8,128)(2,1)S(1)}, bf16[64,1024]{1,0:T(8,128)(2,1)S(1)}, u32[]{:S(2)}, u32[]{:S(2)}) collective-permute-start(bf16[64,1024]{1,0:T(8,128)(2,1)S(1)} %fusion.10), channel_id=1, source_target_pairs={{0,1},{1,0},{2,3},{3,2},{4,5},{5,4},{6,7},{7,6},{8,9},{9,8},{10,11... | collective-permute-start | bytes 393224 | tf_op jit(solution)/shard_map/ppermute | solution.py:475
  139.8 5.5 %collective-permute-start.18 = (bf16[64,1024]{1,0:T(8,128)(2,1)S(1)}, bf16[64,1024]{1,0:T(8,128)(2,1)S(1)}, u32[]{:S(2)}, u32[]{:S(2)}) collective-permute-start(bf16[64,1024]{1,0:T(8,128)(2,1)S(1)} %fusion.6), channel_id=1, source_target_pairs={{0,12},{1,13},{2,14},{3,15},{4,8},{5,9},{6,10},{7,11},{8,4},{9,5},... | collective-permute-start | bytes 393224 | tf_op jit(solution)/shard_map/ppermute | solution.py:475
  142.6 5.4 %collective-permute-start.24 = (bf16[64,1024]{1,0:T(8,128)(2,1)S(1)}, bf16[64,1024]{1,0:T(8,128)(2,1)S(1)}, u32[]{:S(2)}, u32[]{:S(2)}) collective-permute-start(bf16[64,1024]{1,0:T(8,128)(2,1)S(1)} %fusion.2), channel_id=1, source_target_pairs={{0,4},{1,5},{2,6},{3,7},{4,0},{5,1},{6,2},{7,3},{8,12},{9,13},{10,... | collective-permute-start | bytes 393224 | tf_op jit(solution)/shard_map/ppermute | solution.py:475
  (4 other events, 13.4 us)
